TPU v7x, 512 devices: a whole 4x8x8 slice. The times are simulated.
512 devices in a mesh: src: 8 (over z_lo, core), lat: 32 (over y, x), sub: 2 (over z_hi).
Axes of the slice: x: 4, y: 8, z: 8 (z_hi: 2, z_lo: 4; z = z_hi * 4 + z_lo), core: 2. Of those that a mesh axis runs over, the one named last changes fastest.
Arguments:
- sources: float32 [8, 24, 384, 8, 128], P(None, None, ('lat', 'sub'), 'src'), may hold values from -6 to 6
- eigvecs: bfloat16 [32, 24, 384, 8, 128], P(None, None, ('lat', 'sub'), 'src'), may hold values from -6 to 6
- eigvals: float32 [32], replicated, may hold values from 0.5 to 8
- links: float32 [4, 18, 384, 8, 128], P(None, None, ('lat', 'sub')), may hold values from -6 to 6
- damping: float32 [8], P('src'), may hold values from 0.5 to 1
Outputs:
- guess: float32 [8, 24, 384, 8, 128], P(None, None, ('lat', 'sub'), 'src')
- solution: float32 [8, 24, 384, 8, 128], P(None, None, ('lat', 'sub'), 'src')
All inputs are finite; a program needn't handle non-finite values.
Results may differ from a plain program's by a relative error of at most 0.0047.
Values sent between devices are 32-bit elements; how exact they have to be, the bound alone decides.
No kernel may reach another device: no remote copies, remote signals or barrier semaphores. Data moves between devices by JAX's collectives and lax.ppermute only.
A program may use at most 64 MiB of HBM per device.

v0:
```python
import math

import jax
import jax.numpy as jnp
import numpy as np
from jax import lax
from jax.sharding import PartitionSpec as P

LX = 16
ITERS = 2


HOPPING = 0.12
SPIN_BLOCKS = [
    (np.array([[0.0, 0.0], [0.0, 0.0]]), np.array([[0.0, 1.0], [1.0, 0.0]])),
    (np.array([[0.0, -1.0], [1.0, 0.0]]), np.zeros((2, 2))),
    (np.array([[0.0, 0.0], [0.0, 0.0]]), np.array([[1.0, 0.0], [0.0, -1.0]])),
    (np.eye(2), np.zeros((2, 2))),
]


def passed_along(x, axis, by):
    devices = lax.axis_size(axis)
    return lax.ppermute(x, axis, [(i, (i + by) % devices) for i in range(devices)])


def padded_2(x, sides, width):
    for axis, dim in sides:
        devices, length = (lax.axis_size(axis), x.shape[dim])
        up = [(i, (i + 1) % devices) for i in range(devices)]
        down = [(j, i) for i, j in up]
        last = lax.slice_in_dim(x, length - width, length, axis=dim)
        first = lax.slice_in_dim(x, 0, width, axis=dim)
        before = lax.ppermute(last, axis, up)
        after = lax.ppermute(first, axis, down)
        x = jnp.concatenate([before, x, after], axis=dim)
    return x


def spin_apply(table_re, table_im, real_part, imag_part):
    rows_re = []
    rows_im = []
    for row in range(2):
        acc_re = (
            float(table_re[row, 0]) * real_part[:, 0] - float(table_im[row, 0]) * imag_part[:, 0]
        )
        acc_im = (
            float(table_re[row, 0]) * imag_part[:, 0] + float(table_im[row, 0]) * real_part[:, 0]
        )
        acc_re = (
            acc_re
            + float(table_re[row, 1]) * real_part[:, 1]
            - float(table_im[row, 1]) * imag_part[:, 1]
        )
        acc_im = (
            acc_im
            + float(table_re[row, 1]) * imag_part[:, 1]
            + float(table_im[row, 1]) * real_part[:, 1]
        )
        rows_re.append(acc_re)
        rows_im.append(acc_im)
    return (jnp.stack(rows_re, 1), jnp.stack(rows_im, 1))


def project(sign, direction, real_part, imag_part):
    table_re, table_im = SPIN_BLOCKS[direction]
    lower_re, lower_im = spin_apply(table_re, table_im, real_part[:, 2:], imag_part[:, 2:])
    return (real_part[:, :2] + sign * lower_re, imag_part[:, :2] + sign * lower_im)


def rebuild(sign, direction, upper_re, upper_im):
    table_re, table_im = SPIN_BLOCKS[direction]
    lower_re, lower_im = spin_apply(table_re.T, -table_im.T, upper_re, upper_im)
    return (
        jnp.concatenate([upper_re, sign * lower_re], 1),
        jnp.concatenate([upper_im, sign * lower_im], 1),
    )


def color_mul(links_re, links_im, real_part, imag_part):
    rows_re = []
    rows_im = []
    for row in range(3):
        acc_re = links_re[row, 0] * real_part[:, :, 0] - links_im[row, 0] * imag_part[:, :, 0]
        acc_im = links_re[row, 0] * imag_part[:, :, 0] + links_im[row, 0] * real_part[:, :, 0]
        for col in range(1, 3):
            acc_re = (
                acc_re
                + links_re[row, col] * real_part[:, :, col]
                - links_im[row, col] * imag_part[:, :, col]
            )
            acc_im = (
                acc_im
                + links_re[row, col] * imag_part[:, :, col]
                + links_im[row, col] * real_part[:, :, col]
            )
        rows_re.append(acc_re)
        rows_im.append(acc_im)
    return (jnp.stack(rows_re, 2), jnp.stack(rows_im, 2))


def color_adj(links_re, links_im, real_part, imag_part):
    rows_re = []
    rows_im = []
    for row in range(3):
        acc_re = links_re[0, row] * real_part[:, :, 0] + links_im[0, row] * imag_part[:, :, 0]
        acc_im = links_re[0, row] * imag_part[:, :, 0] - links_im[0, row] * real_part[:, :, 0]
        for col in range(1, 3):
            acc_re = (
                acc_re
                + links_re[col, row] * real_part[:, :, col]
                + links_im[col, row] * imag_part[:, :, col]
            )
            acc_im = (
                acc_im
                + links_re[col, row] * imag_part[:, :, col]
                - links_im[col, row] * real_part[:, :, col]
            )
        rows_re.append(acc_re)
        rows_im.append(acc_im)
    return (jnp.stack(rows_re, 2), jnp.stack(rows_im, 2))


def link_parts(links, direction):
    extent = links.shape[2:]
    return (
        links[direction, :9].reshape((3, 3) + extent),
        links[direction, 9:].reshape((3, 3) + extent),
    )


def neighbour(values, direction, step):
    if direction == 0:
        column = jnp.arange(values.shape[-1]) % LX
        border = LX - 1 if step > 0 else 0
        inside = jnp.roll(values, -step, axis=-1)
        wrapped = jnp.roll(values, step * (LX - 1), axis=-1)
        return jnp.where(column == border, wrapped, inside)
    if direction == 1:
        return jnp.roll(values, -step * LX, axis=-1)
    return jnp.roll(values, -step, axis=-2)


def split_parts(spinor):
    count = spinor.shape[0]
    extent = spinor.shape[2:]
    return (
        spinor[:, :12].reshape((count, 4, 3) + extent),
        spinor[:, 12:].reshape((count, 4, 3) + extent),
    )


def join_parts(real_part, imag_part):
    count = real_part.shape[0]
    extent = real_part.shape[3:]
    return jnp.concatenate(
        [real_part.reshape((count, 12) + extent), imag_part.reshape((count, 12) + extent)], 1
    )


def shards(sources, eigvecs, eigvals, links, damping):
    count = sources.shape[0]
    flat_src = sources.astype(jnp.bfloat16).reshape(count, 24, -1)
    swapped = jnp.concatenate([flat_src[:, 12:], -flat_src[:, :12]], 1)
    stacked = jnp.concatenate([flat_src, swapped], 0).reshape(2 * count, -1)
    flat_vec = eigvecs.reshape(eigvecs.shape[0], -1)
    partial_value = lax.dot_general(
        flat_vec, stacked, (((1,), (1,)), ((), ())), preferred_element_type=jnp.float32
    )
    correlation = lax.psum(partial_value, ("src", "lat", "sub"))
    sites_all = flat_vec.shape[1] // 24 * lax.axis_size(("src", "lat", "sub"))
    correlation = correlation / math.sqrt(24 * sites_all)
    weights = (
        jnp.concatenate([correlation[:, :count].T, correlation[:, count:].T], 0) / eigvals[None, :]
    )
    weights = weights.astype(jnp.bfloat16)
    mixed = jnp.dot(weights, flat_vec, preferred_element_type=jnp.float32)
    middle = mixed.shape[1] // 2
    guess = jnp.concatenate(
        [
            mixed[:count, :middle] - mixed[count:, middle:],
            mixed[:count, middle:] + mixed[count:, :middle],
        ],
        1,
    ).reshape(sources.shape)
    source, iterate = (
        lax.all_to_all(sources, "src", split_axis=0, concat_axis=3, tiled=True),
        lax.all_to_all(guess, "src", split_axis=0, concat_axis=3, tiled=True),
    )
    extent = lax.axis_size(("lat", "sub"))
    place = lax.axis_index(("lat", "sub"))
    slices = links.shape[2]
    slice_index = jnp.arange(slices)
    top_flip = jnp.where(place == extent - 1, -1.0, 1.0)
    bottom_flip = jnp.where(place == 0, -1.0, 1.0)
    top_sign = jnp.where(slice_index == slices - 1, top_flip, 1.0).astype(jnp.float32)[
        :, None, None
    ]
    bottom_sign = jnp.where(slice_index == 0, bottom_flip, 1.0).astype(jnp.float32)[:, None, None]
    time_re, time_im = link_parts(links, 3)
    space_links = []
    for direction in range(3):
        links_re, links_im = link_parts(links, direction)
        space_links.append(
            (
                links_re,
                links_im,
                neighbour(links_re, direction, -1),
                neighbour(links_im, direction, -1),
            )
        )
    rim_links = passed_along(links[3, :, slices - 1 :], ("lat", "sub"), 1)
    behind_links = jnp.concatenate([rim_links, links[3, :, : slices - 1]], 1)
    back_re = behind_links[:9].reshape((3, 3) + behind_links.shape[1:])
    back_im = behind_links[9:].reshape((3, 3) + behind_links.shape[1:])
    rate = damping[:, None, None, None, None]
    for sweep in range(ITERS):
        real_part, imag_part = split_parts(iterate)
        terms = []
        for apply_direction in range(3):
            apply_links_re, apply_links_im, behind_lre, behind_lim = space_links[apply_direction]
            ahead_re = neighbour(real_part, apply_direction, 1)
            ahead_im = neighbour(imag_part, apply_direction, 1)
            carried = color_mul(apply_links_re, apply_links_im, ahead_re, ahead_im)
            terms.append(rebuild(-1.0, apply_direction, *project(-1.0, apply_direction, *carried)))
            behind_re = neighbour(real_part, apply_direction, -1)
            behind_im = neighbour(imag_part, apply_direction, -1)
            carried = color_adj(behind_lre, behind_lim, behind_re, behind_im)
            terms.append(rebuild(1.0, apply_direction, *project(1.0, apply_direction, *carried)))
        padded = padded_2(iterate, ((("lat", "sub"), 2),), 1)
        ahead_re, ahead_im = split_parts(padded[:, :, 2:] * top_sign)
        carried = color_mul(time_re, time_im, ahead_re, ahead_im)
        terms.append(rebuild(-1.0, 3, *project(-1.0, 3, *carried)))
        behind_re, behind_im = split_parts(padded[:, :, :slices] * bottom_sign)
        carried = color_adj(back_re, back_im, behind_re, behind_im)
        terms.append(rebuild(1.0, 3, *project(1.0, 3, *carried)))
        total_re, total_im = terms[0]
        for extra in terms[1:]:
            total_re = total_re + extra[0]
            total_im = total_im + extra[1]
        iterate = iterate + rate * (source - (iterate - HOPPING * join_parts(total_re, total_im)))
    solution = lax.all_to_all(iterate, "src", split_axis=3, concat_axis=0, tiled=True)
    return (guess, solution)


def solution(mesh):
    return jax.shard_map(
        shards,
        mesh=mesh,
        in_specs=(
            P(None, None, ("lat", "sub"), "src", None),
            P(None, None, ("lat", "sub"), "src", None),
            P(),
            P(None, None, ("lat", "sub"), None, None),
            P("src"),
        ),
        out_specs=(
            P(None, None, ("lat", "sub"), "src", None),
            P(None, None, ("lat", "sub"), "src", None),
        ),
        check_vma=False,
    )
```

profile of v0, /device:TPU:1, one launch (start us, length us, event | category | flops | bytes accessed | tf_op | source)
XLA Modules:
  0.0 232.8 jit_solution(8140742136384353029)
XLA Ops:
  0.6 2.6 %convert_reduce_fusion = bf16[8,24,6,128]{3,2,1,0:T(8,128)(2,1)S(1)} fusion(f32[8,24,6,1,128]{4,3,2,1,0:T(1,128)} %param.5), kind=kLoop, calls=%fused_computation.40 | loop fusion | flops 147456 | bytes 884736 | tf_op jit(solution)/shard_map/convert_element_type | solution.py:163
  3.3 0.4 reshape.6009
  3.6 1.0 concatenate.768
  4.7 1.6 copy.464
  6.3 1.3 reshape.6010
  7.9 0.7 copy-done.13
  8.6 0.4 convolution_bitcast_fusion
  9.0 106.1 %psum.7 = f32[32,16]{0,1:T(8,128)S(1)} all-reduce(f32[32,16]{0,1:T(8,128)S(1)} %convolution_bitcast_fusion), channel_id=1, replica_groups=mesh['src'=8,'lat'=32,'sub'=2] {'src','lat','sub'}, use_global_device_ids=true, to_apply=%region_0.0 | all-reduce | flops 512 | bytes 4096 | tf_op jit(solution)/shard_map/psum | solution.py:170
  115.1 0.3 fusion.157
  115.6 1.0 copy.465
  116.6 4.1 %all-to-all-start = ((f32[8,24,6,1,128]{4,1,3,2,0:T(8,128)}), f32[8,24,6,1,128]{4,1,3,2,0:T(8,128)S(1)}, u32[]{:S(2)}, u32[]{:S(2)}) async-start(f32[8,24,6,1,128]{4,1,3,2,0:T(8,128)} %copy.465), calls=%async_computation | async-start | bytes 1179648 | tf_op jit(solution)/shard_map/all_to_all | solution.py:188
  120.7 0.9 slice_bitcast_fusion.1
  121.6 4.1 %collective-permute-start.1 = (f32[18,1,8,128]{3,2,1,0:T(8,128)S(1)}, f32[18,1,8,128]{3,2,1,0:T(8,128)}, u32[]{:S(2)}, u32[]{:S(2)}) collective-permute-start(f32[18,1,8,128]{3,2,1,0:T(8,128)S(1)} %slice_bitcast_fusion.1), channel_id=1, source_target_pairs={{0,1},{1,2},{2,3},{3,4},{4,5},{5,6},{6,7},{7,8},{8,9},{9,10},{10,1... | collective-permute-start | bytes 221192 | tf_op jit(solution)/shard_map/ppermute | solution.py:24
  125.7 2.4 %fusion.194 = (f32[1,9,6,8,128]{4,3,2,1,0:T(8,128)S(1)}, f32[1,9,6,8,128]{4,3,2,1,0:T(8,128)}, f32[1,9,6,8,128]{4,3,2,1,0:T(8,128)S(1)}, f32[1,9,6,8,128]{4,3,2,...) fusion(f32[4,18,6,8,128]{4,3,2,1,0:T(8,128)} %param.8), kind=kLoop, calls=%fused_computation.843 | loop fusion | bytes 3538944 | tf_op jit(solution)/shard_map/slice | solution.py:127
  128.1 0.8 slice.1779
  128.9 0.8 slice.1781
  129.7 0.8 slice_bitcast_fusion.108
  130.5 0.8 slice.1791
  131.3 0.8 slice.1789
  132.1 0.8 slice.3635
  132.9 0.8 slice_bitcast_fusion.66
  133.7 0.8 slice.3627
  134.6 0.8 slice_bitcast_fusion.48
  135.4 0.9 copy.467
  136.9 1.6 maximum_select_fusion.8
  138.5 0.7 slice_bitcast_fusion.90
  139.3 0.8 fusion.129
  140.1 0.8 fusion.145
  140.9 0.7 fusion.97
  141.6 0.7 fusion.113
  142.3 0.7 slice_bitcast_fusion.36
  143.0 1.0 slice_bitcast_fusion
  144.1 0.8 fusion.39
  144.9 0.8 slice_bitcast_fusion.18
  145.8 5.4 %all-to-all-start.1 = ((f32[8,24,6,1,128]{4,1,3,2,0:T(8,128)}), f32[8,24,6,1,128]{4,1,3,2,0:T(8,128)S(1)}, u32[]{:S(2)}, u32[]{:S(2)}) async-start(f32[8,24,6,1,128]{4,1,3,2,0:T(8,128)} %copy.467), calls=%async_computation.1 | async-start | bytes 1179648 | tf_op jit(solution)/shard_map/all_to_all | solution.py:187
  153.3 5.4 %collective-permute-start.2 = (f32[1,24,1,8,128]{4,3,2,1,0:T(8,128)S(1)}, f32[1,24,1,8,128]{4,3,2,1,0:T(8,128)S(1)}, u32[]{:S(2)}, u32[]{:S(2)}) collective-permute-start(f32[1,24,1,8,128]{4,3,2,1,0:T(8,128)S(1)} %get-tuple-element.256), channel_id=1, source_target_pairs={{0,1},{1,2},{2,3},{3,4},{4,5},{5,6},{6,7},{7,8},{8,9},{9,10},{10,1... | collective-permute-start | bytes 294920 | tf_op jit(solution)/shard_map/ppermute | solution.py:34
  158.7 8.2 %collective-permute-start = (f32[1,24,1,8,128]{4,3,2,1,0:T(8,128)S(1)}, f32[1,24,1,8,128]{4,3,2,1,0:T(8,128)S(1)}, u32[]{:S(2)}, u32[]{:S(2)}) collective-permute-start(f32[1,24,1,8,128]{4,3,2,1,0:T(8,128)S(1)} %get-tuple-element.257), channel_id=1, source_target_pairs={{1,0},{2,1},{3,2},{4,3},{5,4},{6,5},{7,6},{8,7},{9,8},{10,9},{11,1... | collective-permute-start | bytes 294920 | tf_op jit(solution)/shard_map/ppermute | solution.py:35
  167.0 0.7 maximum_select_fusion
  168.0 0.4 copy-done.134
  169.0 0.4 copy-done.194
  170.2 0.5 copy-done.4
  171.1 0.3 copy-done.110
  172.3 0.4 copy-done.242
  173.3 0.5 copy-done.7
  174.2 0.4 copy-done.86
  175.4 0.4 copy-done.218
  176.8 0.5 copy-done.74
  178.1 0.4 copy-done.62
  179.7 0.4 fusion.10
  181.4 0.4 maximum_select_fusion.4
  182.8 0.4 maximum_select_fusion.6
  185.1 0.4 copy-done.123
  186.2 0.4 copy-done.243
  187.4 0.4 copy-done.99
  188.3 0.4 multiply_add_fusion.8
  189.2 1.9 collective-permute-start.4
  191.2 11.5 %collective-permute-start.3 = (f32[1,24,1,8,128]{4,3,2,1,0:T(8,128)S(1)}, f32[1,24,1,8,128]{4,3,2,1,0:T(8,128)S(1)}, u32[]{:S(2)}, u32[]{:S(2)}) collective-permute-start(f32[1,24,1,8,128]{4,3,2,1,0:T(8,128)S(1)} %get-tuple-element.243), channel_id=1, source_target_pairs={{1,0},{2,1},{3,2},{4,3},{5,4},{6,5},{7,6},{8,7},{9,8},{10,9},{11,1... | collective-permute-start | bytes 294920 | tf_op jit(solution)/shard_map/ppermute | solution.py:35
  204.6 0.3 copy-done.75
  205.7 0.4 copy-done.63
  207.8 1.0 copy.470
  208.8 6.8 %all-to-all-start.2 = ((f32[1,24,6,8,128]{4,1,2,0,3:T(8,128)}), f32[1,24,6,8,128]{4,1,2,0,3:T(8,128)S(1)}, u32[]{:S(2)}, u32[]{:S(2)}) async-start(f32[1,24,6,8,128]{4,1,2,0,3:T(8,128)} %copy.470), calls=%async_computation.2 | async-start | bytes 1179648 | tf_op jit(solution)/shard_map/all_to_all | solution.py:242
  215.6 1.4 copy.472
  217.0 14.3 %all-to-all-done.2 = f32[1,24,6,8,128]{4,1,2,0,3:T(8,128)S(1)} async-done(((f32[1,24,6,8,128]{4,1,2,0,3:T(8,128)}), f32[1,24,6,8,128]{4,1,2,0,3:T(8,128)S(1)}, u32[]{:S(2)}, u32[]{:S(2)}) %all-to-all-start.2) | async-done | bytes 589856 | tf_op jit(solution)/shard_map/all_to_all | solution.py:242
  231.3 1.4 copy.473
  (716 shorter events, 18.0 us)
Async XLA Ops:
  7.7 1.0 copy-start.13
  7.8 107.3 %copy-start.254 = (f32[32]{0:T(128)S(1)}, f32[32]{0:T(128)}, u32[]{:S(2)}) copy-start(f32[32]{0:T(128)} %param.7) | copy-start | bytes 388
  116.6 29.2 %all-to-all-start = ((f32[8,24,6,1,128]{4,1,3,2,0:T(8,128)}), f32[8,24,6,1,128]{4,1,3,2,0:T(8,128)S(1)}, u32[]{:S(2)}, u32[]{:S(2)}) async-start(f32[8,24,6,1,128]{4,1,3,2,0:T(8,128)} %copy.465), calls=%async_computation | async-start | bytes 1179648 | tf_op jit(solution)/shard_map/all_to_all | solution.py:188
  121.6 22.5 %collective-permute-start.1 = (f32[18,1,8,128]{3,2,1,0:T(8,128)S(1)}, f32[18,1,8,128]{3,2,1,0:T(8,128)}, u32[]{:S(2)}, u32[]{:S(2)}) collective-permute-start(f32[18,1,8,128]{3,2,1,0:T(8,128)S(1)} %slice_bitcast_fusion.1), channel_id=1, source_target_pairs={{0,1},{1,2},{2,3},{3,4},{4,5},{5,6},{6,7},{7,8},{8,9},{9,10},{10,1... | collective-permute-start | bytes 221192 | tf_op jit(solution)/shard_map/ppermute | solution.py:24
  132.9 2.5 %copy-start = (f32[8,24,6,1,128]{4,3,2,1,0:T(1,128)S(1)}, f32[8,24,6,1,128]{4,3,2,1,0:T(1,128)}, u32[]{:S(2)}) copy-start(f32[8,24,6,1,128]{4,3,2,1,0:T(1,128)} %param.5) | copy-start | bytes 1769476
  136.9 2.4 %copy-start.2 = (f32[3,3,6,8,16]{4,3,2,1,0:T(8,128)S(1)}, f32[3,3,6,8,16]{4,3,2,1,0:T(8,128)}, u32[]{:S(2)}) copy-start(f32[3,3,6,8,16]{4,3,2,1,0:T(8,128)} %slice.3635) | copy-start | bytes 82948
  138.5 1.6 copy-start.3
  139.3 30.4 %copy-start.170 = (f32[6,8,128]{2,1,0:T(8,128)}, f32[6,8,128]{2,1,0:T(8,128)S(1)}, u32[]{:S(2)}) copy-start(f32[6,8,128]{2,1,0:T(8,128)S(1)} %get-tuple-element.563) | copy-start | bytes 73732
  139.3 30.4 %copy-start.172 = (f32[6,8,128]{2,1,0:T(8,128)}, f32[6,8,128]{2,1,0:T(8,128)S(1)}, u32[]{:S(2)}) copy-start(f32[6,8,128]{2,1,0:T(8,128)S(1)} %get-tuple-element.570) | copy-start | bytes 73732
  139.3 30.4 %copy-start.174 = (f32[6,8,128]{2,1,0:T(8,128)}, f32[6,8,128]{2,1,0:T(8,128)S(1)}, u32[]{:S(2)}) copy-start(f32[6,8,128]{2,1,0:T(8,128)S(1)} %get-tuple-element.571) | copy-start | bytes 73732
  139.3 30.5 %copy-start.176 = (f32[6,8,128]{2,1,0:T(8,128)}, f32[6,8,128]{2,1,0:T(8,128)S(1)}, u32[]{:S(2)}) copy-start(f32[6,8,128]{2,1,0:T(8,128)S(1)} %get-tuple-element.613) | copy-start | bytes 73732
  139.3 30.5 %copy-start.178 = (f32[6,8,128]{2,1,0:T(8,128)}, f32[6,8,128]{2,1,0:T(8,128)S(1)}, u32[]{:S(2)}) copy-start(f32[6,8,128]{2,1,0:T(8,128)S(1)} %get-tuple-element.614) | copy-start | bytes 73732
  139.3 30.5 %copy-start.180 = (f32[6,8,128]{2,1,0:T(8,128)}, f32[6,8,128]{2,1,0:T(8,128)S(1)}, u32[]{:S(2)}) copy-start(f32[6,8,128]{2,1,0:T(8,128)S(1)} %get-tuple-element.621) | copy-start | bytes 73732
  139.3 3.0 %copy-start.1 = (f32[1,9,6,8,128]{4,3,2,1,0:T(8,128)S(1)}, f32[1,9,6,8,128]{4,3,2,1,0:T(8,128)}, u32[]{:S(2)}) copy-start(f32[1,9,6,8,128]{4,3,2,1,0:T(8,128)} %get-tuple-element.149) | copy-start | bytes 663556
  143.0 34.6 %copy-start.26 = (f32[6,8,128]{2,1,0:T(8,128)}, f32[6,8,128]{2,1,0:T(8,128)S(1)}, u32[]{:S(2)}) copy-start(f32[6,8,128]{2,1,0:T(8,128)S(1)} %get-tuple-element.509) | copy-start | bytes 73732
  143.0 34.6 %copy-start.28 = (f32[6,8,128]{2,1,0:T(8,128)}, f32[6,8,128]{2,1,0:T(8,128)S(1)}, u32[]{:S(2)}) copy-start(f32[6,8,128]{2,1,0:T(8,128)S(1)} %get-tuple-element.516) | copy-start | bytes 73732
  143.0 34.6 %copy-start.30 = (f32[6,8,128]{2,1,0:T(8,128)}, f32[6,8,128]{2,1,0:T(8,128)S(1)}, u32[]{:S(2)}) copy-start(f32[6,8,128]{2,1,0:T(8,128)S(1)} %get-tuple-element.517) | copy-start | bytes 73732
  143.0 34.6 %copy-start.32 = (f32[6,8,128]{2,1,0:T(8,128)}, f32[6,8,128]{2,1,0:T(8,128)S(1)}, u32[]{:S(2)}) copy-start(f32[6,8,128]{2,1,0:T(8,128)S(1)} %get-tuple-element.650) | copy-start | bytes 73732
  143.0 34.6 %copy-start.34 = (f32[6,8,128]{2,1,0:T(8,128)}, f32[6,8,128]{2,1,0:T(8,128)S(1)}, u32[]{:S(2)}) copy-start(f32[6,8,128]{2,1,0:T(8,128)S(1)} %get-tuple-element.651) | copy-start | bytes 73732
  143.0 34.6 %copy-start.36 = (f32[6,8,128]{2,1,0:T(8,128)}, f32[6,8,128]{2,1,0:T(8,128)S(1)}, u32[]{:S(2)}) copy-start(f32[6,8,128]{2,1,0:T(8,128)S(1)} %get-tuple-element.658) | copy-start | bytes 73732
  145.7 33.2 %copy-start.14 = (f32[6,8,128]{2,1,0:T(8,128)}, f32[6,8,128]{2,1,0:T(8,128)S(1)}, u32[]{:S(2)}) copy-start(f32[6,8,128]{2,1,0:T(8,128)S(1)} %get-tuple-element.491) | copy-start | bytes 73732
  145.7 33.2 %copy-start.16 = (f32[6,8,128]{2,1,0:T(8,128)}, f32[6,8,128]{2,1,0:T(8,128)S(1)}, u32[]{:S(2)}) copy-start(f32[6,8,128]{2,1,0:T(8,128)S(1)} %get-tuple-element.498) | copy-start | bytes 73732
  145.7 33.2 %copy-start.18 = (f32[6,8,128]{2,1,0:T(8,128)}, f32[6,8,128]{2,1,0:T(8,128)S(1)}, u32[]{:S(2)}) copy-start(f32[6,8,128]{2,1,0:T(8,128)S(1)} %get-tuple-element.499) | copy-start | bytes 73732
  145.7 33.2 %copy-start.20 = (f32[6,8,128]{2,1,0:T(8,128)}, f32[6,8,128]{2,1,0:T(8,128)S(1)}, u32[]{:S(2)}) copy-start(f32[6,8,128]{2,1,0:T(8,128)S(1)} %get-tuple-element.659) | copy-start | bytes 73732
  145.7 33.2 %copy-start.22 = (f32[6,8,128]{2,1,0:T(8,128)}, f32[6,8,128]{2,1,0:T(8,128)S(1)}, u32[]{:S(2)}) copy-start(f32[6,8,128]{2,1,0:T(8,128)S(1)} %get-tuple-element.660) | copy-start | bytes 73732
  145.7 33.2 %copy-start.24 = (f32[6,8,128]{2,1,0:T(8,128)}, f32[6,8,128]{2,1,0:T(8,128)S(1)}, u32[]{:S(2)}) copy-start(f32[6,8,128]{2,1,0:T(8,128)S(1)} %get-tuple-element.667) | copy-start | bytes 73732
  145.8 33.9 %all-to-all-start.1 = ((f32[8,24,6,1,128]{4,1,3,2,0:T(8,128)}), f32[8,24,6,1,128]{4,1,3,2,0:T(8,128)S(1)}, u32[]{:S(2)}, u32[]{:S(2)}) async-start(f32[8,24,6,1,128]{4,1,3,2,0:T(8,128)} %copy.467), calls=%async_computation.1 | async-start | bytes 1179648 | tf_op jit(solution)/shard_map/all_to_all | solution.py:187
  153.3 23.1 %collective-permute-start.2 = (f32[1,24,1,8,128]{4,3,2,1,0:T(8,128)S(1)}, f32[1,24,1,8,128]{4,3,2,1,0:T(8,128)S(1)}, u32[]{:S(2)}, u32[]{:S(2)}) collective-permute-start(f32[1,24,1,8,128]{4,3,2,1,0:T(8,128)S(1)} %get-tuple-element.256), channel_id=1, source_target_pairs={{0,1},{1,2},{2,3},{3,4},{4,5},{5,6},{6,7},{7,8},{8,9},{9,10},{10,1... | collective-permute-start | bytes 294920 | tf_op jit(solution)/shard_map/ppermute | solution.py:34
  158.7 17.8 %collective-permute-start = (f32[1,24,1,8,128]{4,3,2,1,0:T(8,128)S(1)}, f32[1,24,1,8,128]{4,3,2,1,0:T(8,128)S(1)}, u32[]{:S(2)}, u32[]{:S(2)}) collective-permute-start(f32[1,24,1,8,128]{4,3,2,1,0:T(8,128)S(1)} %get-tuple-element.257), channel_id=1, source_target_pairs={{1,0},{2,1},{3,2},{4,3},{5,4},{6,5},{7,6},{8,7},{9,8},{10,9},{11,1... | collective-permute-start | bytes 294920 | tf_op jit(solution)/shard_map/ppermute | solution.py:35
  166.9 0.9 copy-start.158
  166.9 0.9 copy-start.160
  166.9 0.9 copy-start.162
  166.9 0.9 copy-start.164
  166.9 0.9 copy-start.166
  166.9 0.9 copy-start.168
  166.9 1.0 copy-start.146
  166.9 1.0 copy-start.148
  166.9 1.0 copy-start.150
  167.0 1.0 copy-start.152
  167.0 1.0 copy-start.154
  167.0 1.0 copy-start.156
  170.1 0.9 copy-start.122
  170.1 0.9 copy-start.124
  170.1 0.9 copy-start.126
  170.1 0.9 copy-start.128
  170.1 0.9 copy-start.130
  170.1 0.9 copy-start.132
  173.2 0.9 copy-start.98
  173.2 0.9 copy-start.100
  173.2 0.9 copy-start.102
  173.2 0.9 copy-start.104
  173.2 0.9 copy-start.106
  173.2 0.9 copy-start.108
  181.4 0.9 copy-start.147
  181.4 0.9 copy-start.149
  184.8 0.9 copy-start.111
  184.8 0.9 copy-start.113
  184.8 0.9 copy-start.115
  184.8 0.9 copy-start.117
  184.9 0.9 copy-start.119
  184.9 0.9 copy-start.121
  189.2 15.0 %collective-permute-start.4 = (f32[1,24,1,8,128]{4,3,2,1,0:T(8,128)S(1)}, f32[1,24,1,8,128]{4,3,2,1,0:T(8,128)S(1)}, u32[]{:S(2)}, u32[]{:S(2)}) collective-permute-start(f32[1,24,1,8,128]{4,3,2,1,0:T(8,128)S(1)} %get-tuple-element.242), channel_id=1, source_target_pairs={{0,1},{1,2},{2,3},{3,4},{4,5},{5,6},{6,7},{7,8},{8,9},{9,10},{10,1... | collective-permute-start | bytes 294920 | tf_op jit(solution)/shard_map/ppermute | solution.py:34
  191.2 13.1 %collective-permute-start.3 = (f32[1,24,1,8,128]{4,3,2,1,0:T(8,128)S(1)}, f32[1,24,1,8,128]{4,3,2,1,0:T(8,128)S(1)}, u32[]{:S(2)}, u32[]{:S(2)}) collective-permute-start(f32[1,24,1,8,128]{4,3,2,1,0:T(8,128)S(1)} %get-tuple-element.243), channel_id=1, source_target_pairs={{1,0},{2,1},{3,2},{4,3},{5,4},{6,5},{7,6},{8,7},{9,8},{10,9},{11,1... | collective-permute-start | bytes 294920 | tf_op jit(solution)/shard_map/ppermute | solution.py:35
  208.8 22.5 %all-to-all-start.2 = ((f32[1,24,6,8,128]{4,1,2,0,3:T(8,128)}), f32[1,24,6,8,128]{4,1,2,0,3:T(8,128)S(1)}, u32[]{:S(2)}, u32[]{:S(2)}) async-start(f32[1,24,6,8,128]{4,1,2,0,3:T(8,128)} %copy.470), calls=%async_computation.2 | async-start | bytes 1179648 | tf_op jit(solution)/shard_map/all_to_all | solution.py:242
  (199 other events, 155.2 us)
where the time goes:
time: 235 us; the launch traced here: 233 us
  blocking collectives  106 us (45%)
  starting transfers between devices  47.4 us (20%)
  local copies, waits for them, and re-layouts  38.7 us (16%)
  other arithmetic  20.1 us (9%)
  waiting for transfers between devices  14.4 us (6%)
  between operations  5.37 us (2%)
    psum x1, blocking collectives, shards(): correlation = lax.psum(partial_value, ('src', 'lat', 'sub'))  106 us
    ppermute x2, starting transfers between devices, padded_2(): after = lax.ppermute(first, axis, down)  19.7 us
    unnamed x515, local copies, waits for them, and re-layouts  15.9 us
    all_to_all x1, waiting for transfers between devices, shards(): lax.all_to_all(iterate, 'src', split_axis=3, concat_axis=0, tiled=True)  14.3 us
    ppermute x2, starting transfers between devices, padded_2(): before = lax.ppermute(last, axis, up)  7.3 us
    all_to_all x1, starting transfers between devices, shards(): lax.all_to_all(iterate, 'src', split_axis=3, concat_axis=0, tiled=True)  6.78 us
    all_to_all x1, starting transfers between devices, shards(): lax.all_to_all(sources, 'src', split_axis=0, concat_axis=3, tiled=True)  5.39 us
  transfers between devices with their start and end apart: 8, of which 1 were waited for; matrix products, arithmetic and copies ran while one was open for 13% of the time, Pallas kernels for 0%

commit v1 on v0

v1 whole, which is shorter than its diff:
```python
import functools
import math

import jax
import jax.numpy as jnp
from jax import lax
from jax.experimental import pallas as pl
from jax.experimental.pallas import tpu as pltpu
from jax.sharding import PartitionSpec as P

LX = 16
ITERS = 2
HOPPING = 0.12

BLOCKS = [
    {(0, 1): 1, (1, 0): 1},
    {(0, 1): 2, (1, 0): 0},
    {(0, 0): 1, (1, 1): 3},
    {(0, 0): 0, (1, 1): 0},
]


def times_power(power, re, im):
    return [
        ((1, re), (1, im)),
        ((-1, im), (1, re)),
        ((-1, re), (-1, im)),
        ((1, im), (-1, re)),
    ][power % 4]


def add_signed(base, sign, value):
    return base + value if sign > 0 else base - value


def project(sign, direction, load):
    half = []
    for row in range(2):
        col, power = next((c, p) for (r, c), p in BLOCKS[direction].items() if r == row)
        colours = []
        for colour in range(3):
            lower_re, lower_im = load(0, 2 + col, colour), load(1, 2 + col, colour)
            (sr, vr), (si, vi) = times_power(power, lower_re, lower_im)
            colours.append(
                (
                    add_signed(load(0, row, colour), sr * sign, vr),
                    add_signed(load(1, row, colour), si * sign, vi),
                )
            )
        half.append(colours)
    return half


def rebuild_into(acc, sign, direction, half):
    def put(key, sgn, value):
        if key in acc:
            acc[key] = add_signed(acc[key], sgn, value)
        else:
            acc[key] = value if sgn > 0 else -value

    for row in range(2):
        for colour in range(3):
            re, im = half[row][colour]
            put((0, row, colour), 1, re)
            put((1, row, colour), 1, im)
    for (row, col), power in BLOCKS[direction].items():
        for colour in range(3):
            re, im = half[row][colour]
            (sr, vr), (si, vi) = times_power(-power, re, im)
            put((0, 2 + col, colour), sr * sign, vr)
            put((1, 2 + col, colour), si * sign, vi)


def colour_mul(link, half, adjoint):
    out = []
    for spin in range(2):
        rows = []
        for row in range(3):
            re = im = None
            for col in range(3):
                lr, li = link[(col, row)] if adjoint else link[(row, col)]
                hr, hi = half[spin][col]
                if adjoint:
                    tr, ti = lr * hr + li * hi, lr * hi - li * hr
                else:
                    tr, ti = lr * hr - li * hi, lr * hi + li * hr
                re = tr if re is None else re + tr
                im = ti if im is None else im + ti
            rows.append((re, im))
        out.append(rows)
    return out


def map_half(fn, half):
    return [[(fn(re), fn(im)) for re, im in rows] for rows in half]


def load_half(load):
    return [[(load(3 * s + c), load(6 + 3 * s + c)) for c in range(3)] for s in range(2)]


def store_half(store, half):
    for s in range(2):
        for c in range(3):
            store(3 * s + c, half[s][c][0])
            store(6 + 3 * s + c, half[s][c][1])


def load_link(links_ref, slices, zdim, direction, t, z):
    def one(comp):
        row = ((direction * 18 + comp) * slices + t) * zdim + z
        return jnp.broadcast_to(links_ref[pl.ds(row, 1), :], (8, 128))

    return {(a, c): (one(3 * a + c), one(9 + 3 * a + c)) for a in range(3) for c in range(3)}


def moved(direction, step):
    def fn(v):
        if direction == 1:
            return pltpu.roll(v, (-step * LX) % 128, 1)
        column = lax.rem(lax.broadcasted_iota(jnp.int32, v.shape, 1), LX)
        border = LX - 1 if step > 0 else 0
        inside = pltpu.roll(v, (-step) % 128, 1)
        wrapped = pltpu.roll(v, (step * (LX - 1)) % 128, 1)
        return jnp.where(column == border, wrapped, inside)

    return fn


def correlation_kernel(eig_ref, src_ref, damp_ref, out_ref, *, nev, slices):
    comps = 24
    sources = 8
    lhs = jnp.concatenate(
        [
            src_ref[pl.ds(t, sources * comps, stride=slices), :].astype(jnp.bfloat16)
            for t in range(slices)
        ],
        axis=1,
    )
    rhs = jnp.concatenate(
        [eig_ref[:, t].reshape(nev * comps, 128) for t in range(slices)], axis=1
    )
    full = lax.dot_general(
        lhs, rhs, (((1,), (1,)), ((), ())), preferred_element_type=jnp.float32
    )
    row = lax.rem(lax.broadcasted_iota(jnp.int32, (sources * comps, 1), 0), comps)
    col = lax.rem(lax.broadcasted_iota(jnp.int32, (1, nev * comps), 1), comps)
    gap = row - col
    straight = jnp.where(gap == 0, full, 0.0)
    crossed = jnp.where(gap == 12, full, 0.0) - jnp.where(gap == -12, full, 0.0)
    straight = straight.reshape(sources, comps, nev * comps).sum(1)
    crossed = crossed.reshape(sources, comps, nev * comps).sum(1)
    first = lax.broadcasted_iota(jnp.int32, (nev * comps, 128), 0)
    lane = lax.broadcasted_iota(jnp.int32, (nev * comps, 128), 1)

    def gather(which):
        start = (lane - which * nev) * comps
        return jnp.where((first >= start) & (first < start + comps), 1.0, 0.0)

    dot = functools.partial(
        jnp.dot, precision=lax.Precision.HIGHEST, preferred_element_type=jnp.float32
    )
    total = dot(straight, gather(0)) + dot(crossed, gather(1))
    mine = lax.axis_index("src")
    holder = (lax.axis_index("lat") == 0) & (lax.axis_index("sub") == 0)
    value = jnp.where(holder, damp_ref[0], 0.0)
    at_row = lax.broadcasted_iota(jnp.int32, (8, 128), 0) == mine
    at_lane = lax.broadcasted_iota(jnp.int32, (8, 128), 1) == 2 * nev
    total = total + jnp.where(at_row & at_lane, value, 0.0)
    out_ref[...] = jnp.broadcast_to(total[None], out_ref.shape)


def emit_halos(load, links_ref, z, t, zup_ref, zdown_ref, slices, zdim):
    up = project(1, 2, load)
    up = colour_mul(load_link(links_ref, slices, zdim, 2, t, z), up, True)
    store_half(lambda i, v: zup_ref.__setitem__((t, i), v), up)
    down = project(-1, 2, load)
    store_half(lambda i, v: zdown_ref.__setitem__((t, i), v), down)


def emit_time_halos(x_ref, links_ref, z, tup_ref, tdown_ref, slices, zdim):
    extent = lax.axis_size(("lat", "sub"))
    place = lax.axis_index(("lat", "sub"))
    up_sign = jnp.where(place == extent - 1, -1.0, 1.0)
    down_sign = jnp.where(place == 0, -1.0, 1.0)
    last = slices - 1
    up = project(1, 3, lambda p, s, c: x_ref[last, 12 * p + 3 * s + c])
    up = colour_mul(load_link(links_ref, slices, zdim, 3, last, z), up, True)
    store_half(lambda i, v: tup_ref.__setitem__(i, v * up_sign), up)
    down = project(-1, 3, lambda p, s, c: x_ref[0, 12 * p + 3 * s + c])
    store_half(lambda i, v: tdown_ref.__setitem__(i, v * down_sign), down)


def guess_kernel(
    part_ref, ev_ref, eig_ref, links_ref,
    guess_ref, x_ref, rate_ref, zup_ref, zdown_ref, tup_ref, tdown_ref,
    *, nev, slices, zdim, norm,
):
    comps = 24
    total = part_ref[0]
    for i in range(1, part_ref.shape[0]):
        total = total + part_ref[i]
    ev = ev_ref[...]
    w_re = ((total[:, :nev] / norm) / ev).astype(jnp.bfloat16)
    w_im = ((total[:, nev : 2 * nev] / norm) / ev).astype(jnp.bfloat16)
    rate_ref[...] = jnp.broadcast_to(total[:, 2 * nev : 2 * nev + 1], (8, 128))
    row = lax.broadcasted_iota(jnp.int32, (nev, nev * comps), 0) * comps
    col = lax.broadcasted_iota(jnp.int32, (nev, nev * comps), 1)
    spread = jnp.where((col >= row) & (col < row + comps), 1.0, 0.0).astype(jnp.bfloat16)
    w_re = jnp.dot(w_re, spread, preferred_element_type=jnp.float32)
    w_im = jnp.dot(w_im, spread, preferred_element_type=jnp.float32)
    comp = lax.rem(lax.broadcasted_iota(jnp.int32, (8, nev * comps), 1), comps)
    blocks = []
    for c in range(comps):
        other, turned = (c + 12, -w_im) if c < 12 else (c - 12, w_im)
        blocks.append(jnp.where(comp == c, w_re, jnp.where(comp == other, turned, 0.0)))
    mix = jnp.concatenate(blocks, axis=0).astype(jnp.bfloat16)
    for t in range(slices):
        res = jnp.dot(
            mix, eig_ref[:, t].reshape(nev * comps, 128), preferred_element_type=jnp.float32
        )
        x_ref[t] = res.reshape(comps, 8, 128)
    z = lax.axis_index("src")

    def step(t, carry):
        for c in range(comps):
            guess_ref[pl.ds(c * slices + t, 8, stride=comps * slices), :] = x_ref[t, c]
        emit_halos(
            lambda p, s, c: x_ref[t, 12 * p + 3 * s + c],
            links_ref, z, t, zup_ref, zdown_ref, slices, zdim,
        )
        return carry

    lax.fori_loop(0, slices, step, 0)
    emit_time_halos(x_ref, links_ref, z, tup_ref, tdown_ref, slices, zdim)


def sweep_slice(x_ref, src_ref, links_ref, rate, from_below, from_above, behind_ref, tin_ref, t, z, slices, zdim):
    load = lambda p, s, c: x_ref[t, 12 * p + 3 * s + c]
    acc = {}
    for direction in range(2):
        link = load_link(links_ref, slices, zdim, direction, t, z)
        ahead = map_half(moved(direction, 1), project(-1, direction, load))
        rebuild_into(acc, -1, direction, colour_mul(link, ahead, False))
        behind = colour_mul(link, project(1, direction, load), True)
        rebuild_into(acc, 1, direction, map_half(moved(direction, -1), behind))
    link = load_link(links_ref, slices, zdim, 2, t, z)
    ahead = load_half(lambda i: from_above[t, i])
    rebuild_into(acc, -1, 2, colour_mul(link, ahead, False))
    rebuild_into(acc, 1, 2, load_half(lambda i: from_below[t, i]))
    link = load_link(links_ref, slices, zdim, 3, t, z)
    last = t == slices - 1
    following = jnp.minimum(t + 1, slices - 1)
    ahead = project(-1, 3, lambda p, s, c: x_ref[following, 12 * p + 3 * s + c])
    edge = load_half(lambda i: tin_ref[i])
    ahead = [
        [
            tuple(jnp.where(last, e, a) for a, e in zip(ahead[s][c], edge[s][c]))
            for c in range(3)
        ]
        for s in range(2)
    ]
    rebuild_into(acc, -1, 3, colour_mul(link, ahead, False))
    rebuild_into(acc, 1, 3, load_half(lambda i: behind_ref[i]))
    up = colour_mul(link, project(1, 3, load), True)
    store_half(lambda i, v: behind_ref.__setitem__(i, v), up)
    out = {}
    for (p, s, c), hop in acc.items():
        comp = 12 * p + 3 * s + c
        source = src_ref[pl.ds(comp * slices + t, 8, stride=24 * slices), :]
        value = load(p, s, c)
        out[(p, s, c)] = value + rate * (source - (value - HOPPING * hop))
    return out


def sweep_kernel(
    x_ref, src_ref, links_ref, rate_ref, below_ref, above_ref, tbelow_ref, tabove_ref, *refs,
    slices, zdim, final,
):
    z = lax.axis_index("src")
    behind_ref = refs[-1]
    behind_ref[...] = tbelow_ref[...]

    def step(t, carry):
        rate = rate_ref[...]
        new = sweep_slice(
            x_ref, src_ref, links_ref, rate, below_ref, above_ref, behind_ref, tabove_ref,
            t, z, slices, zdim,
        )
        for (p, s, c), value in new.items():
            comp = 12 * p + 3 * s + c
            if final:
                refs[0][pl.ds(comp * slices + t, 8, stride=24 * slices), :] = value
            else:
                refs[0][t, comp] = value
        if not final:
            emit_halos(
                lambda p, s, c: new[(p, s, c)],
                links_ref, z, t, refs[1], refs[2], slices, zdim,
            )
        return carry

    lax.fori_loop(0, slices, step, 0)
    if not final:
        emit_time_halos(refs[0], links_ref, z, refs[3], refs[4], slices, zdim)


def vmem():
    return pl.BlockSpec(memory_space=pltpu.VMEM)


def call(kernel, outs, name, ins, flops, smem=(), scratch=()):
    return pl.pallas_call(
        kernel,
        out_shape=outs,
        in_specs=[
            pl.BlockSpec(memory_space=pltpu.SMEM) if i in smem else vmem() for i in range(ins)
        ],
        out_specs=jax.tree.map(lambda _: vmem(), outs),
        scratch_shapes=list(scratch),
        name=name,
        compiler_params=pltpu.CompilerParams(vmem_limit_bytes=24 << 20),
        cost_estimate=pl.CostEstimate(
            flops=flops, bytes_accessed=3_000_000, transcendentals=0
        ),
    )


def shards(sources, eigvecs, eigvals, links, damping):
    count, comps, slices = sources.shape[:3]
    nev = eigvecs.shape[0]
    zdim = links.shape[3]
    devices = lax.axis_size(("src", "lat", "sub"))
    norm = math.sqrt(comps * slices * 128 * devices)
    f32 = jnp.float32

    src = sources.reshape(count * comps * slices, 128)
    eig = eigvecs.transpose(0, 2, 3, 1, 4).reshape(nev, slices, comps, 128)
    flat_links = links.reshape(4 * 18 * slices * zdim, 128)

    shape = lambda *dims: jax.ShapeDtypeStruct(dims, f32)
    lat, rest = lax.axis_size("lat"), lax.axis_size(("sub", "src"))
    partial = call(
        functools.partial(correlation_kernel, nev=nev, slices=slices),
        shape(lat, 8, 128), "correlation", 3, 226_000_000, smem=(2,),
    )(eig, src, damping)
    partial = lax.all_to_all(partial, "lat", 0, 0, tiled=True)
    partial = jnp.broadcast_to(partial.sum(0)[None], (rest, 8, 128))
    partial = lax.all_to_all(partial, ("sub", "src"), 0, 0, tiled=True)

    field = shape(slices, comps, 8, 128)
    halos = (shape(slices, 12, 8, 128),) * 2 + (shape(12, 8, 128),) * 2
    flat = shape(count * comps * slices, 128)
    guess, x, rate, *send = call(
        functools.partial(guess_kernel, nev=nev, slices=slices, zdim=zdim, norm=norm),
        (flat, field, shape(8, 128)) + halos, "guess", 4, 226_000_000,
    )(partial, eigvals.reshape(1, nev), eig, flat_links)

    def exchange(send):
        zup, zdown, tup, tdown = send
        nz, nt = lax.axis_size("src"), lax.axis_size(("lat", "sub"))
        up = lambda n: [(i, (i + 1) % n) for i in range(n)]
        down = lambda n: [((i + 1) % n, i) for i in range(n)]
        return (
            lax.ppermute(zup, "src", up(nz)),
            lax.ppermute(zdown, "src", down(nz)),
            lax.ppermute(tup, ("lat", "sub"), up(nt)),
            lax.ppermute(tdown, ("lat", "sub"), down(nt)),
        )

    for sweep in range(ITERS):
        final = sweep == ITERS - 1
        got = exchange(send)
        outs = flat if final else (field,) + halos
        res = call(
            functools.partial(sweep_kernel, slices=slices, zdim=zdim, final=final),
            outs, "last_sweep" if final else "sweep", 8, 10_000_000,
            scratch=[pltpu.VMEM((12, 8, 128), f32)],
        )(x, src, flat_links, rate, *got)
        if final:
            x = res
        else:
            x, *send = res
    return (guess.reshape(sources.shape), x.reshape(sources.shape))


def solution(mesh):
    return jax.shard_map(
        shards,
        mesh=mesh,
        in_specs=(
            P(None, None, ("lat", "sub"), "src", None),
            P(None, None, ("lat", "sub"), "src", None),
            P(),
            P(None, None, ("lat", "sub"), None, None),
            P("src"),
        ),
        out_specs=(
            P(None, None, ("lat", "sub"), "src", None),
            P(None, None, ("lat", "sub"), "src", None),
        ),
        check_vma=False,
    )
```

time: 235 us -> 99 us (0.42)
  the two profiles are of different devices: /device:TPU:1 before, /device:TPU:62 now
where the time goes in v1:
time: 99 us; the launch traced here: 98.5 us
  starting transfers between devices  39.4 us (40%)
  blocking collectives  33.7 us (34%)
  waiting for transfers between devices  12.9 us (13%)
  Pallas kernels  7.28 us (7%)
  local copies, waits for them, and re-layouts  3.62 us (4%)
  between operations  1.53 us (2%)
    all_to_all x1, blocking collectives, shards(): partial = lax.all_to_all(partial, ('sub', 'src'), 0, 0, tiled=True)  18 us
    all_to_all x1, blocking collectives, shards(): partial = lax.all_to_all(partial, 'lat', 0, 0, tiled=True)  15.7 us
    ppermute x2, starting transfers between devices, exchange(): lax.ppermute(tup, ('lat', 'sub'), up(nt))  15.2 us
    ppermute x2, waiting for transfers between devices, exchange(): lax.ppermute(tdown, ('lat', 'sub'), down(nt))  12.3 us
    ppermute x2, starting transfers between devices, exchange(): lax.ppermute(zdown, 'src', down(nz))  10.5 us
    ppermute x2, starting transfers between devices, exchange(): lax.ppermute(tdown, ('lat', 'sub'), down(nt))  9.53 us
    ppermute x2, starting transfers between devices, exchange(): lax.ppermute(zup, 'src', up(nz))  4.21 us
    pallas_call x2, Pallas kernels, shards(): call(functools.partial(sweep_kernel, slices=slices, zdim=zdim, final=fina...  4.04 us
  transfers between devices with their start and end apart: 8, of which 3 were waited for; matrix products, arithmetic and copies ran while one was open for 0% of the time, Pallas kernels for 0%

profile of v1, /device:TPU:62, one launch (start us, length us, event | category | flops | bytes accessed | tf_op | source)
XLA Modules:
  0.0 98.5 jit_solution(14198712150698729640)
XLA Ops:
  0.6 0.0 copy-start
  1.4 0.0 copy-start.1
  1.4 1.1 %copy-done.1 = f32[8,24,6,1,128]{4,3,2,1,0:T(1,128)S(1)} copy-done((f32[8,24,6,1,128]{4,3,2,1,0:T(1,128)S(1)}, f32[8,24,6,1,128]{4,3,2,1,0:T(1,128)}, u32[]{:S(2)}) %copy-start.1) | copy-done | bytes 589848
  2.5 0.0 copy-start.3
  2.5 1.3 %copy-done.3 = bf16[32,24,6,1,128]{4,1,3,2,0:T(8,128)(2,1)S(1)} copy-done((bf16[32,24,6,1,128]{4,1,3,2,0:T(8,128)(2,1)S(1)}, bf16[32,24,6,1,128]{4,1,3,2,0:T(8,128)(2,1)}, u32[]{:S(2)}) %copy-start.3) | copy-done | bytes 1179672
  3.8 0.0 copy-start.5
  3.8 1.3 %correlation.1 = f32[32,8,128]{2,1,0:T(8,128)S(1)} custom-call(bf16[32,6,24,128]{3,2,1,0:T(8,128)(2,1)S(1)} %bitcast.16, f32[1152,128]{1,0:T(8,128)S(1)} %bitcast.13, f32[1]{0:T(128)S(6)} %copy.13.damp_ref), custom_call_target="tpu_custom_call" | custom-call | flops 226000000 | bytes 3000000 | tf_op jit(solution)/shard_map/correlation/pallas_call | solution.py:343
  5.0 0.0 copy-start.2
  5.0 15.7 %all_to_all.10 = f32[32,8,128]{2,1,0:T(8,128)S(1)} all-to-all(f32[32,8,128]{2,1,0:T(8,128)S(1)} %correlation.1), channel_id=1, replica_groups=mesh['src'=8,'lat'=32,'sub'=2] {'lat'}, dimensions={0} | all-to-all | bytes 262144 | tf_op jit(solution)/shard_map/all_to_all | solution.py:347
  20.8 18.0 %all_to_all.11.part_ref = f32[16,8,128]{2,1,0:T(8,128)S(1)} all-to-all(f32[16,8,128]{2,1,0:T(8,128)S(1)} %broadcast_in_dim.2), channel_id=1, replica_groups=mesh['src'=8,'lat'=32,'sub'=2] {'sub','src'}, dimensions={0} | all-to-all | bytes 131072 | tf_op jit(solution)/shard_map/all_to_all | solution.py:349
  38.8 0.0 copy-done
  38.8 0.0 copy-done.5
  38.8 0.0 copy-start.4
  38.8 1.3 %copy-done.4 = bf16[32,24,6,1,128]{4,1,3,2,0:T(8,128)(2,1)S(1)} copy-done((bf16[32,24,6,1,128]{4,1,3,2,0:T(8,128)(2,1)S(1)}, bf16[32,24,6,1,128]{4,1,3,2,0:T(8,128)(2,1)}, u32[]{:S(2)}) %copy-start.4) | copy-done | bytes 1179672
  40.1 2.0 %guess.1 = (f32[1152,128]{1,0:T(8,128)}, f32[6,24,8,128]{3,2,1,0:T(8,128)S(1)}, f32[8,128]{1,0:T(8,128)S(1)}, f32[6,12,8,128]{3,2,1,0:T(8,128)S(1)}, f32[6,12,8,...) custom-call(f32[16,8,128]{2,1,0:T(8,128)S(1)} %all_to_all.11.part_ref, ...), custom_call_target="tpu_custom_call" | custom-call | flops 226000000 | bytes 3000000 | tf_op jit(solution)/shard_map/guess/pallas_call | solution.py:354
  42.1 2.3 %collective-permute-start = (f32[6,12,8,128]{3,2,1,0:T(8,128)S(1)}, f32[6,12,8,128]{3,2,1,0:T(8,128)S(1)}, u32[]{:S(2)}, u32[]{:S(2)}) collective-permute-start(f32[6,12,8,128]{3,2,1,0:T(8,128)S(1)} %get-tuple-element.17), channel_id=1, source_target_pairs={{0,64},{64,128},{128,192},{192,256},{256,320},{320,384},{384,448},... | collective-permute-start | bytes 884744 | tf_op jit(solution)/shard_map/ppermute | solution.py:365
  44.4 5.1 %collective-permute-start.1 = (f32[6,12,8,128]{3,2,1,0:T(8,128)S(1)}, f32[6,12,8,128]{3,2,1,0:T(8,128)S(1)}, u32[]{:S(2)}, u32[]{:S(2)}) collective-permute-start(f32[6,12,8,128]{3,2,1,0:T(8,128)S(1)} %get-tuple-element.18), channel_id=1, source_target_pairs={{64,0},{128,64},{192,128},{256,192},{320,256},{384,320},{448,384},... | collective-permute-start | bytes 884744 | tf_op jit(solution)/shard_map/ppermute | solution.py:366
  49.4 3.0 %collective-permute-start.2 = (f32[12,8,128]{2,1,0:T(8,128)S(1)}, f32[12,8,128]{2,1,0:T(8,128)S(1)}, u32[]{:S(2)}, u32[]{:S(2)}) collective-permute-start(f32[12,8,128]{2,1,0:T(8,128)S(1)} %get-tuple-element.19), channel_id=1, source_target_pairs={{0,1},{1,2},{2,3},{3,4},{4,5},{5,6},{6,7},{7,8},{8,9},{9,10},{10,1... | collective-permute-start | bytes 147464 | tf_op jit(solution)/shard_map/ppermute | solution.py:367
  52.5 7.6 %collective-permute-start.3 = (f32[12,8,128]{2,1,0:T(8,128)S(1)}, f32[12,8,128]{2,1,0:T(8,128)S(1)}, u32[]{:S(2)}, u32[]{:S(2)}) collective-permute-start(f32[12,8,128]{2,1,0:T(8,128)S(1)} %get-tuple-element.20), channel_id=1, source_target_pairs={{1,0},{2,1},{3,2},{4,3},{5,4},{6,5},{7,6},{8,7},{9,8},{10,9},{11,1... | collective-permute-start | bytes 147464 | tf_op jit(solution)/shard_map/ppermute | solution.py:368
  60.1 0.6 collective-permute-done.2.tbelow_ref
  60.7 4.3 %collective-permute-done.3.tabove_ref = f32[12,8,128]{2,1,0:T(8,128)S(1)} collective-permute-done((f32[12,8,128]{2,1,0:T(8,128)S(1)}, f32[12,8,128]{2,1,0:T(8,128)S(1)}, u32[]{:S(2)}, u32[]{:S(2)}) %collective-permute-start.3) | collective-permute-done | bytes 49184 | tf_op jit(solution)/shard_map/ppermute | solution.py:368
  65.0 0.0 collective-permute-done.below_ref
  65.0 0.0 collective-permute-done.1.above_ref
  65.0 0.0 copy-done.2
  65.0 1.7 %sweep.1 = (f32[6,24,8,128]{3,2,1,0:T(8,128)S(1)}, f32[6,12,8,128]{3,2,1,0:T(8,128)S(1)}, f32[6,12,8,128]{3,2,1,0:T(8,128)S(1)}, f32[12,8,128]{2,1,0:T(8,128)S(1)}, f32[12,8,128]{2,1,0:T(8,128)S(1)}) custom-call(f32[6,24,8,128]{3,2,1,0:T(8,128)S(1)} %get-tuple-element.15.x_ref, f32[1152,128]{1,0:T(8,128)S(1)} %bitcast.14, f32[3456,128]{1,0:T(8,128)S(1)} %bitcast.11, ...), custom_call_target="tpu_custom_call" | custom-call | flops 10000000 | bytes 3000000 | tf_op jit(solution)/shard_map/sweep/pallas_call | solution.py:375
  66.7 1.9 %collective-permute-start.4 = (f32[6,12,8,128]{3,2,1,0:T(8,128)S(1)}, f32[6,12,8,128]{3,2,1,0:T(8,128)S(1)}, u32[]{:S(2)}, u32[]{:S(2)}) collective-permute-start(f32[6,12,8,128]{3,2,1,0:T(8,128)S(1)} %get-tuple-element.22), channel_id=1, source_target_pairs={{0,64},{64,128},{128,192},{192,256},{256,320},{320,384},{384,448},... | collective-permute-start | bytes 884744 | tf_op jit(solution)/shard_map/ppermute | solution.py:365
  68.6 5.4 %collective-permute-start.5 = (f32[6,12,8,128]{3,2,1,0:T(8,128)S(1)}, f32[6,12,8,128]{3,2,1,0:T(8,128)S(1)}, u32[]{:S(2)}, u32[]{:S(2)}) collective-permute-start(f32[6,12,8,128]{3,2,1,0:T(8,128)S(1)} %get-tuple-element.23), channel_id=1, source_target_pairs={{64,0},{128,64},{192,128},{256,192},{320,256},{384,320},{448,384},... | collective-permute-start | bytes 884744 | tf_op jit(solution)/shard_map/ppermute | solution.py:366
  74.1 12.2 %collective-permute-start.6 = (f32[12,8,128]{2,1,0:T(8,128)S(1)}, f32[12,8,128]{2,1,0:T(8,128)S(1)}, u32[]{:S(2)}, u32[]{:S(2)}) collective-permute-start(f32[12,8,128]{2,1,0:T(8,128)S(1)} %get-tuple-element.24), channel_id=1, source_target_pairs={{0,1},{1,2},{2,3},{3,4},{4,5},{5,6},{6,7},{7,8},{8,9},{9,10},{10,1... | collective-permute-start | bytes 147464 | tf_op jit(solution)/shard_map/ppermute | solution.py:367
  86.2 1.9 %collective-permute-start.7 = (f32[12,8,128]{2,1,0:T(8,128)S(1)}, f32[12,8,128]{2,1,0:T(8,128)S(1)}, u32[]{:S(2)}, u32[]{:S(2)}) collective-permute-start(f32[12,8,128]{2,1,0:T(8,128)S(1)} %get-tuple-element.25), channel_id=1, source_target_pairs={{1,0},{2,1},{3,2},{4,3},{5,4},{6,5},{7,6},{8,7},{9,8},{10,9},{11,1... | collective-permute-start | bytes 147464 | tf_op jit(solution)/shard_map/ppermute | solution.py:368
  88.2 0.0 collective-permute-done.6.tbelow_ref
  88.2 8.0 %collective-permute-done.7.tabove_ref = f32[12,8,128]{2,1,0:T(8,128)S(1)} collective-permute-done((f32[12,8,128]{2,1,0:T(8,128)S(1)}, f32[12,8,128]{2,1,0:T(8,128)S(1)}, u32[]{:S(2)}, u32[]{:S(2)}) %collective-permute-start.7) | collective-permute-done | bytes 49184 | tf_op jit(solution)/shard_map/ppermute | solution.py:368
  96.1 0.0 collective-permute-done.4.below_ref
  96.1 0.0 collective-permute-done.5.above_ref
  96.1 2.3 %last_sweep.1 = f32[1152,128]{1,0:T(8,128)} custom-call(f32[6,24,8,128]{3,2,1,0:T(8,128)S(1)} %get-tuple-element.21.x_ref, f32[1152,128]{1,0:T(8,128)S(1)} %bitcast.15, f32[3456,128]{1,0:T(8,128)S(1)} %bitcast.12, f32[8,128]{1,0:T(8,128)S(1)} %get-tuple-element.16.rate_ref, f32[6,12,8,128]{3,2,1,0:T(8,128)S(1)} %collective-permute-done.4.below_ref, ...), custom_call_target="tpu_custom_call" | custom-call | flops 10000000 | bytes 3000000 | tf_op jit(solution)/shard_map/last_sweep/pallas_call | solution.py:375
  (2 shorter events, 0.0 us)
Async XLA Ops:
  0.6 38.2 %copy-start = (f32[4,18,6,8,128]{4,3,2,1,0:T(8,128)S(1)}, f32[4,18,6,8,128]{4,3,2,1,0:T(8,128)}, u32[]{:S(2)}) copy-start(f32[4,18,6,8,128]{4,3,2,1,0:T(8,128)} %param.8) | copy-start | bytes 5308420
  1.4 1.1 %copy-start.1 = (f32[8,24,6,1,128]{4,3,2,1,0:T(1,128)S(1)}, f32[8,24,6,1,128]{4,3,2,1,0:T(1,128)}, u32[]{:S(2)}) copy-start(f32[8,24,6,1,128]{4,3,2,1,0:T(1,128)} %param.5) | copy-start | bytes 1769476
  2.5 1.3 %copy-start.3 = (bf16[32,24,6,1,128]{4,1,3,2,0:T(8,128)(2,1)S(1)}, bf16[32,24,6,1,128]{4,1,3,2,0:T(8,128)(2,1)}, u32[]{:S(2)}) copy-start(bf16[32,24,6,1,128]{4,1,3,2,0:T(8,128)(2,1)} %param.6) | copy-start | bytes 3538948
  3.8 35.0 %copy-start.5 = (f32[32]{0:T(128)S(1)}, f32[32]{0:T(128)}, u32[]{:S(2)}) copy-start(f32[32]{0:T(128)} %param.7) | copy-start | bytes 388
  5.0 60.0 %copy-start.2 = (f32[8,24,6,1,128]{4,3,2,1,0:T(1,128)S(1)}, f32[8,24,6,1,128]{4,3,2,1,0:T(1,128)}, u32[]{:S(2)}) copy-start(f32[8,24,6,1,128]{4,3,2,1,0:T(1,128)} %param.5) | copy-start | bytes 1769476
  38.8 1.3 %copy-start.4 = (bf16[32,24,6,1,128]{4,1,3,2,0:T(8,128)(2,1)S(1)}, bf16[32,24,6,1,128]{4,1,3,2,0:T(8,128)(2,1)}, u32[]{:S(2)}) copy-start(bf16[32,24,6,1,128]{4,1,3,2,0:T(8,128)(2,1)} %param.6) | copy-start | bytes 3538948
  42.1 22.9 %collective-permute-start = (f32[6,12,8,128]{3,2,1,0:T(8,128)S(1)}, f32[6,12,8,128]{3,2,1,0:T(8,128)S(1)}, u32[]{:S(2)}, u32[]{:S(2)}) collective-permute-start(f32[6,12,8,128]{3,2,1,0:T(8,128)S(1)} %get-tuple-element.17), channel_id=1, source_target_pairs={{0,64},{64,128},{128,192},{192,256},{256,320},{320,384},{384,448},... | collective-permute-start | bytes 884744 | tf_op jit(solution)/shard_map/ppermute | solution.py:365
  44.4 20.6 %collective-permute-start.1 = (f32[6,12,8,128]{3,2,1,0:T(8,128)S(1)}, f32[6,12,8,128]{3,2,1,0:T(8,128)S(1)}, u32[]{:S(2)}, u32[]{:S(2)}) collective-permute-start(f32[6,12,8,128]{3,2,1,0:T(8,128)S(1)} %get-tuple-element.18), channel_id=1, source_target_pairs={{64,0},{128,64},{192,128},{256,192},{320,256},{384,320},{448,384},... | collective-permute-start | bytes 884744 | tf_op jit(solution)/shard_map/ppermute | solution.py:366
  49.4 11.3 %collective-permute-start.2 = (f32[12,8,128]{2,1,0:T(8,128)S(1)}, f32[12,8,128]{2,1,0:T(8,128)S(1)}, u32[]{:S(2)}, u32[]{:S(2)}) collective-permute-start(f32[12,8,128]{2,1,0:T(8,128)S(1)} %get-tuple-element.19), channel_id=1, source_target_pairs={{0,1},{1,2},{2,3},{3,4},{4,5},{5,6},{6,7},{7,8},{8,9},{9,10},{10,1... | collective-permute-start | bytes 147464 | tf_op jit(solution)/shard_map/ppermute | solution.py:367
  52.5 12.5 %collective-permute-start.3 = (f32[12,8,128]{2,1,0:T(8,128)S(1)}, f32[12,8,128]{2,1,0:T(8,128)S(1)}, u32[]{:S(2)}, u32[]{:S(2)}) collective-permute-start(f32[12,8,128]{2,1,0:T(8,128)S(1)} %get-tuple-element.20), channel_id=1, source_target_pairs={{1,0},{2,1},{3,2},{4,3},{5,4},{6,5},{7,6},{8,7},{9,8},{10,9},{11,1... | collective-permute-start | bytes 147464 | tf_op jit(solution)/shard_map/ppermute | solution.py:368
  66.7 29.4 %collective-permute-start.4 = (f32[6,12,8,128]{3,2,1,0:T(8,128)S(1)}, f32[6,12,8,128]{3,2,1,0:T(8,128)S(1)}, u32[]{:S(2)}, u32[]{:S(2)}) collective-permute-start(f32[6,12,8,128]{3,2,1,0:T(8,128)S(1)} %get-tuple-element.22), channel_id=1, source_target_pairs={{0,64},{64,128},{128,192},{192,256},{256,320},{320,384},{384,448},... | collective-permute-start | bytes 884744 | tf_op jit(solution)/shard_map/ppermute | solution.py:365
  68.6 27.5 %collective-permute-start.5 = (f32[6,12,8,128]{3,2,1,0:T(8,128)S(1)}, f32[6,12,8,128]{3,2,1,0:T(8,128)S(1)}, u32[]{:S(2)}, u32[]{:S(2)}) collective-permute-start(f32[6,12,8,128]{3,2,1,0:T(8,128)S(1)} %get-tuple-element.23), channel_id=1, source_target_pairs={{64,0},{128,64},{192,128},{256,192},{320,256},{384,320},{448,384},... | collective-permute-start | bytes 884744 | tf_op jit(solution)/shard_map/ppermute | solution.py:366
  74.1 14.1 %collective-permute-start.6 = (f32[12,8,128]{2,1,0:T(8,128)S(1)}, f32[12,8,128]{2,1,0:T(8,128)S(1)}, u32[]{:S(2)}, u32[]{:S(2)}) collective-permute-start(f32[12,8,128]{2,1,0:T(8,128)S(1)} %get-tuple-element.24), channel_id=1, source_target_pairs={{0,1},{1,2},{2,3},{3,4},{4,5},{5,6},{6,7},{7,8},{8,9},{9,10},{10,1... | collective-permute-start | bytes 147464 | tf_op jit(solution)/shard_map/ppermute | solution.py:367
  86.2 9.9 %collective-permute-start.7 = (f32[12,8,128]{2,1,0:T(8,128)S(1)}, f32[12,8,128]{2,1,0:T(8,128)S(1)}, u32[]{:S(2)}, u32[]{:S(2)}) collective-permute-start(f32[12,8,128]{2,1,0:T(8,128)S(1)} %get-tuple-element.25), channel_id=1, source_target_pairs={{1,0},{2,1},{3,2},{4,3},{5,4},{6,5},{7,6},{8,7},{9,8},{10,9},{11,1... | collective-permute-start | bytes 147464 | tf_op jit(solution)/shard_map/ppermute | solution.py:368

commit v2 on v1

v2 whole, which is shorter than its diff:
```python
import functools
import math

import jax
import jax.numpy as jnp
from jax import lax
from jax.experimental import pallas as pl
from jax.experimental.pallas import tpu as pltpu
from jax.sharding import PartitionSpec as P

LX = 16
ITERS = 2
HOPPING = 0.12

BLOCKS = [
    {(0, 1): 1, (1, 0): 1},
    {(0, 1): 2, (1, 0): 0},
    {(0, 0): 1, (1, 1): 3},
    {(0, 0): 0, (1, 1): 0},
]


def times_power(power, re, im):
    return [
        ((1, re), (1, im)),
        ((-1, im), (1, re)),
        ((-1, re), (-1, im)),
        ((1, im), (-1, re)),
    ][power % 4]


def add_signed(base, sign, value):
    return base + value if sign > 0 else base - value


def project(sign, direction, load):
    half = []
    for row in range(2):
        col, power = next((c, p) for (r, c), p in BLOCKS[direction].items() if r == row)
        colours = []
        for colour in range(3):
            lower_re, lower_im = load(0, 2 + col, colour), load(1, 2 + col, colour)
            (sr, vr), (si, vi) = times_power(power, lower_re, lower_im)
            colours.append(
                (
                    add_signed(load(0, row, colour), sr * sign, vr),
                    add_signed(load(1, row, colour), si * sign, vi),
                )
            )
        half.append(colours)
    return half


def rebuild_into(acc, sign, direction, half):
    def put(key, sgn, value):
        if key in acc:
            acc[key] = add_signed(acc[key], sgn, value)
        else:
            acc[key] = value if sgn > 0 else -value

    for row in range(2):
        for colour in range(3):
            re, im = half[row][colour]
            put((0, row, colour), 1, re)
            put((1, row, colour), 1, im)
    for (row, col), power in BLOCKS[direction].items():
        for colour in range(3):
            re, im = half[row][colour]
            (sr, vr), (si, vi) = times_power(-power, re, im)
            put((0, 2 + col, colour), sr * sign, vr)
            put((1, 2 + col, colour), si * sign, vi)


def colour_mul(link, half, adjoint):
    out = []
    for spin in range(2):
        rows = []
        for row in range(3):
            re = im = None
            for col in range(3):
                lr, li = link[(col, row)] if adjoint else link[(row, col)]
                hr, hi = half[spin][col]
                if adjoint:
                    tr, ti = lr * hr + li * hi, lr * hi - li * hr
                else:
                    tr, ti = lr * hr - li * hi, lr * hi + li * hr
                re = tr if re is None else re + tr
                im = ti if im is None else im + ti
            rows.append((re, im))
        out.append(rows)
    return out


def map_half(fn, half):
    return [[(fn(re), fn(im)) for re, im in rows] for rows in half]


def load_half(load):
    return [[(load(3 * s + c), load(6 + 3 * s + c)) for c in range(3)] for s in range(2)]


def store_half(store, half):
    for s in range(2):
        for c in range(3):
            store(3 * s + c, half[s][c][0])
            store(6 + 3 * s + c, half[s][c][1])


def load_link(links_ref, slices, direction, t):
    def one(comp):
        row = (direction * 18 + comp) * slices + t
        return jnp.broadcast_to(links_ref[pl.ds(row, 1), :], (8, 128))

    return {(a, c): (one(3 * a + c), one(9 + 3 * a + c)) for a in range(3) for c in range(3)}


def moved(direction, step):
    def fn(v):
        if direction == 1:
            return pltpu.roll(v, (-step * LX) % 128, 1)
        column = lax.rem(lax.broadcasted_iota(jnp.int32, v.shape, 1), LX)
        border = LX - 1 if step > 0 else 0
        inside = pltpu.roll(v, (-step) % 128, 1)
        wrapped = pltpu.roll(v, (step * (LX - 1)) % 128, 1)
        return jnp.where(column == border, wrapped, inside)

    return fn


def correlation_kernel(
    eig_hbm, src_hbm, links_hbm, damp_ref, out_ref, eig_ref, links_ref, src_ref, sems, *, nev, slices
):
    comps = 24
    sources = 8
    rows = sources * comps * slices // 2
    src_copies = [
        pltpu.make_async_copy(
            src_hbm.at[pl.ds(i * rows, rows)], src_ref.at[pl.ds(i * rows, rows)], sems.at[slices + i]
        )
        for i in range(2)
    ]
    eig_copies = [
        pltpu.make_async_copy(eig_hbm.at[:, t], eig_ref.at[:, t], sems.at[t]) for t in range(slices)
    ]
    links_copy = pltpu.make_async_copy(
        links_hbm.at[:, lax.axis_index("src")], links_ref, sems.at[slices + 2]
    )
    for copy in src_copies + eig_copies + [links_copy]:
        copy.start()
    for copy in src_copies:
        copy.wait()
    full = jnp.zeros((sources * comps, nev * comps), jnp.float32)
    for t in range(0, slices, 2):
        lhs = [
            src_ref[pl.ds(u, sources * comps, stride=slices), :].astype(jnp.bfloat16)
            for u in (t, t + 1)
        ]
        eig_copies[t].wait()
        eig_copies[t + 1].wait()
        rhs = [eig_ref[:, u].reshape(nev * comps, 128) for u in (t, t + 1)]
        full = full + lax.dot_general(
            jnp.concatenate(lhs, axis=1), jnp.concatenate(rhs, axis=1),
            (((1,), (1,)), ((), ())), preferred_element_type=jnp.float32,
        )
    row = lax.rem(lax.broadcasted_iota(jnp.int32, (sources * comps, 1), 0), comps)
    col = lax.rem(lax.broadcasted_iota(jnp.int32, (1, nev * comps), 1), comps)
    gap = row - col
    straight = jnp.where(gap == 0, full, 0.0)
    crossed = jnp.where(gap == 12, full, 0.0) - jnp.where(gap == -12, full, 0.0)
    straight = straight.reshape(sources, comps, nev * comps).sum(1)
    crossed = crossed.reshape(sources, comps, nev * comps).sum(1)
    first = lax.broadcasted_iota(jnp.int32, (nev * comps, 128), 0)
    lane = lax.broadcasted_iota(jnp.int32, (nev * comps, 128), 1)

    def gather(which):
        start = (lane - which * nev) * comps
        return jnp.where((first >= start) & (first < start + comps), 1.0, 0.0)

    dot = functools.partial(
        jnp.dot, precision=lax.Precision.HIGHEST, preferred_element_type=jnp.float32
    )
    total = dot(straight, gather(0)) + dot(crossed, gather(1))
    links_copy.wait()
    holder = (lax.axis_index("lat") == 0) & (lax.axis_index("sub") == 0)
    value = jnp.where(holder, damp_ref[0], 0.0)
    at_row = lax.broadcasted_iota(jnp.int32, (8, 128), 0) == lax.axis_index("src")
    at_lane = lax.broadcasted_iota(jnp.int32, (8, 128), 1) == 2 * nev
    total = total + jnp.where(at_row & at_lane, value, 0.0)
    out_ref[...] = jnp.broadcast_to(total[None], out_ref.shape)


def choose(flag, half_true, half_false):
    return [
        [
            tuple(jnp.where(flag, a, b) for a, b in zip(half_true[s][c], half_false[s][c]))
            for c in range(3)
        ]
        for s in range(2)
    ]


def z_even():
    return lax.rem(lax.axis_index("src"), 2) == 0


def t_place():
    place = lax.axis_index(("lat", "sub"))
    return place, lax.rem(place, 2) == 0


def emit_halos(load, links_ref, t, near_ref, far_ref, slices):
    even = z_even()
    up = project(1, 2, load)
    up = colour_mul(load_link(links_ref, slices, 2, t), up, True)
    down = project(-1, 2, load)
    store_half(lambda i, v: near_ref.__setitem__((t, i), v), choose(even, up, down))
    store_half(lambda i, v: far_ref.__setitem__((t, i), v), choose(even, down, up))


def emit_time_halos(x_ref, links_ref, near_ref, far_ref, slices):
    place, even = t_place()
    extent = lax.axis_size(("lat", "sub"))
    up_sign = jnp.where(place == extent - 1, -1.0, 1.0)
    down_sign = jnp.where(place == 0, -1.0, 1.0)
    last = slices - 1
    up = project(1, 3, lambda p, s, c: x_ref[last, 12 * p + 3 * s + c])
    up = colour_mul(load_link(links_ref, slices, 3, last), up, True)
    up = map_half(lambda v: v * up_sign, up)
    down = project(-1, 3, lambda p, s, c: x_ref[0, 12 * p + 3 * s + c])
    down = map_half(lambda v: v * down_sign, down)
    store_half(lambda i, v: near_ref.__setitem__(i, v), choose(even, up, down))
    store_half(lambda i, v: far_ref.__setitem__(i, v), choose(even, down, up))


def guess_kernel(
    part_ref, ev_ref, eig_ref, links_ref, x_ref, rate_ref, znear_ref, zfar_ref, tnear_ref, tfar_ref,
    *, nev, slices, norm,
):
    comps = 24
    total = part_ref[0]
    for i in range(1, part_ref.shape[0]):
        total = total + part_ref[i]
    ev = ev_ref[...]
    w_re = ((total[:, :nev] / norm) / ev).astype(jnp.bfloat16)
    w_im = ((total[:, nev : 2 * nev] / norm) / ev).astype(jnp.bfloat16)
    rate_ref[...] = jnp.broadcast_to(total[:, 2 * nev : 2 * nev + 1], (8, 128))
    row = lax.broadcasted_iota(jnp.int32, (nev, nev * comps), 0) * comps
    col = lax.broadcasted_iota(jnp.int32, (nev, nev * comps), 1)
    spread = jnp.where((col >= row) & (col < row + comps), 1.0, 0.0).astype(jnp.bfloat16)
    w_re = jnp.dot(w_re, spread, preferred_element_type=jnp.float32)
    w_im = jnp.dot(w_im, spread, preferred_element_type=jnp.float32)
    comp = lax.rem(lax.broadcasted_iota(jnp.int32, (8, nev * comps), 1), comps)
    blocks = []
    for c in range(comps):
        other, turned = (c + 12, -w_im) if c < 12 else (c - 12, w_im)
        blocks.append(jnp.where(comp == c, w_re, jnp.where(comp == other, turned, 0.0)))
    mix = jnp.concatenate(blocks, axis=0).astype(jnp.bfloat16)
    for t in range(slices):
        res = jnp.dot(
            mix, eig_ref[:, t].reshape(nev * comps, 128), preferred_element_type=jnp.float32
        )
        x_ref[t] = res.reshape(comps, 8, 128)

    def step(t, carry):
        emit_halos(
            lambda p, s, c: x_ref[t, 12 * p + 3 * s + c],
            links_ref, t, znear_ref, zfar_ref, slices,
        )
        return carry

    lax.fori_loop(0, slices, step, 0)
    emit_time_halos(x_ref, links_ref, tnear_ref, tfar_ref, slices)


def local_kernel(x_ref, src_ref, links_ref, rate_ref, *refs, slices, keep):
    y_ref, behind_ref = refs[0], refs[-1]
    behind_ref[...] = jnp.zeros_like(behind_ref)

    def step(t, carry):
        load = lambda p, s, c: x_ref[t, 12 * p + 3 * s + c]
        acc = {}
        for direction in range(2):
            link = load_link(links_ref, slices, direction, t)
            ahead = map_half(moved(direction, 1), project(-1, direction, load))
            rebuild_into(acc, -1, direction, colour_mul(link, ahead, False))
            behind = colour_mul(link, project(1, direction, load), True)
            rebuild_into(acc, 1, direction, map_half(moved(direction, -1), behind))
        link = load_link(links_ref, slices, 3, t)
        inside = jnp.where(t == slices - 1, 0.0, 1.0)
        following = jnp.minimum(t + 1, slices - 1)
        ahead = project(-1, 3, lambda p, s, c: x_ref[following, 12 * p + 3 * s + c])
        ahead = map_half(lambda v: v * inside, ahead)
        rebuild_into(acc, -1, 3, colour_mul(link, ahead, False))
        rebuild_into(acc, 1, 3, load_half(lambda i: behind_ref[i]))
        up = colour_mul(link, project(1, 3, load), True)
        store_half(lambda i, v: behind_ref.__setitem__(i, v), up)
        rate = rate_ref[...]
        for (p, s, c), hop in acc.items():
            comp = 12 * p + 3 * s + c
            where = pl.ds(comp * slices + t, 8, stride=24 * slices)
            value = load(p, s, c)
            y_ref[t, comp] = value + rate * (src_ref[where, :] - (value - HOPPING * hop))
            if keep:
                refs[1][where, :] = value
        return carry

    lax.fori_loop(0, slices, step, 0)


def halo_kernel(
    y_ref, links_ref, rate_ref, znear_ref, zfar_ref, tnear_ref, tfar_ref, *refs, slices, final
):
    above_near = z_even()
    _, t_even = t_place()
    edge_ref = refs[-1]
    last = slices - 1
    near, far = (load_half(lambda i, ref=ref: ref[i]) for ref in (tnear_ref, tfar_ref))
    link = load_link(links_ref, slices, 3, last)
    above = colour_mul(link, choose(t_even, near, far), False)
    store_half(lambda i, v: edge_ref.__setitem__((0, i), v), above)
    store_half(lambda i, v: edge_ref.__setitem__((1, i), v), choose(t_even, far, near))

    def step(t, carry):
        acc = {}
        near, far = (load_half(lambda i, ref=ref: ref[t, i]) for ref in (znear_ref, zfar_ref))
        link = load_link(links_ref, slices, 2, t)
        rebuild_into(acc, -1, 2, colour_mul(link, choose(above_near, near, far), False))
        rebuild_into(acc, 1, 2, choose(above_near, far, near))
        top, bottom = (jnp.where(t == edge, 1.0, 0.0) for edge in (last, 0))
        rebuild_into(acc, -1, 3, map_half(lambda v: v * top, load_half(lambda i: edge_ref[0, i])))
        rebuild_into(acc, 1, 3, map_half(lambda v: v * bottom, load_half(lambda i: edge_ref[1, i])))
        rate = rate_ref[...] * HOPPING
        new = {}
        for (p, s, c), hop in acc.items():
            comp = 12 * p + 3 * s + c
            value = y_ref[t, comp] + rate * hop
            new[(p, s, c)] = value
            if final:
                refs[0][pl.ds(comp * slices + t, 8, stride=24 * slices), :] = value
            else:
                refs[0][t, comp] = value
        if not final:
            emit_halos(
                lambda p, s, c: new[(p, s, c)], links_ref, t, refs[1], refs[2], slices
            )
        return carry

    lax.fori_loop(0, slices, step, 0)
    if not final:
        emit_time_halos(refs[0], links_ref, refs[3], refs[4], slices)


def call(kernel, outs, ins, flops, hbm=(), smem=(), scratch=()):
    space = lambda i: pltpu.HBM if i in hbm else pltpu.SMEM if i in smem else pltpu.VMEM
    return pl.pallas_call(
        kernel,
        out_shape=outs,
        in_specs=[pl.BlockSpec(memory_space=space(i)) for i in range(ins)],
        out_specs=jax.tree.map(lambda _: pl.BlockSpec(memory_space=pltpu.VMEM), outs),
        scratch_shapes=list(scratch),
        compiler_params=pltpu.CompilerParams(vmem_limit_bytes=24 << 20),
        cost_estimate=pl.CostEstimate(
            flops=flops, bytes_accessed=3_000_000, transcendentals=0
        ),
    )


def exchange(send):
    znear, zfar, tnear, tfar = send
    nz, nt = lax.axis_size("src"), lax.axis_size(("lat", "sub"))
    near = lambda n: [(i, i ^ 1) for i in range(n)]
    far = lambda n: [(i, (i + 1 if i % 2 else i - 1) % n) for i in range(n)]

    return (
        lax.ppermute(znear, "src", near(nz)),
        lax.ppermute(zfar, "src", far(nz)),
        lax.ppermute(tnear, ("lat", "sub"), near(nt)),
        lax.ppermute(tfar, ("lat", "sub"), far(nt)),
    )


def shards(sources, eigvecs, eigvals, links, damping):
    count, comps, slices = sources.shape[:3]
    nev = eigvecs.shape[0]
    zdim = links.shape[3]
    devices = lax.axis_size(("src", "lat", "sub"))
    norm = math.sqrt(comps * slices * 128 * devices)
    f32 = jnp.float32

    src = sources.reshape(count * comps * slices, 128)
    eig = eigvecs.transpose(0, 2, 3, 1, 4).reshape(nev, slices, comps, 128)

    shape = lambda *dims: jax.ShapeDtypeStruct(dims, f32)
    lat, rest = lax.axis_size("lat"), lax.axis_size(("sub", "src"))
    links = links.reshape(4 * 18 * slices, zdim, 128)
    partial, eig, flat_links = call(
        functools.partial(correlation_kernel, nev=nev, slices=slices),
        (
            shape(lat, 8, 128),
            jax.ShapeDtypeStruct(eig.shape, eig.dtype),
            shape(4 * 18 * slices, 128),
        ),
        4, 226_000_000, hbm=(0, 1, 2), smem=(3,),
        scratch=[
            pltpu.VMEM(src.shape, f32),
            pltpu.SemaphoreType.DMA((slices + 3,)),
        ],
    )(*(pltpu.with_memory_space_constraint(x, pltpu.HBM) for x in (eig, src, links)), damping)
    partial = lax.all_to_all(partial, "lat", 0, 0, tiled=True)
    partial = jnp.broadcast_to(partial.sum(0)[None], (rest, 8, 128))
    partial = lax.all_to_all(partial, ("sub", "src"), 0, 0, tiled=True)

    field = shape(slices, comps, 8, 128)
    halos = (shape(slices, 12, 8, 128),) * 2 + (shape(12, 8, 128),) * 2
    flat = shape(count * comps * slices, 128)
    x, rate, *send = call(
        functools.partial(guess_kernel, nev=nev, slices=slices, norm=norm),
        (field, shape(8, 128)) + halos, 4, 226_000_000,
    )(partial, eigvals.reshape(1, nev), eig, flat_links)

    guess = None
    for sweep in range(ITERS):
        final = sweep == ITERS - 1
        keep = sweep == 0
        got = exchange(send)
        y, *kept = call(
            functools.partial(local_kernel, slices=slices, keep=keep),
            (field,) + ((flat,) if keep else ()), 4, 10_000_000,
            scratch=[pltpu.VMEM((12, 8, 128), f32)],
        )(x, src, flat_links, rate)
        if keep:
            guess = kept[0]
        outs = flat if final else (field,) + halos
        res = call(
            functools.partial(halo_kernel, slices=slices, final=final),
            outs, 7, 5_000_000,
            scratch=[pltpu.VMEM((2, 12, 8, 128), f32)],
        )(y, flat_links, rate, *got)
        if final:
            x = res
        else:
            x, *send = res
    return (guess.reshape(sources.shape), x.reshape(sources.shape))


def solution(mesh):
    return jax.shard_map(
        shards,
        mesh=mesh,
        in_specs=(
            P(None, None, ("lat", "sub"), "src", None),
            P(None, None, ("lat", "sub"), "src", None),
            P(),
            P(None, None, ("lat", "sub"), None, None),
            P("src"),
        ),
        out_specs=(
            P(None, None, ("lat", "sub"), "src", None),
            P(None, None, ("lat", "sub"), "src", None),
        ),
        check_vma=False,
    )
```

time: 99 us -> 91.3 us (0.922)
  the two profiles are of different devices: /device:TPU:62 before, /device:TPU:1 now
where the time goes in v2:
time: 91.3 us; the launch traced here: 90.8 us
  blocking collectives  39.7 us (43%)
  starting transfers between devices  28.6 us (31%)
  waiting for transfers between devices  12 us (13%)
  Pallas kernels  8.99 us (10%)
  between operations  1.39 us (2%)
    all_to_all x1, blocking collectives, shards(): partial = lax.all_to_all(partial, ('sub', 'src'), 0, 0, tiled=True)  20 us
    all_to_all x1, blocking collectives, shards(): partial = lax.all_to_all(partial, 'lat', 0, 0, tiled=True)  19.8 us
    ppermute x2, waiting for transfers between devices, exchange(): lax.ppermute(tfar, ('lat', 'sub'), far(nt))  12 us
    ppermute x2, starting transfers between devices, exchange(): lax.ppermute(tfar, ('lat', 'sub'), far(nt))  11.1 us
    ppermute x2, starting transfers between devices, exchange(): lax.ppermute(znear, 'src', near(nz))  6.6 us
    ppermute x2, starting transfers between devices, exchange(): lax.ppermute(tnear, ('lat', 'sub'), near(nt))  6.55 us
    ppermute x2, starting transfers between devices, exchange(): lax.ppermute(zfar, 'src', far(nz))  4.31 us
    pallas_call x2, Pallas kernels, shards(): call(functools.partial(local_kernel, slices=slices, keep=keep), (field,)...  3.3 us
  transfers between devices with their start and end apart: 8, of which 2 were waited for; matrix products, arithmetic and copies ran while one was open for 0% of the time, Pallas kernels for 4%

profile of v2, /device:TPU:1, one launch (start us, length us, event | category | flops | bytes accessed | tf_op | source)
XLA Modules:
  0.0 90.8 jit_solution(3252773641477270499)
XLA Ops:
  1.3 0.0 copy-start.1
  1.3 2.8 %shard_map.68 = (f32[32,8,128]{2,1,0:T(8,128)S(1)}, bf16[32,6,24,128]{3,2,1,0:T(8,128)(2,1)S(1)}, f32[432,128]{1,0:T(8,128)S(1)}) custom-call(bf16[32,6,24,128]{3,2,1,0:T(8,128)(2,1)} %bitcast.15, f32[1152,128]{1,0:T(8,128)} %bitcast.10, f32[432,8,128]{2,1,0:T(8,128)} %bitcast.14, f32[1]{0:T(128)S(6)} %copy.13.damp_ref), custom_call_target="tpu_custom_call" | custom-call | flops 226000000 | bytes 3000000 | tf_op jit(solution)/shard_map/pallas_call | solution.py:396
  4.1 0.0 copy-start
  4.1 19.8 %all_to_all.10 = f32[32,8,128]{2,1,0:T(8,128)S(1)} all-to-all(f32[32,8,128]{2,1,0:T(8,128)S(1)} %get-tuple-element.18), channel_id=1, replica_groups=mesh['src'=8,'lat'=32,'sub'=2] {'lat'}, dimensions={0} | all-to-all | bytes 262144 | tf_op jit(solution)/shard_map/all_to_all | solution.py:409
  24.0 20.0 %all_to_all.11.part_ref = f32[16,8,128]{2,1,0:T(8,128)S(1)} all-to-all(f32[16,8,128]{2,1,0:T(8,128)S(1)} %broadcast_in_dim.2), channel_id=1, replica_groups=mesh['src'=8,'lat'=32,'sub'=2] {'sub','src'}, dimensions={0} | all-to-all | bytes 131072 | tf_op jit(solution)/shard_map/all_to_all | solution.py:411
  43.9 0.0 copy-done.1
  43.9 1.1 %shard_map.69 = (f32[6,24,8,128]{3,2,1,0:T(8,128)S(1)}, f32[8,128]{1,0:T(8,128)S(1)}, f32[6,12,8,128]{3,2,1,0:T(8,128)S(1)}, f32[6,12,8,128]{3,2,1,0:T(8,128)S(1...) custom-call(f32[16,8,128]{2,1,0:T(8,128)S(1)} %all_to_all.11.part_ref, f32[1,32]{1,0:T(1,128)S(1)} %bitcast.13, ...), custom_call_target="tpu_custom_call" | custom-call | flops 226000000 | bytes 3000000 | tf_op jit(solution)/shard_map/pallas_call | solution.py:416
  45.0 2.0 %collective-permute-start = (f32[6,12,8,128]{3,2,1,0:T(8,128)S(1)}, f32[6,12,8,128]{3,2,1,0:T(8,128)S(1)}, u32[]{:S(2)}, u32[]{:S(2)}) collective-permute-start(f32[6,12,8,128]{3,2,1,0:T(8,128)S(1)} %get-tuple-element.25), channel_id=1, source_target_pairs={{0,64},{64,0},{128,192},{192,128},{256,320},{320,256},{384,448},{4... | collective-permute-start | bytes 884744 | tf_op jit(solution)/shard_map/ppermute | solution.py:375
  47.1 2.4 %collective-permute-start.1 = (f32[6,12,8,128]{3,2,1,0:T(8,128)S(1)}, f32[6,12,8,128]{3,2,1,0:T(8,128)S(1)}, u32[]{:S(2)}, u32[]{:S(2)}) collective-permute-start(f32[6,12,8,128]{3,2,1,0:T(8,128)S(1)} %get-tuple-element.26), channel_id=1, source_target_pairs={{0,448},{64,128},{128,64},{192,256},{256,192},{320,384},{384,320},... | collective-permute-start | bytes 884744 | tf_op jit(solution)/shard_map/ppermute | solution.py:376
  49.5 3.4 %collective-permute-start.2 = (f32[12,8,128]{2,1,0:T(8,128)S(1)}, f32[12,8,128]{2,1,0:T(8,128)S(1)}, u32[]{:S(2)}, u32[]{:S(2)}) collective-permute-start(f32[12,8,128]{2,1,0:T(8,128)S(1)} %get-tuple-element.27), channel_id=1, source_target_pairs={{0,1},{1,0},{2,3},{3,2},{4,5},{5,4},{6,7},{7,6},{8,9},{9,8},{10,11... | collective-permute-start | bytes 147464 | tf_op jit(solution)/shard_map/ppermute | solution.py:377
  52.9 6.2 %collective-permute-start.3 = (f32[12,8,128]{2,1,0:T(8,128)S(1)}, f32[12,8,128]{2,1,0:T(8,128)S(1)}, u32[]{:S(2)}, u32[]{:S(2)}) collective-permute-start(f32[12,8,128]{2,1,0:T(8,128)S(1)} %get-tuple-element.28), channel_id=1, source_target_pairs={{0,63},{1,2},{2,1},{3,4},{4,3},{5,6},{6,5},{7,8},{8,7},{9,10},{10,... | collective-permute-start | bytes 147464 | tf_op jit(solution)/shard_map/ppermute | solution.py:378
  59.1 0.0 copy-done
  59.1 2.1 %shard_map.70 = (f32[6,24,8,128]{3,2,1,0:T(8,128)S(1)}, f32[1152,128]{1,0:T(8,128)}) custom-call(f32[6,24,8,128]{3,2,1,0:T(8,128)S(1)} %get-tuple-element.21.x_ref, f32[1152,128]{1,0:T(8,128)S(1)} %bitcast.11, f32[432,128]{1,0:T(8,128)S(1)} %get-tuple-element.20.links_ref, f32[8,128]{1,0:T(8,128)S(1)} %get-tuple-element.22.rate_ref), custom_call_target="tpu_custom_call" | custom-call | flops 10000000 | bytes 3000000 | tf_op jit(solution)/shard_map/pallas_call | solution.py:426
  61.2 0.0 collective-permute-done.2.tnear_ref
  61.2 5.1 %collective-permute-done.3.tfar_ref = f32[12,8,128]{2,1,0:T(8,128)S(1)} collective-permute-done((f32[12,8,128]{2,1,0:T(8,128)S(1)}, f32[12,8,128]{2,1,0:T(8,128)S(1)}, u32[]{:S(2)}, u32[]{:S(2)}) %collective-permute-start.3) | collective-permute-done | bytes 49184 | tf_op jit(solution)/shard_map/ppermute | solution.py:378
  66.2 0.0 collective-permute-done.znear_ref
  66.2 0.0 collective-permute-done.1.zfar_ref
  66.3 0.5 shard_map.71
  66.8 4.6 %collective-permute-start.4 = (f32[6,12,8,128]{3,2,1,0:T(8,128)S(1)}, f32[6,12,8,128]{3,2,1,0:T(8,128)S(1)}, u32[]{:S(2)}, u32[]{:S(2)}) collective-permute-start(f32[6,12,8,128]{3,2,1,0:T(8,128)S(1)} %get-tuple-element.30), channel_id=1, source_target_pairs={{0,64},{64,0},{128,192},{192,128},{256,320},{320,256},{384,448},{4... | collective-permute-start | bytes 884744 | tf_op jit(solution)/shard_map/ppermute | solution.py:375
  71.4 1.9 %collective-permute-start.5 = (f32[6,12,8,128]{3,2,1,0:T(8,128)S(1)}, f32[6,12,8,128]{3,2,1,0:T(8,128)S(1)}, u32[]{:S(2)}, u32[]{:S(2)}) collective-permute-start(f32[6,12,8,128]{3,2,1,0:T(8,128)S(1)} %get-tuple-element.31), channel_id=1, source_target_pairs={{0,448},{64,128},{128,64},{192,256},{256,192},{320,384},{384,320},... | collective-permute-start | bytes 884744 | tf_op jit(solution)/shard_map/ppermute | solution.py:376
  73.3 3.1 %collective-permute-start.6 = (f32[12,8,128]{2,1,0:T(8,128)S(1)}, f32[12,8,128]{2,1,0:T(8,128)S(1)}, u32[]{:S(2)}, u32[]{:S(2)}) collective-permute-start(f32[12,8,128]{2,1,0:T(8,128)S(1)} %get-tuple-element.32), channel_id=1, source_target_pairs={{0,1},{1,0},{2,3},{3,2},{4,5},{5,4},{6,7},{7,6},{8,9},{9,8},{10,11... | collective-permute-start | bytes 147464 | tf_op jit(solution)/shard_map/ppermute | solution.py:377
  76.4 4.9 %collective-permute-start.7 = (f32[12,8,128]{2,1,0:T(8,128)S(1)}, f32[12,8,128]{2,1,0:T(8,128)S(1)}, u32[]{:S(2)}, u32[]{:S(2)}) collective-permute-start(f32[12,8,128]{2,1,0:T(8,128)S(1)} %get-tuple-element.33), channel_id=1, source_target_pairs={{0,63},{1,2},{2,1},{3,4},{4,3},{5,6},{6,5},{7,8},{8,7},{9,10},{10,... | collective-permute-start | bytes 147464 | tf_op jit(solution)/shard_map/ppermute | solution.py:378
  81.4 1.2 %shard_map.72.y_ref = f32[6,24,8,128]{3,2,1,0:T(8,128)S(1)} custom-call(f32[6,24,8,128]{3,2,1,0:T(8,128)S(1)} %get-tuple-element.29.x_ref, f32[1152,128]{1,0:T(8,128)S(1)} %bitcast.12, f32[432,128]{1,0:T(8,128)S(1)} %get-tuple-element.20.links_ref, f32[8,128]{1,0:T(8,128)S(1)} %get-tuple-element.22.rate_ref), custom_call_target="tpu_custom_call" | custom-call | flops 10000000 | bytes 3000000 | tf_op jit(solution)/shard_map/pallas_call | solution.py:426
  82.6 0.0 collective-permute-done.6.tnear_ref
  82.6 6.9 %collective-permute-done.7.tfar_ref = f32[12,8,128]{2,1,0:T(8,128)S(1)} collective-permute-done((f32[12,8,128]{2,1,0:T(8,128)S(1)}, f32[12,8,128]{2,1,0:T(8,128)S(1)}, u32[]{:S(2)}, u32[]{:S(2)}) %collective-permute-start.7) | collective-permute-done | bytes 49184 | tf_op jit(solution)/shard_map/ppermute | solution.py:378
  89.6 0.0 collective-permute-done.4.znear_ref
  89.6 0.0 collective-permute-done.5.zfar_ref
  89.6 1.2 %shard_map.73 = f32[1152,128]{1,0:T(8,128)} custom-call(f32[6,24,8,128]{3,2,1,0:T(8,128)S(1)} %shard_map.72.y_ref, f32[432,128]{1,0:T(8,128)S(1)} %get-tuple-element.20.links_ref, f32[8,128]{1,0:T(8,128)S(1)} %get-tuple-element.22.rate_ref, f32[6,12,8,128]{3,2,1,0:T(8,128)S(1)} %collective-permute-done.4.znear_ref, ...), custom_call_target="tpu_custom_call" | custom-call | flops 5000000 | bytes 3000000 | tf_op jit(solution)/shard_map/pallas_call | solution.py:434
  (2 shorter events, 0.0 us)
Async XLA Ops:
  1.3 42.7 %copy-start.1 = (f32[32]{0:T(128)S(1)}, f32[32]{0:T(128)}, u32[]{:S(2)}) copy-start(f32[32]{0:T(128)} %param.7) | copy-start | bytes 388
  4.1 55.0 %copy-start = (f32[8,24,6,1,128]{4,3,2,1,0:T(1,128)S(1)}, f32[8,24,6,1,128]{4,3,2,1,0:T(1,128)}, u32[]{:S(2)}) copy-start(f32[8,24,6,1,128]{4,3,2,1,0:T(1,128)} %param.5) | copy-start | bytes 1769476
  45.0 21.2 %collective-permute-start = (f32[6,12,8,128]{3,2,1,0:T(8,128)S(1)}, f32[6,12,8,128]{3,2,1,0:T(8,128)S(1)}, u32[]{:S(2)}, u32[]{:S(2)}) collective-permute-start(f32[6,12,8,128]{3,2,1,0:T(8,128)S(1)} %get-tuple-element.25), channel_id=1, source_target_pairs={{0,64},{64,0},{128,192},{192,128},{256,320},{320,256},{384,448},{4... | collective-permute-start | bytes 884744 | tf_op jit(solution)/shard_map/ppermute | solution.py:375
  47.1 19.2 %collective-permute-start.1 = (f32[6,12,8,128]{3,2,1,0:T(8,128)S(1)}, f32[6,12,8,128]{3,2,1,0:T(8,128)S(1)}, u32[]{:S(2)}, u32[]{:S(2)}) collective-permute-start(f32[6,12,8,128]{3,2,1,0:T(8,128)S(1)} %get-tuple-element.26), channel_id=1, source_target_pairs={{0,448},{64,128},{128,64},{192,256},{256,192},{320,384},{384,320},... | collective-permute-start | bytes 884744 | tf_op jit(solution)/shard_map/ppermute | solution.py:376
  49.5 11.7 %collective-permute-start.2 = (f32[12,8,128]{2,1,0:T(8,128)S(1)}, f32[12,8,128]{2,1,0:T(8,128)S(1)}, u32[]{:S(2)}, u32[]{:S(2)}) collective-permute-start(f32[12,8,128]{2,1,0:T(8,128)S(1)} %get-tuple-element.27), channel_id=1, source_target_pairs={{0,1},{1,0},{2,3},{3,2},{4,5},{5,4},{6,7},{7,6},{8,9},{9,8},{10,11... | collective-permute-start | bytes 147464 | tf_op jit(solution)/shard_map/ppermute | solution.py:377
  52.9 13.4 %collective-permute-start.3 = (f32[12,8,128]{2,1,0:T(8,128)S(1)}, f32[12,8,128]{2,1,0:T(8,128)S(1)}, u32[]{:S(2)}, u32[]{:S(2)}) collective-permute-start(f32[12,8,128]{2,1,0:T(8,128)S(1)} %get-tuple-element.28), channel_id=1, source_target_pairs={{0,63},{1,2},{2,1},{3,4},{4,3},{5,6},{6,5},{7,8},{8,7},{9,10},{10,... | collective-permute-start | bytes 147464 | tf_op jit(solution)/shard_map/ppermute | solution.py:378
  66.8 22.8 %collective-permute-start.4 = (f32[6,12,8,128]{3,2,1,0:T(8,128)S(1)}, f32[6,12,8,128]{3,2,1,0:T(8,128)S(1)}, u32[]{:S(2)}, u32[]{:S(2)}) collective-permute-start(f32[6,12,8,128]{3,2,1,0:T(8,128)S(1)} %get-tuple-element.30), channel_id=1, source_target_pairs={{0,64},{64,0},{128,192},{192,128},{256,320},{320,256},{384,448},{4... | collective-permute-start | bytes 884744 | tf_op jit(solution)/shard_map/ppermute | solution.py:375
  71.4 18.2 %collective-permute-start.5 = (f32[6,12,8,128]{3,2,1,0:T(8,128)S(1)}, f32[6,12,8,128]{3,2,1,0:T(8,128)S(1)}, u32[]{:S(2)}, u32[]{:S(2)}) collective-permute-start(f32[6,12,8,128]{3,2,1,0:T(8,128)S(1)} %get-tuple-element.31), channel_id=1, source_target_pairs={{0,448},{64,128},{128,64},{192,256},{256,192},{320,384},{384,320},... | collective-permute-start | bytes 884744 | tf_op jit(solution)/shard_map/ppermute | solution.py:376
  73.3 9.4 %collective-permute-start.6 = (f32[12,8,128]{2,1,0:T(8,128)S(1)}, f32[12,8,128]{2,1,0:T(8,128)S(1)}, u32[]{:S(2)}, u32[]{:S(2)}) collective-permute-start(f32[12,8,128]{2,1,0:T(8,128)S(1)} %get-tuple-element.32), channel_id=1, source_target_pairs={{0,1},{1,0},{2,3},{3,2},{4,5},{5,4},{6,7},{7,6},{8,9},{9,8},{10,11... | collective-permute-start | bytes 147464 | tf_op jit(solution)/shard_map/ppermute | solution.py:377
  76.4 13.1 %collective-permute-start.7 = (f32[12,8,128]{2,1,0:T(8,128)S(1)}, f32[12,8,128]{2,1,0:T(8,128)S(1)}, u32[]{:S(2)}, u32[]{:S(2)}) collective-permute-start(f32[12,8,128]{2,1,0:T(8,128)S(1)} %get-tuple-element.33), channel_id=1, source_target_pairs={{0,63},{1,2},{2,1},{3,4},{4,3},{5,6},{6,5},{7,8},{8,7},{9,10},{10,... | collective-permute-start | bytes 147464 | tf_op jit(solution)/shard_map/ppermute | solution.py:378

commit v3 on v2

--- a/solution.py
+++ b/solution.py
@@ -128,7 +128,7 @@
 
 
 def correlation_kernel(
-    eig_hbm, src_hbm, links_hbm, damp_ref, out_ref, eig_ref, links_ref, src_ref, sems, *, nev, slices
+    eig_hbm, src_hbm, out_ref, eig_ref, slot_ref, src_ref, sems, *, nev, slices
 ):
     comps = 24
     sources = 8
@@ -142,10 +142,7 @@
     eig_copies = [
         pltpu.make_async_copy(eig_hbm.at[:, t], eig_ref.at[:, t], sems.at[t]) for t in range(slices)
     ]
-    links_copy = pltpu.make_async_copy(
-        links_hbm.at[:, lax.axis_index("src")], links_ref, sems.at[slices + 2]
-    )
-    for copy in src_copies + eig_copies + [links_copy]:
+    for copy in src_copies + eig_copies:
         copy.start()
     for copy in src_copies:
         copy.wait()
@@ -180,13 +177,17 @@
         jnp.dot, precision=lax.Precision.HIGHEST, preferred_element_type=jnp.float32
     )
     total = dot(straight, gather(0)) + dot(crossed, gather(1))
-    links_copy.wait()
-    holder = (lax.axis_index("lat") == 0) & (lax.axis_index("sub") == 0)
-    value = jnp.where(holder, damp_ref[0], 0.0)
+    out_ref[...] = jnp.broadcast_to(total[None], out_ref.shape)
     at_row = lax.broadcasted_iota(jnp.int32, (8, 128), 0) == lax.axis_index("src")
     at_lane = lax.broadcasted_iota(jnp.int32, (8, 128), 1) == 2 * nev
-    total = total + jnp.where(at_row & at_lane, value, 0.0)
-    out_ref[...] = jnp.broadcast_to(total[None], out_ref.shape)
+    holder = jnp.where(lax.axis_index("sub") == 0, 1.0, 0.0)
+    slot_ref[...] = jnp.where(at_row & at_lane, holder, 0.0)
+
+
+def slab_kernel(links_hbm, links_ref, sem):
+    copy = pltpu.make_async_copy(links_hbm.at[:, lax.axis_index("src")], links_ref, sem)
+    copy.start()
+    copy.wait()
 
 
 def choose(flag, half_true, half_false):
@@ -393,21 +394,23 @@
     shape = lambda *dims: jax.ShapeDtypeStruct(dims, f32)
     lat, rest = lax.axis_size("lat"), lax.axis_size(("sub", "src"))
     links = links.reshape(4 * 18 * slices, zdim, 128)
-    partial, eig, flat_links = call(
+    hbm = lambda x: pltpu.with_memory_space_constraint(x, pltpu.HBM)
+    partial, eig, slot = call(
         functools.partial(correlation_kernel, nev=nev, slices=slices),
-        (
-            shape(lat, 8, 128),
-            jax.ShapeDtypeStruct(eig.shape, eig.dtype),
-            shape(4 * 18 * slices, 128),
-        ),
-        4, 226_000_000, hbm=(0, 1, 2), smem=(3,),
+        (shape(lat, 8, 128), jax.ShapeDtypeStruct(eig.shape, eig.dtype), shape(8, 128)),
+        2, 226_000_000, hbm=(0, 1),
         scratch=[
             pltpu.VMEM(src.shape, f32),
-            pltpu.SemaphoreType.DMA((slices + 3,)),
+            pltpu.SemaphoreType.DMA((slices + 2,)),
         ],
-    )(*(pltpu.with_memory_space_constraint(x, pltpu.HBM) for x in (eig, src, links)), damping)
+    )(hbm(eig), hbm(src))
     partial = lax.all_to_all(partial, "lat", 0, 0, tiled=True)
-    partial = jnp.broadcast_to(partial.sum(0)[None], (rest, 8, 128))
+    flat_links = call(
+        slab_kernel, shape(4 * 18 * slices, 128), 1, 1000, hbm=(0,),
+        scratch=[pltpu.SemaphoreType.DMA],
+    )(hbm(links))
+    partial = partial.sum(0) + slot * damping[0]
+    partial = jnp.broadcast_to(partial[None], (rest, 8, 128))
     partial = lax.all_to_all(partial, ("sub", "src"), 0, 0, tiled=True)
 
     field = shape(slices, comps, 8, 128)

time: 91.3 us -> 92.2 us (level)
  blocking collectives: 39.7 us -> 0 us
  starting transfers between devices: 28.6 us -> 51.5 us
  waiting for transfers between devices: 12 us -> 27.5 us
  Pallas kernels: 8.99 us -> 10.6 us
    all_to_all x2 -> x0, blocking collectives: 39.7 us -> none  [the longest x1 20 us: shards(): partial = lax.all_to_all(partial, ('sub', 'src'), 0, 0, tiled=True)]
    all_to_all x0 -> x2, starting transfers between devices: none -> 22.9 us  [the longest x1 12.4 us: shards(): partial = lax.all_to_all(partial, ('sub', 'src'), 0, 0, tiled=True)]
    all_to_all x0 -> x2, waiting for transfers between devices: none -> 15.5 us  [the longest x1 8.67 us: shards(): partial = lax.all_to_all(partial, 'lat', 0, 0, tiled=True)]
    pallas_call x0 -> x1, Pallas kernels: none -> 0.94 us  [shards(): call(slab_kernel, shape(4 * 18 * slices, 128), 1, 1000, hbm=(0,), scratch...]
  transfers between devices with their start and end apart: 8 -> 10, of which waited for: 2 -> 4; matrix products, arithmetic and copies ran while one was open for 0% -> 0% of each run, Pallas kernels for 4% -> 5%
where the time goes in v3:
time: 92.2 us; the launch traced here: 91.7 us
  starting transfers between devices  51.5 us (56%)
  waiting for transfers between devices  27.5 us (30%)
  Pallas kernels  10.6 us (11%)
  between operations  1.42 us (2%)
    all_to_all x1, starting transfers between devices, shards(): partial = lax.all_to_all(partial, ('sub', 'src'), 0, 0, tiled=True)  12.4 us
    ppermute x2, waiting for transfers between devices, exchange(): lax.ppermute(tfar, ('lat', 'sub'), far(nt))  12 us
    ppermute x2, starting transfers between devices, exchange(): lax.ppermute(tfar, ('lat', 'sub'), far(nt))  11.2 us
    all_to_all x1, starting transfers between devices, shards(): partial = lax.all_to_all(partial, 'lat', 0, 0, tiled=True)  10.5 us
    all_to_all x1, waiting for transfers between devices, shards(): partial = lax.all_to_all(partial, 'lat', 0, 0, tiled=True)  8.67 us
    all_to_all x1, waiting for transfers between devices, shards(): partial = lax.all_to_all(partial, ('sub', 'src'), 0, 0, tiled=True)  6.81 us
    ppermute x2, starting transfers between devices, exchange(): lax.ppermute(znear, 'src', near(nz))  6.6 us
    ppermute x2, starting transfers between devices, exchange(): lax.ppermute(tnear, ('lat', 'sub'), near(nt))  6.55 us
  transfers between devices with their start and end apart: 10, of which 4 were waited for; matrix products, arithmetic and copies ran while one was open for 0% of the time, Pallas kernels for 5%

profile of v3, /device:TPU:1, one launch (start us, length us, event | category | flops | bytes accessed | tf_op | source)
XLA Modules:
  0.0 91.7 jit_solution(7168557055322009458)
XLA Ops:
  0.6 3.5 %shard_map.68 = (f32[32,8,128]{2,1,0:T(8,128)}, bf16[32,6,24,128]{3,2,1,0:T(8,128)(2,1)S(1)}, f32[8,128]{1,0:T(8,128)S(1)}) custom-call(bf16[32,6,24,128]{3,2,1,0:T(8,128)(2,1)} %bitcast.17, f32[1152,128]{1,0:T(8,128)} %bitcast.12), custom_call_target="tpu_custom_call" | custom-call | flops 226000000 | bytes 3000000 | tf_op jit(solution)/shard_map/pallas_call | solution.py:398
  4.1 10.5 %all-to-all-start = ((f32[32,8,128]{2,1,0:T(8,128)}), f32[32,8,128]{2,1,0:T(8,128)S(1)}, u32[]{:S(2)}, u32[]{:S(2)}) async-start(f32[32,8,128]{2,1,0:T(8,128)} %get-tuple-element.18), calls=%async_computation | async-start | bytes 262144 | tf_op jit(solution)/shard_map/all_to_all | solution.py:407
  14.6 0.0 copy-start.1
  15.3 8.7 %all-to-all-done = f32[32,8,128]{2,1,0:T(8,128)S(1)} async-done(((f32[32,8,128]{2,1,0:T(8,128)}), f32[32,8,128]{2,1,0:T(8,128)S(1)}, u32[]{:S(2)}, u32[]{:S(2)}) %all-to-all-start) | async-done | bytes 131104 | tf_op jit(solution)/shard_map/all_to_all | solution.py:407
  24.0 0.6 broadcast_in_dim.2
  24.7 12.4 %all-to-all-start.1 = ((f32[16,8,128]{2,1,0:T(8,128)}), f32[16,8,128]{2,1,0:T(8,128)S(1)}, u32[]{:S(2)}, u32[]{:S(2)}) async-start(f32[16,8,128]{2,1,0:T(8,128)} %broadcast_in_dim.2), calls=%async_computation.1 | async-start | bytes 131072 | tf_op jit(solution)/shard_map/all_to_all | solution.py:414
  37.1 0.9 %shard_map.69.links_ref = f32[432,128]{1,0:T(8,128)S(1)} custom-call(f32[432,8,128]{2,1,0:T(8,128)} %bitcast.16), custom_call_target="tpu_custom_call" | custom-call | flops 1000 | bytes 3000000 | tf_op jit(solution)/shard_map/pallas_call | solution.py:408
  38.0 0.0 copy-start
  38.0 6.8 %all-to-all-done.1.part_ref = f32[16,8,128]{2,1,0:T(8,128)S(1)} async-done(((f32[16,8,128]{2,1,0:T(8,128)}), f32[16,8,128]{2,1,0:T(8,128)S(1)}, u32[]{:S(2)}, u32[]{:S(2)}) %all-to-all-start.1) | async-done | bytes 65568 | tf_op jit(solution)/shard_map/all_to_all | solution.py:414
  44.8 0.0 copy-done.1
  44.8 1.1 %shard_map.70 = (f32[6,24,8,128]{3,2,1,0:T(8,128)S(1)}, f32[8,128]{1,0:T(8,128)S(1)}, f32[6,12,8,128]{3,2,1,0:T(8,128)S(1)}, f32[6,12,8,128]{3,2,1,0:T(8,128)S(1...) custom-call(f32[16,8,128]{2,1,0:T(8,128)S(1)} %all-to-all-done.1.part_ref, f32[1,32]{1,0:T(1,128)S(1)} %bitcast.15, ...), custom_call_target="tpu_custom_call" | custom-call | flops 226000000 | bytes 3000000 | tf_op jit(solution)/shard_map/pallas_call | solution.py:419
  45.9 2.0 %collective-permute-start = (f32[6,12,8,128]{3,2,1,0:T(8,128)S(1)}, f32[6,12,8,128]{3,2,1,0:T(8,128)S(1)}, u32[]{:S(2)}, u32[]{:S(2)}) collective-permute-start(f32[6,12,8,128]{3,2,1,0:T(8,128)S(1)} %get-tuple-element.25), channel_id=1, source_target_pairs={{0,64},{64,0},{128,192},{192,128},{256,320},{320,256},{384,448},{4... | collective-permute-start | bytes 884744 | tf_op jit(solution)/shard_map/ppermute | solution.py:376
  48.0 2.4 %collective-permute-start.1 = (f32[6,12,8,128]{3,2,1,0:T(8,128)S(1)}, f32[6,12,8,128]{3,2,1,0:T(8,128)S(1)}, u32[]{:S(2)}, u32[]{:S(2)}) collective-permute-start(f32[6,12,8,128]{3,2,1,0:T(8,128)S(1)} %get-tuple-element.26), channel_id=1, source_target_pairs={{0,448},{64,128},{128,64},{192,256},{256,192},{320,384},{384,320},... | collective-permute-start | bytes 884744 | tf_op jit(solution)/shard_map/ppermute | solution.py:377
  50.4 3.4 %collective-permute-start.2 = (f32[12,8,128]{2,1,0:T(8,128)S(1)}, f32[12,8,128]{2,1,0:T(8,128)S(1)}, u32[]{:S(2)}, u32[]{:S(2)}) collective-permute-start(f32[12,8,128]{2,1,0:T(8,128)S(1)} %get-tuple-element.27), channel_id=1, source_target_pairs={{0,1},{1,0},{2,3},{3,2},{4,5},{5,4},{6,7},{7,6},{8,9},{9,8},{10,11... | collective-permute-start | bytes 147464 | tf_op jit(solution)/shard_map/ppermute | solution.py:378
  53.8 6.2 %collective-permute-start.3 = (f32[12,8,128]{2,1,0:T(8,128)S(1)}, f32[12,8,128]{2,1,0:T(8,128)S(1)}, u32[]{:S(2)}, u32[]{:S(2)}) collective-permute-start(f32[12,8,128]{2,1,0:T(8,128)S(1)} %get-tuple-element.28), channel_id=1, source_target_pairs={{0,63},{1,2},{2,1},{3,4},{4,3},{5,6},{6,5},{7,8},{8,7},{9,10},{10,... | collective-permute-start | bytes 147464 | tf_op jit(solution)/shard_map/ppermute | solution.py:379
  60.0 0.0 copy-done
  60.0 2.1 %shard_map.71 = (f32[6,24,8,128]{3,2,1,0:T(8,128)S(1)}, f32[1152,128]{1,0:T(8,128)}) custom-call(f32[6,24,8,128]{3,2,1,0:T(8,128)S(1)} %get-tuple-element.21.x_ref, f32[1152,128]{1,0:T(8,128)S(1)} %bitcast.13, f32[432,128]{1,0:T(8,128)S(1)} %shard_map.69.links_ref, f32[8,128]{1,0:T(8,128)S(1)} %get-tuple-element.22.rate_ref), custom_call_target="tpu_custom_call" | custom-call | flops 10000000 | bytes 3000000 | tf_op jit(solution)/shard_map/pallas_call | solution.py:429
  62.1 0.0 collective-permute-done.2.tnear_ref
  62.1 5.0 %collective-permute-done.3.tfar_ref = f32[12,8,128]{2,1,0:T(8,128)S(1)} collective-permute-done((f32[12,8,128]{2,1,0:T(8,128)S(1)}, f32[12,8,128]{2,1,0:T(8,128)S(1)}, u32[]{:S(2)}, u32[]{:S(2)}) %collective-permute-start.3) | collective-permute-done | bytes 49184 | tf_op jit(solution)/shard_map/ppermute | solution.py:379
  67.1 0.0 collective-permute-done.znear_ref
  67.1 0.0 collective-permute-done.1.zfar_ref
  67.1 0.5 shard_map.72
  67.7 4.6 %collective-permute-start.4 = (f32[6,12,8,128]{3,2,1,0:T(8,128)S(1)}, f32[6,12,8,128]{3,2,1,0:T(8,128)S(1)}, u32[]{:S(2)}, u32[]{:S(2)}) collective-permute-start(f32[6,12,8,128]{3,2,1,0:T(8,128)S(1)} %get-tuple-element.30), channel_id=1, source_target_pairs={{0,64},{64,0},{128,192},{192,128},{256,320},{320,256},{384,448},{4... | collective-permute-start | bytes 884744 | tf_op jit(solution)/shard_map/ppermute | solution.py:376
  72.3 1.9 %collective-permute-start.5 = (f32[6,12,8,128]{3,2,1,0:T(8,128)S(1)}, f32[6,12,8,128]{3,2,1,0:T(8,128)S(1)}, u32[]{:S(2)}, u32[]{:S(2)}) collective-permute-start(f32[6,12,8,128]{3,2,1,0:T(8,128)S(1)} %get-tuple-element.31), channel_id=1, source_target_pairs={{0,448},{64,128},{128,64},{192,256},{256,192},{320,384},{384,320},... | collective-permute-start | bytes 884744 | tf_op jit(solution)/shard_map/ppermute | solution.py:377
  74.2 3.1 %collective-permute-start.6 = (f32[12,8,128]{2,1,0:T(8,128)S(1)}, f32[12,8,128]{2,1,0:T(8,128)S(1)}, u32[]{:S(2)}, u32[]{:S(2)}) collective-permute-start(f32[12,8,128]{2,1,0:T(8,128)S(1)} %get-tuple-element.32), channel_id=1, source_target_pairs={{0,1},{1,0},{2,3},{3,2},{4,5},{5,4},{6,7},{7,6},{8,9},{9,8},{10,11... | collective-permute-start | bytes 147464 | tf_op jit(solution)/shard_map/ppermute | solution.py:378
  77.3 4.9 %collective-permute-start.7 = (f32[12,8,128]{2,1,0:T(8,128)S(1)}, f32[12,8,128]{2,1,0:T(8,128)S(1)}, u32[]{:S(2)}, u32[]{:S(2)}) collective-permute-start(f32[12,8,128]{2,1,0:T(8,128)S(1)} %get-tuple-element.33), channel_id=1, source_target_pairs={{0,63},{1,2},{2,1},{3,4},{4,3},{5,6},{6,5},{7,8},{8,7},{9,10},{10,... | collective-permute-start | bytes 147464 | tf_op jit(solution)/shard_map/ppermute | solution.py:379
  82.3 1.2 %shard_map.73.y_ref = f32[6,24,8,128]{3,2,1,0:T(8,128)S(1)} custom-call(f32[6,24,8,128]{3,2,1,0:T(8,128)S(1)} %get-tuple-element.29.x_ref, f32[1152,128]{1,0:T(8,128)S(1)} %bitcast.14, f32[432,128]{1,0:T(8,128)S(1)} %shard_map.69.links_ref, f32[8,128]{1,0:T(8,128)S(1)} %get-tuple-element.22.rate_ref), custom_call_target="tpu_custom_call" | custom-call | flops 10000000 | bytes 3000000 | tf_op jit(solution)/shard_map/pallas_call | solution.py:429
  83.5 0.0 collective-permute-done.6.tnear_ref
  83.5 6.9 %collective-permute-done.7.tfar_ref = f32[12,8,128]{2,1,0:T(8,128)S(1)} collective-permute-done((f32[12,8,128]{2,1,0:T(8,128)S(1)}, f32[12,8,128]{2,1,0:T(8,128)S(1)}, u32[]{:S(2)}, u32[]{:S(2)}) %collective-permute-start.7) | collective-permute-done | bytes 49184 | tf_op jit(solution)/shard_map/ppermute | solution.py:379
  90.5 0.0 collective-permute-done.4.znear_ref
  90.5 0.0 collective-permute-done.5.zfar_ref
  90.5 1.2 %shard_map.74 = f32[1152,128]{1,0:T(8,128)} custom-call(f32[6,24,8,128]{3,2,1,0:T(8,128)S(1)} %shard_map.73.y_ref, f32[432,128]{1,0:T(8,128)S(1)} %shard_map.69.links_ref, f32[8,128]{1,0:T(8,128)S(1)} %get-tuple-element.22.rate_ref, f32[6,12,8,128]{3,2,1,0:T(8,128)S(1)} %collective-permute-done.4.znear_ref, ...), custom_call_target="tpu_custom_call" | custom-call | flops 5000000 | bytes 3000000 | tf_op jit(solution)/shard_map/pallas_call | solution.py:437
  (2 shorter events, 0.0 us)
Async XLA Ops:
  4.1 19.9 %all-to-all-start = ((f32[32,8,128]{2,1,0:T(8,128)}), f32[32,8,128]{2,1,0:T(8,128)S(1)}, u32[]{:S(2)}, u32[]{:S(2)}) async-start(f32[32,8,128]{2,1,0:T(8,128)} %get-tuple-element.18), calls=%async_computation | async-start | bytes 262144 | tf_op jit(solution)/shard_map/all_to_all | solution.py:407
  14.6 30.2 %copy-start.1 = (f32[32]{0:T(128)S(1)}, f32[32]{0:T(128)}, u32[]{:S(2)}) copy-start(f32[32]{0:T(128)} %param.7) | copy-start | bytes 388
  24.7 20.2 %all-to-all-start.1 = ((f32[16,8,128]{2,1,0:T(8,128)}), f32[16,8,128]{2,1,0:T(8,128)S(1)}, u32[]{:S(2)}, u32[]{:S(2)}) async-start(f32[16,8,128]{2,1,0:T(8,128)} %broadcast_in_dim.2), calls=%async_computation.1 | async-start | bytes 131072 | tf_op jit(solution)/shard_map/all_to_all | solution.py:414
  38.0 22.0 %copy-start = (f32[8,24,6,1,128]{4,3,2,1,0:T(1,128)S(1)}, f32[8,24,6,1,128]{4,3,2,1,0:T(1,128)}, u32[]{:S(2)}) copy-start(f32[8,24,6,1,128]{4,3,2,1,0:T(1,128)} %param.5) | copy-start | bytes 1769476
  45.9 21.2 %collective-permute-start = (f32[6,12,8,128]{3,2,1,0:T(8,128)S(1)}, f32[6,12,8,128]{3,2,1,0:T(8,128)S(1)}, u32[]{:S(2)}, u32[]{:S(2)}) collective-permute-start(f32[6,12,8,128]{3,2,1,0:T(8,128)S(1)} %get-tuple-element.25), channel_id=1, source_target_pairs={{0,64},{64,0},{128,192},{192,128},{256,320},{320,256},{384,448},{4... | collective-permute-start | bytes 884744 | tf_op jit(solution)/shard_map/ppermute | solution.py:376
  48.0 19.2 %collective-permute-start.1 = (f32[6,12,8,128]{3,2,1,0:T(8,128)S(1)}, f32[6,12,8,128]{3,2,1,0:T(8,128)S(1)}, u32[]{:S(2)}, u32[]{:S(2)}) collective-permute-start(f32[6,12,8,128]{3,2,1,0:T(8,128)S(1)} %get-tuple-element.26), channel_id=1, source_target_pairs={{0,448},{64,128},{128,64},{192,256},{256,192},{320,384},{384,320},... | collective-permute-start | bytes 884744 | tf_op jit(solution)/shard_map/ppermute | solution.py:377
  50.4 11.7 %collective-permute-start.2 = (f32[12,8,128]{2,1,0:T(8,128)S(1)}, f32[12,8,128]{2,1,0:T(8,128)S(1)}, u32[]{:S(2)}, u32[]{:S(2)}) collective-permute-start(f32[12,8,128]{2,1,0:T(8,128)S(1)} %get-tuple-element.27), channel_id=1, source_target_pairs={{0,1},{1,0},{2,3},{3,2},{4,5},{5,4},{6,7},{7,6},{8,9},{9,8},{10,11... | collective-permute-start | bytes 147464 | tf_op jit(solution)/shard_map/ppermute | solution.py:378
  53.8 13.4 %collective-permute-start.3 = (f32[12,8,128]{2,1,0:T(8,128)S(1)}, f32[12,8,128]{2,1,0:T(8,128)S(1)}, u32[]{:S(2)}, u32[]{:S(2)}) collective-permute-start(f32[12,8,128]{2,1,0:T(8,128)S(1)} %get-tuple-element.28), channel_id=1, source_target_pairs={{0,63},{1,2},{2,1},{3,4},{4,3},{5,6},{6,5},{7,8},{8,7},{9,10},{10,... | collective-permute-start | bytes 147464 | tf_op jit(solution)/shard_map/ppermute | solution.py:379
  67.7 22.8 %collective-permute-start.4 = (f32[6,12,8,128]{3,2,1,0:T(8,128)S(1)}, f32[6,12,8,128]{3,2,1,0:T(8,128)S(1)}, u32[]{:S(2)}, u32[]{:S(2)}) collective-permute-start(f32[6,12,8,128]{3,2,1,0:T(8,128)S(1)} %get-tuple-element.30), channel_id=1, source_target_pairs={{0,64},{64,0},{128,192},{192,128},{256,320},{320,256},{384,448},{4... | collective-permute-start | bytes 884744 | tf_op jit(solution)/shard_map/ppermute | solution.py:376
  72.3 18.2 %collective-permute-start.5 = (f32[6,12,8,128]{3,2,1,0:T(8,128)S(1)}, f32[6,12,8,128]{3,2,1,0:T(8,128)S(1)}, u32[]{:S(2)}, u32[]{:S(2)}) collective-permute-start(f32[6,12,8,128]{3,2,1,0:T(8,128)S(1)} %get-tuple-element.31), channel_id=1, source_target_pairs={{0,448},{64,128},{128,64},{192,256},{256,192},{320,384},{384,320},... | collective-permute-start | bytes 884744 | tf_op jit(solution)/shard_map/ppermute | solution.py:377
  74.2 9.4 %collective-permute-start.6 = (f32[12,8,128]{2,1,0:T(8,128)S(1)}, f32[12,8,128]{2,1,0:T(8,128)S(1)}, u32[]{:S(2)}, u32[]{:S(2)}) collective-permute-start(f32[12,8,128]{2,1,0:T(8,128)S(1)} %get-tuple-element.32), channel_id=1, source_target_pairs={{0,1},{1,0},{2,3},{3,2},{4,5},{5,4},{6,7},{7,6},{8,9},{9,8},{10,11... | collective-permute-start | bytes 147464 | tf_op jit(solution)/shard_map/ppermute | solution.py:378
  77.3 13.1 %collective-permute-start.7 = (f32[12,8,128]{2,1,0:T(8,128)S(1)}, f32[12,8,128]{2,1,0:T(8,128)S(1)}, u32[]{:S(2)}, u32[]{:S(2)}) collective-permute-start(f32[12,8,128]{2,1,0:T(8,128)S(1)} %get-tuple-element.33), channel_id=1, source_target_pairs={{0,63},{1,2},{2,1},{3,4},{4,3},{5,6},{6,5},{7,8},{8,7},{9,10},{10,... | collective-permute-start | bytes 147464 | tf_op jit(solution)/shard_map/ppermute | solution.py:379

commit v4 on v3

--- a/solution.py
+++ b/solution.py
@@ -184,10 +184,36 @@
     slot_ref[...] = jnp.where(at_row & at_lane, holder, 0.0)
 
 
-def slab_kernel(links_hbm, links_ref, sem):
+def fringe_kernel(eig_ref, links_hbm, links_ref, near_ref, far_ref, sem, *, nev, slices):
     copy = pltpu.make_async_copy(links_hbm.at[:, lax.axis_index("src")], links_ref, sem)
     copy.start()
+    place, even = t_place()
+    extent = lax.axis_size(("lat", "sub"))
+    half = nev * 12
+    row = lax.broadcasted_iota(jnp.int32, (half, 1), 0)
+    part = lax.rem(row, 12)
+    upper = 2 * (row - part) + part + jnp.where(part >= 6, 6, 0)
+    col = lax.broadcasted_iota(jnp.int32, (1, nev * 24), 1)
+    gap = col - upper
+
+    def edge(sign, t, flip):
+        pick = jnp.where(gap == 0, 1.0, jnp.where(gap == 6, float(sign), 0.0)).astype(jnp.bfloat16)
+        modes = eig_ref[:, t].reshape(nev * 24, 128)
+        value = jnp.dot(pick, modes, preferred_element_type=jnp.float32)
+        return value * jnp.where(flip, -1.0, 1.0)
+
+    up = edge(1, slices - 1, place == extent - 1)
+    down = edge(-1, 0, place == 0)
+    near_ref[0:half, :] = jnp.where(even, up, down)
+    far_ref[0:half, :] = jnp.where(even, down, up)
     copy.wait()
+    for comp in range(18):
+        link = links_ref[pl.ds((3 * 18 + comp) * slices + slices - 1, 1), :]
+        near_ref[half + comp : half + comp + 1, :] = link
+        far_ref[half + comp : half + comp + 1, :] = link
+    rest = near_ref.shape[0] - half - 18
+    near_ref[half + 18 :, :] = jnp.zeros((rest, 128), jnp.float32)
+    far_ref[half + 18 :, :] = jnp.zeros((rest, 128), jnp.float32)
 
 
 def choose(flag, half_true, half_false):
@@ -234,7 +260,8 @@
 
 
 def guess_kernel(
-    part_ref, ev_ref, eig_ref, links_ref, x_ref, rate_ref, znear_ref, zfar_ref, tnear_ref, tfar_ref,
+    part_ref, ev_ref, eig_ref, links_ref, near_ref, far_ref,
+    x_ref, rate_ref, znear_ref, zfar_ref, tbelow_ref, tabove_ref,
     *, nev, slices, norm,
 ):
     comps = 24
@@ -245,17 +272,21 @@
     w_re = ((total[:, :nev] / norm) / ev).astype(jnp.bfloat16)
     w_im = ((total[:, nev : 2 * nev] / norm) / ev).astype(jnp.bfloat16)
     rate_ref[...] = jnp.broadcast_to(total[:, 2 * nev : 2 * nev + 1], (8, 128))
-    row = lax.broadcasted_iota(jnp.int32, (nev, nev * comps), 0) * comps
-    col = lax.broadcasted_iota(jnp.int32, (nev, nev * comps), 1)
-    spread = jnp.where((col >= row) & (col < row + comps), 1.0, 0.0).astype(jnp.bfloat16)
-    w_re = jnp.dot(w_re, spread, preferred_element_type=jnp.float32)
-    w_im = jnp.dot(w_im, spread, preferred_element_type=jnp.float32)
-    comp = lax.rem(lax.broadcasted_iota(jnp.int32, (8, nev * comps), 1), comps)
-    blocks = []
-    for c in range(comps):
-        other, turned = (c + 12, -w_im) if c < 12 else (c - 12, w_im)
-        blocks.append(jnp.where(comp == c, w_re, jnp.where(comp == other, turned, 0.0)))
-    mix = jnp.concatenate(blocks, axis=0).astype(jnp.bfloat16)
+
+    def mixing(width, offset):
+        row = lax.broadcasted_iota(jnp.int32, (nev, nev * width), 0) * width
+        col = lax.broadcasted_iota(jnp.int32, (nev, nev * width), 1)
+        spread = jnp.where((col >= row) & (col < row + width), 1.0, 0.0).astype(jnp.bfloat16)
+        re = jnp.dot(w_re, spread, preferred_element_type=jnp.float32)
+        im = jnp.dot(w_im, spread, preferred_element_type=jnp.float32)
+        comp = lax.rem(lax.broadcasted_iota(jnp.int32, (8, nev * width), 1), width)
+        blocks = []
+        for c in range(width):
+            other, turned = (c + offset, -im) if c < offset else (c - offset, im)
+            blocks.append(jnp.where(comp == c, re, jnp.where(comp == other, turned, 0.0)))
+        return jnp.concatenate(blocks, axis=0)
+
+    mix = mixing(comps, 12).astype(jnp.bfloat16)
     for t in range(slices):
         res = jnp.dot(
             mix, eig_ref[:, t].reshape(nev * comps, 128), preferred_element_type=jnp.float32
@@ -270,7 +301,27 @@
         return carry
 
     lax.fori_loop(0, slices, step, 0)
-    emit_time_halos(x_ref, links_ref, tnear_ref, tfar_ref, slices)
+    half = nev * 12
+    mix = mixing(12, 6)
+    near, far = (
+        jnp.dot(
+            mix, ref[0:half, :], precision=lax.Precision.HIGHEST, preferred_element_type=jnp.float32
+        ).reshape(12, 8, 128)
+        for ref in (near_ref, far_ref)
+    )
+    near, far = (load_half(lambda i, v=v: v[i]) for v in (near, far))
+    _, even = t_place()
+
+    def link_of(comp):
+        rows = [ref[half + comp : half + comp + 1, :] for ref in (far_ref, near_ref)]
+        return jnp.broadcast_to(jnp.where(even, *rows), (8, 128))
+
+    link = {
+        (a, c): (link_of(3 * a + c), link_of(9 + 3 * a + c)) for a in range(3) for c in range(3)
+    }
+    below = colour_mul(link, choose(even, far, near), True)
+    store_half(lambda i, v: tbelow_ref.__setitem__(i, v), below)
+    store_half(lambda i, v: tabove_ref.__setitem__(i, v), choose(even, near, far))
 
 
 def local_kernel(x_ref, src_ref, links_ref, rate_ref, *refs, slices, keep):
@@ -309,7 +360,7 @@
 
 
 def halo_kernel(
-    y_ref, links_ref, rate_ref, znear_ref, zfar_ref, tnear_ref, tfar_ref, *refs, slices, final
+    y_ref, links_ref, rate_ref, znear_ref, zfar_ref, tnear_ref, tfar_ref, *refs, slices, final, sorted_t
 ):
     above_near = z_even()
     _, t_even = t_place()
@@ -317,9 +368,9 @@
     last = slices - 1
     near, far = (load_half(lambda i, ref=ref: ref[i]) for ref in (tnear_ref, tfar_ref))
     link = load_link(links_ref, slices, 3, last)
-    above = colour_mul(link, choose(t_even, near, far), False)
-    store_half(lambda i, v: edge_ref.__setitem__((0, i), v), above)
-    store_half(lambda i, v: edge_ref.__setitem__((1, i), v), choose(t_even, far, near))
+    below, above = (near, far) if sorted_t else (choose(t_even, far, near), choose(t_even, near, far))
+    store_half(lambda i, v: edge_ref.__setitem__((0, i), v), colour_mul(link, above, False))
+    store_half(lambda i, v: edge_ref.__setitem__((1, i), v), below)
 
     def step(t, carry):
         acc = {}
@@ -366,18 +417,10 @@
     )
 
 
-def exchange(send):
-    znear, zfar, tnear, tfar = send
-    nz, nt = lax.axis_size("src"), lax.axis_size(("lat", "sub"))
-    near = lambda n: [(i, i ^ 1) for i in range(n)]
-    far = lambda n: [(i, (i + 1 if i % 2 else i - 1) % n) for i in range(n)]
-
-    return (
-        lax.ppermute(znear, "src", near(nz)),
-        lax.ppermute(zfar, "src", far(nz)),
-        lax.ppermute(tnear, ("lat", "sub"), near(nt)),
-        lax.ppermute(tfar, ("lat", "sub"), far(nt)),
-    )
+def swap(x, axis, far):
+    n = lax.axis_size(axis)
+    partner = lambda i: (i + 1 if i % 2 else i - 1) % n if far else i ^ 1
+    return lax.ppermute(x, axis, [(i, partner(i)) for i in range(n)])
 
 
 def shards(sources, eigvecs, eigvals, links, damping):
@@ -405,10 +448,15 @@
         ],
     )(hbm(eig), hbm(src))
     partial = lax.all_to_all(partial, "lat", 0, 0, tiled=True)
-    flat_links = call(
-        slab_kernel, shape(4 * 18 * slices, 128), 1, 1000, hbm=(0,),
+    fringe = shape(nev * 12 + 24, 128)
+    flat_links, near, far = call(
+        functools.partial(fringe_kernel, nev=nev, slices=slices),
+        (shape(4 * 18 * slices, 128), fringe, fringe), 2, 1000, hbm=(1,),
         scratch=[pltpu.SemaphoreType.DMA],
-    )(hbm(links))
+    )(eig, hbm(links))
+    time = ("lat", "sub")
+    far = swap(far, time, True)
+    near = swap(near, time, False)
     partial = partial.sum(0) + slot * damping[0]
     partial = jnp.broadcast_to(partial[None], (rest, 8, 128))
     partial = lax.all_to_all(partial, ("sub", "src"), 0, 0, tiled=True)
@@ -418,14 +466,18 @@
     flat = shape(count * comps * slices, 128)
     x, rate, *send = call(
         functools.partial(guess_kernel, nev=nev, slices=slices, norm=norm),
-        (field, shape(8, 128)) + halos, 4, 226_000_000,
-    )(partial, eigvals.reshape(1, nev), eig, flat_links)
+        (field, shape(8, 128)) + halos, 6, 226_000_000,
+    )(partial, eigvals.reshape(1, nev), eig, flat_links, near, far)
 
     guess = None
     for sweep in range(ITERS):
         final = sweep == ITERS - 1
         keep = sweep == 0
-        got = exchange(send)
+        got = [swap(send[0], "src", False), swap(send[1], "src", True)]
+        if sweep == 0:
+            got += send[2:]
+        else:
+            got += [swap(send[2], time, False), swap(send[3], time, True)]
         y, *kept = call(
             functools.partial(local_kernel, slices=slices, keep=keep),
             (field,) + ((flat,) if keep else ()), 4, 10_000_000,
@@ -435,7 +487,7 @@
             guess = kept[0]
         outs = flat if final else (field,) + halos
         res = call(
-            functools.partial(halo_kernel, slices=slices, final=final),
+            functools.partial(halo_kernel, slices=slices, final=final, sorted_t=sweep == 0),
             outs, 7, 5_000_000,
             scratch=[pltpu.VMEM((2, 12, 8, 128), f32)],
         )(y, flat_links, rate, *got)

time: 92.2 us -> 91.6 us (level)
  waiting for transfers between devices: 27.5 us -> 22 us
  starting transfers between devices: 51.5 us -> 55.3 us
  Pallas kernels: 10.6 us -> 11.6 us
    ppermute x8, starting transfers between devices: 28.6 us -> 38.7 us  [swap(): return lax.ppermute(x, axis, [(i, partner(i)) for i in range(n)])]
    all_to_all x1, waiting for transfers between devices: 8.67 us -> 0.01 us  [shards(): partial = lax.all_to_all(partial, 'lat', 0, 0, tiled=True)]
    all_to_all x1, starting transfers between devices: 12.4 us -> 6.1 us  [shards(): partial = lax.all_to_all(partial, ('sub', 'src'), 0, 0, tiled=True)]
    ppermute x8, waiting for transfers between devices: 12 us -> 16.9 us  [swap(): return lax.ppermute(x, axis, [(i, partner(i)) for i in range(n)])]
    all_to_all x1, waiting for transfers between devices: 6.81 us -> 5.09 us  [shards(): partial = lax.all_to_all(partial, ('sub', 'src'), 0, 0, tiled=True)]
  transfers between devices with their start and end apart: 10 -> 10, of which waited for: 4 -> 4; matrix products, arithmetic and copies ran while one was open for 0% -> 1% of each run, Pallas kernels for 5% -> 5%
where the time goes in v4:
time: 91.6 us; the launch traced here: 91 us
  starting transfers between devices  55.3 us (60%)
  waiting for transfers between devices  22 us (24%)
  Pallas kernels  11.6 us (13%)
  between operations  1.43 us (2%)
    ppermute x8, starting transfers between devices, swap(): return lax.ppermute(x, axis, [(i, partner(i)) for i in range(n)])  38.7 us
    ppermute x8, waiting for transfers between devices, swap(): return lax.ppermute(x, axis, [(i, partner(i)) for i in range(n)])  16.9 us
    all_to_all x1, starting transfers between devices, shards(): partial = lax.all_to_all(partial, 'lat', 0, 0, tiled=True)  10.5 us
    all_to_all x1, starting transfers between devices, shards(): partial = lax.all_to_all(partial, ('sub', 'src'), 0, 0, tiled=True)  6.1 us
    all_to_all x1, waiting for transfers between devices, shards(): partial = lax.all_to_all(partial, ('sub', 'src'), 0, 0, tiled=True)  5.09 us
    pallas_call x1, Pallas kernels, shards(): call(functools.partial(correlation_kernel, nev=nev, slices=slices), (shap...  3.48 us
    pallas_call x2, Pallas kernels, shards(): call(functools.partial(local_kernel, slices=slices, keep=keep), (field,)...  3.28 us
  transfers between devices with their start and end apart: 10, of which 4 were waited for; matrix products, arithmetic and copies ran while one was open for 1% of the time, Pallas kernels for 5%

profile of v4, /device:TPU:1, one launch (start us, length us, event | category | flops | bytes accessed | tf_op | source)
XLA Modules:
  0.0 91.0 jit_solution(12559048170880702234)
XLA Ops:
  0.6 3.5 %shard_map.68 = (f32[32,8,128]{2,1,0:T(8,128)}, bf16[32,6,24,128]{3,2,1,0:T(8,128)(2,1)S(1)}, f32[8,128]{1,0:T(8,128)S(1)}) custom-call(bf16[32,6,24,128]{3,2,1,0:T(8,128)(2,1)} %bitcast.17, f32[1152,128]{1,0:T(8,128)} %bitcast.12), custom_call_target="tpu_custom_call" | custom-call | flops 226000000 | bytes 3000000 | tf_op jit(solution)/shard_map/pallas_call | solution.py:441
  4.1 10.5 %all-to-all-start = ((f32[32,8,128]{2,1,0:T(8,128)}), f32[32,8,128]{2,1,0:T(8,128)S(1)}, u32[]{:S(2)}, u32[]{:S(2)}) async-start(f32[32,8,128]{2,1,0:T(8,128)} %get-tuple-element.21), calls=%async_computation | async-start | bytes 262144 | tf_op jit(solution)/shard_map/all_to_all | solution.py:450
  14.6 0.0 copy-start.1
  14.6 1.4 %shard_map.69 = (f32[432,128]{1,0:T(8,128)S(1)}, f32[408,128]{1,0:T(8,128)S(1)}, f32[408,128]{1,0:T(8,128)S(1)}) custom-call(bf16[32,6,24,128]{3,2,1,0:T(8,128)(2,1)S(1)} %get-tuple-element.23.eig_ref, f32[432,8,128]{2,1,0:T(8,128)} %bitcast.16), custom_call_target="tpu_custom_call" | custom-call | flops 1000 | bytes 3000000 | tf_op jit(solution)/shard_map/pallas_call | solution.py:452
  16.0 0.0 copy-start
  16.1 10.8 %collective-permute-start = (f32[408,128]{1,0:T(8,128)S(1)}, f32[408,128]{1,0:T(8,128)S(1)}, u32[]{:S(2)}, u32[]{:S(2)}) collective-permute-start(f32[408,128]{1,0:T(8,128)S(1)} %get-tuple-element.25), channel_id=1, source_target_pairs={{0,1},{1,0},{2,3},{3,2},{4,5},{5,4},{6,7},{7,6},{8,9},{9,8},{10,11... | collective-permute-start | bytes 626696 | tf_op jit(solution)/shard_map/ppermute | solution.py:423
  26.8 6.3 %collective-permute-start.1 = (f32[408,128]{1,0:T(8,128)S(1)}, f32[408,128]{1,0:T(8,128)S(1)}, u32[]{:S(2)}, u32[]{:S(2)}) collective-permute-start(f32[408,128]{1,0:T(8,128)S(1)} %get-tuple-element.26), channel_id=1, source_target_pairs={{0,63},{1,2},{2,1},{3,4},{4,3},{5,6},{6,5},{7,8},{8,7},{9,10},{10,... | collective-permute-start | bytes 626696 | tf_op jit(solution)/shard_map/ppermute | solution.py:423
  33.8 0.0 all-to-all-done
  33.8 0.6 broadcast_in_dim.2
  34.5 6.1 %all-to-all-start.1 = ((f32[16,8,128]{2,1,0:T(8,128)}), f32[16,8,128]{2,1,0:T(8,128)S(1)}, u32[]{:S(2)}, u32[]{:S(2)}) async-start(f32[16,8,128]{2,1,0:T(8,128)} %broadcast_in_dim.2), calls=%async_computation.1 | async-start | bytes 131072 | tf_op jit(solution)/shard_map/all_to_all | solution.py:462
  40.6 0.0 collective-permute-done.near_ref
  40.6 4.9 %collective-permute-done.1.far_ref = f32[408,128]{1,0:T(8,128)S(1)} collective-permute-done((f32[408,128]{1,0:T(8,128)S(1)}, f32[408,128]{1,0:T(8,128)S(1)}, u32[]{:S(2)}, u32[]{:S(2)}) %collective-permute-start.1) | collective-permute-done | bytes 208928 | tf_op jit(solution)/shard_map/ppermute | solution.py:423
  45.5 5.1 %all-to-all-done.1.part_ref = f32[16,8,128]{2,1,0:T(8,128)S(1)} async-done(((f32[16,8,128]{2,1,0:T(8,128)}), f32[16,8,128]{2,1,0:T(8,128)S(1)}, u32[]{:S(2)}, u32[]{:S(2)}) %all-to-all-start.1) | async-done | bytes 65568 | tf_op jit(solution)/shard_map/all_to_all | solution.py:462
  50.6 0.0 copy-done.1
  50.6 1.7 %shard_map.70 = (f32[6,24,8,128]{3,2,1,0:T(8,128)S(1)}, f32[8,128]{1,0:T(8,128)S(1)}, f32[6,12,8,128]{3,2,1,0:T(8,128)S(1)}, f32[6,12,8,128]{3,2,1,0:T(8,128)S(1...) custom-call(f32[16,8,128]{2,1,0:T(8,128)S(1)} %all-to-all-done.1.part_ref, f32[1,32]{1,0:T(1,128)S(1)} %bitcast.15, ...), custom_call_target="tpu_custom_call" | custom-call | flops 226000000 | bytes 3000000 | tf_op jit(solution)/shard_map/pallas_call | solution.py:467
  52.3 2.0 %collective-permute-start.2 = (f32[6,12,8,128]{3,2,1,0:T(8,128)S(1)}, f32[6,12,8,128]{3,2,1,0:T(8,128)S(1)}, u32[]{:S(2)}, u32[]{:S(2)}) collective-permute-start(f32[6,12,8,128]{3,2,1,0:T(8,128)S(1)} %get-tuple-element.31), channel_id=1, source_target_pairs={{0,64},{64,0},{128,192},{192,128},{256,320},{320,256},{384,448},{4... | collective-permute-start | bytes 884744 | tf_op jit(solution)/shard_map/ppermute | solution.py:423
  54.3 1.9 %collective-permute-start.3 = (f32[6,12,8,128]{3,2,1,0:T(8,128)S(1)}, f32[6,12,8,128]{3,2,1,0:T(8,128)S(1)}, u32[]{:S(2)}, u32[]{:S(2)}) collective-permute-start(f32[6,12,8,128]{3,2,1,0:T(8,128)S(1)} %get-tuple-element.32), channel_id=1, source_target_pairs={{0,448},{64,128},{128,64},{192,256},{256,192},{320,384},{384,320},... | collective-permute-start | bytes 884744 | tf_op jit(solution)/shard_map/ppermute | solution.py:423
  56.2 0.0 copy-done
  56.2 2.0 %shard_map.71 = (f32[6,24,8,128]{3,2,1,0:T(8,128)S(1)}, f32[1152,128]{1,0:T(8,128)}) custom-call(f32[6,24,8,128]{3,2,1,0:T(8,128)S(1)} %get-tuple-element.27.x_ref, f32[1152,128]{1,0:T(8,128)S(1)} %bitcast.13, f32[432,128]{1,0:T(8,128)S(1)} %get-tuple-element.24.links_ref, f32[8,128]{1,0:T(8,128)S(1)} %get-tuple-element.28.rate_ref), custom_call_target="tpu_custom_call" | custom-call | flops 10000000 | bytes 3000000 | tf_op jit(solution)/shard_map/pallas_call | solution.py:481
  58.3 0.0 collective-permute-done.2.znear_ref
  58.3 7.2 %collective-permute-done.3.zfar_ref = f32[6,12,8,128]{3,2,1,0:T(8,128)S(1)} collective-permute-done((f32[6,12,8,128]{3,2,1,0:T(8,128)S(1)}, f32[6,12,8,128]{3,2,1,0:T(8,128)S(1)}, u32[]{:S(2)}, u32[]{:S(2)}) %collective-permute-start.3) | collective-permute-done | bytes 294944 | tf_op jit(solution)/shard_map/ppermute | solution.py:423
  65.5 0.5 shard_map.72
  66.0 2.1 %collective-permute-start.4 = (f32[6,12,8,128]{3,2,1,0:T(8,128)S(1)}, f32[6,12,8,128]{3,2,1,0:T(8,128)S(1)}, u32[]{:S(2)}, u32[]{:S(2)}) collective-permute-start(f32[6,12,8,128]{3,2,1,0:T(8,128)S(1)} %get-tuple-element.36), channel_id=1, source_target_pairs={{0,64},{64,0},{128,192},{192,128},{256,320},{320,256},{384,448},{4... | collective-permute-start | bytes 884744 | tf_op jit(solution)/shard_map/ppermute | solution.py:423
  68.1 1.9 %collective-permute-start.5 = (f32[6,12,8,128]{3,2,1,0:T(8,128)S(1)}, f32[6,12,8,128]{3,2,1,0:T(8,128)S(1)}, u32[]{:S(2)}, u32[]{:S(2)}) collective-permute-start(f32[6,12,8,128]{3,2,1,0:T(8,128)S(1)} %get-tuple-element.37), channel_id=1, source_target_pairs={{0,448},{64,128},{128,64},{192,256},{256,192},{320,384},{384,320},... | collective-permute-start | bytes 884744 | tf_op jit(solution)/shard_map/ppermute | solution.py:423
  70.1 6.5 %collective-permute-start.6 = (f32[12,8,128]{2,1,0:T(8,128)S(1)}, f32[12,8,128]{2,1,0:T(8,128)S(1)}, u32[]{:S(2)}, u32[]{:S(2)}) collective-permute-start(f32[12,8,128]{2,1,0:T(8,128)S(1)} %get-tuple-element.38), channel_id=1, source_target_pairs={{0,1},{1,0},{2,3},{3,2},{4,5},{5,4},{6,7},{7,6},{8,9},{9,8},{10,11... | collective-permute-start | bytes 147464 | tf_op jit(solution)/shard_map/ppermute | solution.py:423
  76.5 7.2 %collective-permute-start.7 = (f32[12,8,128]{2,1,0:T(8,128)S(1)}, f32[12,8,128]{2,1,0:T(8,128)S(1)}, u32[]{:S(2)}, u32[]{:S(2)}) collective-permute-start(f32[12,8,128]{2,1,0:T(8,128)S(1)} %get-tuple-element.39), channel_id=1, source_target_pairs={{0,63},{1,2},{2,1},{3,4},{4,3},{5,6},{6,5},{7,8},{8,7},{9,10},{10,... | collective-permute-start | bytes 147464 | tf_op jit(solution)/shard_map/ppermute | solution.py:423
  83.8 1.2 %shard_map.73.y_ref = f32[6,24,8,128]{3,2,1,0:T(8,128)S(1)} custom-call(f32[6,24,8,128]{3,2,1,0:T(8,128)S(1)} %get-tuple-element.35.x_ref, f32[1152,128]{1,0:T(8,128)S(1)} %bitcast.14, f32[432,128]{1,0:T(8,128)S(1)} %get-tuple-element.24.links_ref, f32[8,128]{1,0:T(8,128)S(1)} %get-tuple-element.28.rate_ref), custom_call_target="tpu_custom_call" | custom-call | flops 10000000 | bytes 3000000 | tf_op jit(solution)/shard_map/pallas_call | solution.py:481
  85.0 0.0 collective-permute-done.6.tnear_ref
  85.0 4.7 %collective-permute-done.7.tfar_ref = f32[12,8,128]{2,1,0:T(8,128)S(1)} collective-permute-done((f32[12,8,128]{2,1,0:T(8,128)S(1)}, f32[12,8,128]{2,1,0:T(8,128)S(1)}, u32[]{:S(2)}, u32[]{:S(2)}) %collective-permute-start.7) | collective-permute-done | bytes 49184 | tf_op jit(solution)/shard_map/ppermute | solution.py:423
  89.8 0.0 collective-permute-done.4.znear_ref
  89.8 0.0 collective-permute-done.5.zfar_ref
  89.8 1.2 %shard_map.74 = f32[1152,128]{1,0:T(8,128)} custom-call(f32[6,24,8,128]{3,2,1,0:T(8,128)S(1)} %shard_map.73.y_ref, f32[432,128]{1,0:T(8,128)S(1)} %get-tuple-element.24.links_ref, f32[8,128]{1,0:T(8,128)S(1)} %get-tuple-element.28.rate_ref, f32[6,12,8,128]{3,2,1,0:T(8,128)S(1)} %collective-permute-done.4.znear_ref, ...), custom_call_target="tpu_custom_call" | custom-call | flops 5000000 | bytes 3000000 | tf_op jit(solution)/shard_map/pallas_call | solution.py:489
  (2 shorter events, 0.0 us)
Async XLA Ops:
  4.1 29.6 %all-to-all-start = ((f32[32,8,128]{2,1,0:T(8,128)}), f32[32,8,128]{2,1,0:T(8,128)S(1)}, u32[]{:S(2)}, u32[]{:S(2)}) async-start(f32[32,8,128]{2,1,0:T(8,128)} %get-tuple-element.21), calls=%async_computation | async-start | bytes 262144 | tf_op jit(solution)/shard_map/all_to_all | solution.py:450
  14.6 35.9 %copy-start.1 = (f32[32]{0:T(128)S(1)}, f32[32]{0:T(128)}, u32[]{:S(2)}) copy-start(f32[32]{0:T(128)} %param.7) | copy-start | bytes 388
  16.0 40.2 %copy-start = (f32[8,24,6,1,128]{4,3,2,1,0:T(1,128)S(1)}, f32[8,24,6,1,128]{4,3,2,1,0:T(1,128)}, u32[]{:S(2)}) copy-start(f32[8,24,6,1,128]{4,3,2,1,0:T(1,128)} %param.5) | copy-start | bytes 1769476
  16.1 24.5 %collective-permute-start = (f32[408,128]{1,0:T(8,128)S(1)}, f32[408,128]{1,0:T(8,128)S(1)}, u32[]{:S(2)}, u32[]{:S(2)}) collective-permute-start(f32[408,128]{1,0:T(8,128)S(1)} %get-tuple-element.25), channel_id=1, source_target_pairs={{0,1},{1,0},{2,3},{3,2},{4,5},{5,4},{6,7},{7,6},{8,9},{9,8},{10,11... | collective-permute-start | bytes 626696 | tf_op jit(solution)/shard_map/ppermute | solution.py:423
  26.8 18.6 %collective-permute-start.1 = (f32[408,128]{1,0:T(8,128)S(1)}, f32[408,128]{1,0:T(8,128)S(1)}, u32[]{:S(2)}, u32[]{:S(2)}) collective-permute-start(f32[408,128]{1,0:T(8,128)S(1)} %get-tuple-element.26), channel_id=1, source_target_pairs={{0,63},{1,2},{2,1},{3,4},{4,3},{5,6},{6,5},{7,8},{8,7},{9,10},{10,... | collective-permute-start | bytes 626696 | tf_op jit(solution)/shard_map/ppermute | solution.py:423
  34.5 16.1 %all-to-all-start.1 = ((f32[16,8,128]{2,1,0:T(8,128)}), f32[16,8,128]{2,1,0:T(8,128)S(1)}, u32[]{:S(2)}, u32[]{:S(2)}) async-start(f32[16,8,128]{2,1,0:T(8,128)} %broadcast_in_dim.2), calls=%async_computation.1 | async-start | bytes 131072 | tf_op jit(solution)/shard_map/all_to_all | solution.py:462
  52.3 6.0 %collective-permute-start.2 = (f32[6,12,8,128]{3,2,1,0:T(8,128)S(1)}, f32[6,12,8,128]{3,2,1,0:T(8,128)S(1)}, u32[]{:S(2)}, u32[]{:S(2)}) collective-permute-start(f32[6,12,8,128]{3,2,1,0:T(8,128)S(1)} %get-tuple-element.31), channel_id=1, source_target_pairs={{0,64},{64,0},{128,192},{192,128},{256,320},{320,256},{384,448},{4... | collective-permute-start | bytes 884744 | tf_op jit(solution)/shard_map/ppermute | solution.py:423
  54.3 11.2 %collective-permute-start.3 = (f32[6,12,8,128]{3,2,1,0:T(8,128)S(1)}, f32[6,12,8,128]{3,2,1,0:T(8,128)S(1)}, u32[]{:S(2)}, u32[]{:S(2)}) collective-permute-start(f32[6,12,8,128]{3,2,1,0:T(8,128)S(1)} %get-tuple-element.32), channel_id=1, source_target_pairs={{0,448},{64,128},{128,64},{192,256},{256,192},{320,384},{384,320},... | collective-permute-start | bytes 884744 | tf_op jit(solution)/shard_map/ppermute | solution.py:423
  66.0 23.7 %collective-permute-start.4 = (f32[6,12,8,128]{3,2,1,0:T(8,128)S(1)}, f32[6,12,8,128]{3,2,1,0:T(8,128)S(1)}, u32[]{:S(2)}, u32[]{:S(2)}) collective-permute-start(f32[6,12,8,128]{3,2,1,0:T(8,128)S(1)} %get-tuple-element.36), channel_id=1, source_target_pairs={{0,64},{64,0},{128,192},{192,128},{256,320},{320,256},{384,448},{4... | collective-permute-start | bytes 884744 | tf_op jit(solution)/shard_map/ppermute | solution.py:423
  68.1 21.6 %collective-permute-start.5 = (f32[6,12,8,128]{3,2,1,0:T(8,128)S(1)}, f32[6,12,8,128]{3,2,1,0:T(8,128)S(1)}, u32[]{:S(2)}, u32[]{:S(2)}) collective-permute-start(f32[6,12,8,128]{3,2,1,0:T(8,128)S(1)} %get-tuple-element.37), channel_id=1, source_target_pairs={{0,448},{64,128},{128,64},{192,256},{256,192},{320,384},{384,320},... | collective-permute-start | bytes 884744 | tf_op jit(solution)/shard_map/ppermute | solution.py:423
  70.1 14.9 %collective-permute-start.6 = (f32[12,8,128]{2,1,0:T(8,128)S(1)}, f32[12,8,128]{2,1,0:T(8,128)S(1)}, u32[]{:S(2)}, u32[]{:S(2)}) collective-permute-start(f32[12,8,128]{2,1,0:T(8,128)S(1)} %get-tuple-element.38), channel_id=1, source_target_pairs={{0,1},{1,0},{2,3},{3,2},{4,5},{5,4},{6,7},{7,6},{8,9},{9,8},{10,11... | collective-permute-start | bytes 147464 | tf_op jit(solution)/shard_map/ppermute | solution.py:423
  76.5 13.2 %collective-permute-start.7 = (f32[12,8,128]{2,1,0:T(8,128)S(1)}, f32[12,8,128]{2,1,0:T(8,128)S(1)}, u32[]{:S(2)}, u32[]{:S(2)}) collective-permute-start(f32[12,8,128]{2,1,0:T(8,128)S(1)} %get-tuple-element.39), channel_id=1, source_target_pairs={{0,63},{1,2},{2,1},{3,4},{4,3},{5,6},{6,5},{7,8},{8,7},{9,10},{10,... | collective-permute-start | bytes 147464 | tf_op jit(solution)/shard_map/ppermute | solution.py:423

commit v5 on v2

--- a/solution.py
+++ b/solution.py
@@ -128,7 +128,7 @@
 
 
 def correlation_kernel(
-    eig_hbm, src_hbm, links_hbm, damp_ref, out_ref, eig_ref, links_ref, src_ref, sems, *, nev, slices
+    eig_hbm, src_hbm, damp_ref, out_ref, eig_ref, src_ref, sems, *, nev, slices
 ):
     comps = 24
     sources = 8
@@ -142,10 +142,7 @@
     eig_copies = [
         pltpu.make_async_copy(eig_hbm.at[:, t], eig_ref.at[:, t], sems.at[t]) for t in range(slices)
     ]
-    links_copy = pltpu.make_async_copy(
-        links_hbm.at[:, lax.axis_index("src")], links_ref, sems.at[slices + 2]
-    )
-    for copy in src_copies + eig_copies + [links_copy]:
+    for copy in src_copies + eig_copies:
         copy.start()
     for copy in src_copies:
         copy.wait()
@@ -180,7 +177,6 @@
         jnp.dot, precision=lax.Precision.HIGHEST, preferred_element_type=jnp.float32
     )
     total = dot(straight, gather(0)) + dot(crossed, gather(1))
-    links_copy.wait()
     holder = (lax.axis_index("lat") == 0) & (lax.axis_index("sub") == 0)
     value = jnp.where(holder, damp_ref[0], 0.0)
     at_row = lax.broadcasted_iota(jnp.int32, (8, 128), 0) == lax.axis_index("src")
@@ -217,26 +213,36 @@
     store_half(lambda i, v: far_ref.__setitem__((t, i), v), choose(even, down, up))
 
 
-def emit_time_halos(x_ref, links_ref, near_ref, far_ref, slices):
+def emit_time_halos(load_last, load_first, links_ref, near_ref, far_ref, slices):
     place, even = t_place()
     extent = lax.axis_size(("lat", "sub"))
     up_sign = jnp.where(place == extent - 1, -1.0, 1.0)
     down_sign = jnp.where(place == 0, -1.0, 1.0)
     last = slices - 1
-    up = project(1, 3, lambda p, s, c: x_ref[last, 12 * p + 3 * s + c])
+    up = project(1, 3, load_last)
     up = colour_mul(load_link(links_ref, slices, 3, last), up, True)
     up = map_half(lambda v: v * up_sign, up)
-    down = project(-1, 3, lambda p, s, c: x_ref[0, 12 * p + 3 * s + c])
+    down = project(-1, 3, load_first)
     down = map_half(lambda v: v * down_sign, down)
     store_half(lambda i, v: near_ref.__setitem__(i, v), choose(even, up, down))
     store_half(lambda i, v: far_ref.__setitem__(i, v), choose(even, down, up))
 
 
 def guess_kernel(
-    part_ref, ev_ref, eig_ref, links_ref, x_ref, rate_ref, znear_ref, zfar_ref, tnear_ref, tfar_ref,
+    part_ref, ev_ref, eig_ref, links_hbm,
+    x_ref, links_ref, rate_ref, guess_ref, znear_ref, zfar_ref, tnear_ref, tfar_ref, sems,
     *, nev, slices, norm,
 ):
     comps = 24
+    copies = []
+    for i, first in enumerate((2, 0)):
+        rows = pl.ds(first * 18 * slices, 2 * 18 * slices)
+        copies.append(
+            pltpu.make_async_copy(
+                links_hbm.at[rows, lax.axis_index("src")], links_ref.at[rows], sems.at[i]
+            )
+        )
+        copies[-1].start()
     total = part_ref[0]
     for i in range(1, part_ref.shape[0]):
         total = total + part_ref[i]
@@ -260,8 +266,11 @@
             mix, eig_ref[:, t].reshape(nev * comps, 128), preferred_element_type=jnp.float32
         )
         x_ref[t] = res.reshape(comps, 8, 128)
+    copies[0].wait()
 
     def step(t, carry):
+        for c in range(comps):
+            guess_ref[pl.ds(c * slices + t, 8, stride=comps * slices), :] = x_ref[t, c]
         emit_halos(
             lambda p, s, c: x_ref[t, 12 * p + 3 * s + c],
             links_ref, t, znear_ref, zfar_ref, slices,
@@ -269,11 +278,12 @@
         return carry
 
     lax.fori_loop(0, slices, step, 0)
-    emit_time_halos(x_ref, links_ref, tnear_ref, tfar_ref, slices)
-
-
-def local_kernel(x_ref, src_ref, links_ref, rate_ref, *refs, slices, keep):
-    y_ref, behind_ref = refs[0], refs[-1]
+    load = lambda t: lambda p, s, c: x_ref[t, 12 * p + 3 * s + c]
+    emit_time_halos(load(slices - 1), load(0), links_ref, tnear_ref, tfar_ref, slices)
+    copies[1].wait()
+
+
+def local_kernel(x_ref, src_ref, links_ref, rate_ref, y_ref, behind_ref, *, slices):
     behind_ref[...] = jnp.zeros_like(behind_ref)
 
     def step(t, carry):
@@ -300,17 +310,34 @@
             where = pl.ds(comp * slices + t, 8, stride=24 * slices)
             value = load(p, s, c)
             y_ref[t, comp] = value + rate * (src_ref[where, :] - (value - HOPPING * hop))
-            if keep:
-                refs[1][where, :] = value
         return carry
 
     lax.fori_loop(0, slices, step, 0)
+
+
+def z_hops(links_ref, znear_ref, zfar_ref, t, slices):
+    above_near = z_even()
+    acc = {}
+    near, far = (load_half(lambda i, ref=ref: ref[t, i]) for ref in (znear_ref, zfar_ref))
+    link = load_link(links_ref, slices, 2, t)
+    rebuild_into(acc, -1, 2, colour_mul(link, choose(above_near, near, far), False))
+    rebuild_into(acc, 1, 2, choose(above_near, far, near))
+    return acc
+
+
+def edge_kernel(y_ref, links_ref, rate_ref, znear_ref, zfar_ref, tnear_ref, tfar_ref, *, slices):
+    rate = rate_ref[...] * HOPPING
+
+    def load(t):
+        hops = z_hops(links_ref, znear_ref, zfar_ref, t, slices)
+        return lambda p, s, c: y_ref[t, 12 * p + 3 * s + c] + rate * hops[(p, s, c)]
+
+    emit_time_halos(load(slices - 1), load(0), links_ref, tnear_ref, tfar_ref, slices)
 
 
 def halo_kernel(
     y_ref, links_ref, rate_ref, znear_ref, zfar_ref, tnear_ref, tfar_ref, *refs, slices, final
 ):
-    above_near = z_even()
     _, t_even = t_place()
     edge_ref = refs[-1]
     last = slices - 1
@@ -321,11 +348,7 @@
     store_half(lambda i, v: edge_ref.__setitem__((1, i), v), choose(t_even, far, near))
 
     def step(t, carry):
-        acc = {}
-        near, far = (load_half(lambda i, ref=ref: ref[t, i]) for ref in (znear_ref, zfar_ref))
-        link = load_link(links_ref, slices, 2, t)
-        rebuild_into(acc, -1, 2, colour_mul(link, choose(above_near, near, far), False))
-        rebuild_into(acc, 1, 2, choose(above_near, far, near))
+        acc = z_hops(links_ref, znear_ref, zfar_ref, t, slices)
         top, bottom = (jnp.where(t == edge, 1.0, 0.0) for edge in (last, 0))
         rebuild_into(acc, -1, 3, map_half(lambda v: v * top, load_half(lambda i: edge_ref[0, i])))
         rebuild_into(acc, 1, 3, map_half(lambda v: v * bottom, load_half(lambda i: edge_ref[1, i])))
@@ -346,8 +369,6 @@
         return carry
 
     lax.fori_loop(0, slices, step, 0)
-    if not final:
-        emit_time_halos(refs[0], links_ref, refs[3], refs[4], slices)
 
 
 def call(kernel, outs, ins, flops, hbm=(), smem=(), scratch=()):
@@ -365,18 +386,10 @@
     )
 
 
-def exchange(send):
-    znear, zfar, tnear, tfar = send
-    nz, nt = lax.axis_size("src"), lax.axis_size(("lat", "sub"))
-    near = lambda n: [(i, i ^ 1) for i in range(n)]
-    far = lambda n: [(i, (i + 1 if i % 2 else i - 1) % n) for i in range(n)]
-
-    return (
-        lax.ppermute(znear, "src", near(nz)),
-        lax.ppermute(zfar, "src", far(nz)),
-        lax.ppermute(tnear, ("lat", "sub"), near(nt)),
-        lax.ppermute(tfar, ("lat", "sub"), far(nt)),
-    )
+def swap(x, axis, far):
+    n = lax.axis_size(axis)
+    partner = lambda i: (i + 1 if i % 2 else i - 1) % n if far else i ^ 1
+    return lax.ppermute(x, axis, [(i, partner(i)) for i in range(n)])
 
 
 def shards(sources, eigvecs, eigvals, links, damping):
@@ -392,54 +405,58 @@
 
     shape = lambda *dims: jax.ShapeDtypeStruct(dims, f32)
     lat, rest = lax.axis_size("lat"), lax.axis_size(("sub", "src"))
-    links = links.reshape(4 * 18 * slices, zdim, 128)
-    partial, eig, flat_links = call(
+    hbm = lambda x: pltpu.with_memory_space_constraint(x, pltpu.HBM)
+    partial, eig = call(
         functools.partial(correlation_kernel, nev=nev, slices=slices),
-        (
-            shape(lat, 8, 128),
-            jax.ShapeDtypeStruct(eig.shape, eig.dtype),
-            shape(4 * 18 * slices, 128),
-        ),
-        4, 226_000_000, hbm=(0, 1, 2), smem=(3,),
+        (shape(lat, 8, 128), jax.ShapeDtypeStruct(eig.shape, eig.dtype)),
+        3, 226_000_000, hbm=(0, 1), smem=(2,),
         scratch=[
             pltpu.VMEM(src.shape, f32),
-            pltpu.SemaphoreType.DMA((slices + 3,)),
+            pltpu.SemaphoreType.DMA((slices + 2,)),
         ],
-    )(*(pltpu.with_memory_space_constraint(x, pltpu.HBM) for x in (eig, src, links)), damping)
+    )(hbm(eig), hbm(src), damping)
     partial = lax.all_to_all(partial, "lat", 0, 0, tiled=True)
     partial = jnp.broadcast_to(partial.sum(0)[None], (rest, 8, 128))
     partial = lax.all_to_all(partial, ("sub", "src"), 0, 0, tiled=True)
 
     field = shape(slices, comps, 8, 128)
-    halos = (shape(slices, 12, 8, 128),) * 2 + (shape(12, 8, 128),) * 2
+    z_halos = (shape(slices, 12, 8, 128),) * 2
+    t_halos = (shape(12, 8, 128),) * 2
     flat = shape(count * comps * slices, 128)
-    x, rate, *send = call(
+    slab = shape(4 * 18 * slices, 128)
+    x, flat_links, rate, guess, znear, zfar, tnear, tfar = call(
         functools.partial(guess_kernel, nev=nev, slices=slices, norm=norm),
-        (field, shape(8, 128)) + halos, 4, 226_000_000,
-    )(partial, eigvals.reshape(1, nev), eig, flat_links)
-
-    guess = None
+        (field, slab, shape(8, 128), pltpu.VMEM(flat.shape, f32)) + z_halos + t_halos,
+        4, 226_000_000, hbm=(3,),
+        scratch=[pltpu.SemaphoreType.DMA((2,))],
+    )(partial, eigvals.reshape(1, nev), eig, hbm(links.reshape(4 * 18 * slices, zdim, 128)))
+
+    time = ("lat", "sub")
     for sweep in range(ITERS):
         final = sweep == ITERS - 1
-        keep = sweep == 0
-        got = exchange(send)
-        y, *kept = call(
-            functools.partial(local_kernel, slices=slices, keep=keep),
-            (field,) + ((flat,) if keep else ()), 4, 10_000_000,
-            scratch=[pltpu.VMEM((12, 8, 128), f32)],
+        znear = swap(znear, "src", False)
+        zfar = swap(zfar, "src", True)
+        tnear = swap(tnear, time, False)
+        tfar = swap(tfar, time, True)
+        y = call(
+            functools.partial(local_kernel, slices=slices), field, 4,
+            10_000_000, scratch=[pltpu.VMEM((12, 8, 128), f32)],
         )(x, src, flat_links, rate)
-        if keep:
-            guess = kept[0]
-        outs = flat if final else (field,) + halos
+        if not final:
+            next_tnear, next_tfar = call(
+                functools.partial(edge_kernel, slices=slices), t_halos, 5, 1_000_000,
+            )(y, flat_links, rate, znear, zfar)
+        outs = flat if final else (field,) + z_halos
         res = call(
             functools.partial(halo_kernel, slices=slices, final=final),
             outs, 7, 5_000_000,
             scratch=[pltpu.VMEM((2, 12, 8, 128), f32)],
-        )(y, flat_links, rate, *got)
+        )(y, flat_links, rate, znear, zfar, tnear, tfar)
         if final:
             x = res
         else:
-            x, *send = res
+            x, znear, zfar = res
+            tnear, tfar = next_tnear, next_tfar
     return (guess.reshape(sources.shape), x.reshape(sources.shape))
 
 

time: 91.3 us -> 92.2 us (level)
    pallas_call x1, Pallas kernels: 1.09 us -> 2.06 us  [shards(): call(functools.partial(guess_kernel, nev=nev, slices=slices, norm=norm),...]
    pallas_call x2 -> x3, Pallas kernels: 3.3 us -> 2.6 us  [the longest x2 2.48 us: shards(): call(functools.partial(local_kernel, slices=slices), field, 4, 10000000,...]
  transfers between devices with their start and end apart: 8 -> 8, of which waited for: 2 -> 2; matrix products, arithmetic and copies ran while one was open for 0% -> 1% of each run, Pallas kernels for 4% -> 3%
where the time goes in v5:
time: 92.2 us; the launch traced here: 91.8 us
  blocking collectives  39.6 us (43%)
  starting transfers between devices  28.6 us (31%)
  waiting for transfers between devices  12 us (13%)
  Pallas kernels  9.28 us (10%)
  between operations  1.41 us (2%)
    ppermute x8, starting transfers between devices, swap(): return lax.ppermute(x, axis, [(i, partner(i)) for i in range(n)])  28.6 us
    all_to_all x1, blocking collectives, shards(): partial = lax.all_to_all(partial, ('sub', 'src'), 0, 0, tiled=True)  20 us
    all_to_all x1, blocking collectives, shards(): partial = lax.all_to_all(partial, 'lat', 0, 0, tiled=True)  19.6 us
    ppermute x8, waiting for transfers between devices, swap(): return lax.ppermute(x, axis, [(i, partner(i)) for i in range(n)])  12 us
    pallas_call x1, Pallas kernels, shards(): call(functools.partial(correlation_kernel, nev=nev, slices=slices), (shap...  2.83 us
    pallas_call x2, Pallas kernels, shards(): call(functools.partial(local_kernel, slices=slices), field, 4, 10000000,...  2.48 us
    pallas_call x1, Pallas kernels, shards(): call(functools.partial(guess_kernel, nev=nev, slices=slices, norm=norm),...  2.06 us
  transfers between devices with their start and end apart: 8, of which 2 were waited for; matrix products, arithmetic and copies ran while one was open for 1% of the time, Pallas kernels for 3%

profile of v5, /device:TPU:1, one launch (start us, length us, event | category | flops | bytes accessed | tf_op | source)
XLA Modules:
  0.0 91.8 jit_solution(2905116390572918132)
XLA Ops:
  1.3 0.0 copy-start.1
  1.3 2.8 %shard_map.68 = (f32[32,8,128]{2,1,0:T(8,128)S(1)}, bf16[32,6,24,128]{3,2,1,0:T(8,128)(2,1)S(1)}) custom-call(bf16[32,6,24,128]{3,2,1,0:T(8,128)(2,1)} %bitcast.16, f32[1152,128]{1,0:T(8,128)} %bitcast.11, f32[1]{0:T(128)S(6)} %copy.14.damp_ref), custom_call_target="tpu_custom_call" | custom-call | flops 226000000 | bytes 3000000 | tf_op jit(solution)/shard_map/pallas_call | solution.py:409
  4.1 19.6 %all_to_all.10 = f32[32,8,128]{2,1,0:T(8,128)S(1)} all-to-all(f32[32,8,128]{2,1,0:T(8,128)S(1)} %get-tuple-element.17), channel_id=1, replica_groups=mesh['src'=8,'lat'=32,'sub'=2] {'lat'}, dimensions={0} | all-to-all | bytes 262144 | tf_op jit(solution)/shard_map/all_to_all | solution.py:418
  23.8 20.0 %all_to_all.11.part_ref = f32[16,8,128]{2,1,0:T(8,128)S(1)} all-to-all(f32[16,8,128]{2,1,0:T(8,128)S(1)} %broadcast_in_dim.2), channel_id=1, replica_groups=mesh['src'=8,'lat'=32,'sub'=2] {'sub','src'}, dimensions={0} | all-to-all | bytes 131072 | tf_op jit(solution)/shard_map/all_to_all | solution.py:420
  43.8 0.0 copy-done.1
  43.8 0.0 copy-start
  43.8 2.1 %shard_map.69 = (f32[6,24,8,128]{3,2,1,0:T(8,128)S(1)}, f32[432,128]{1,0:T(8,128)S(1)}, f32[8,128]{1,0:T(8,128)S(1)}, f32[1152,128]{1,0:T(8,128)S(1)}, f32[6,12,...) custom-call(f32[16,8,128]{2,1,0:T(8,128)S(1)} %all_to_all.11.part_re, ...), custom_call_target="tpu_custom_call" | custom-call | flops 226000000 | bytes 3000000 | tf_op jit(solution)/shard_map/pallas_call | solution.py:427
  45.9 2.0 %collective-permute-start = (f32[6,12,8,128]{3,2,1,0:T(8,128)S(1)}, f32[6,12,8,128]{3,2,1,0:T(8,128)S(1)}, u32[]{:S(2)}, u32[]{:S(2)}) collective-permute-start(f32[6,12,8,128]{3,2,1,0:T(8,128)S(1)} %get-tuple-element.23), channel_id=1, source_target_pairs={{0,64},{64,0},{128,192},{192,128},{256,320},{320,256},{384,448},{4... | collective-permute-start | bytes 884744 | tf_op jit(solution)/shard_map/ppermute | solution.py:392
  47.9 2.4 %collective-permute-start.1 = (f32[6,12,8,128]{3,2,1,0:T(8,128)S(1)}, f32[6,12,8,128]{3,2,1,0:T(8,128)S(1)}, u32[]{:S(2)}, u32[]{:S(2)}) collective-permute-start(f32[6,12,8,128]{3,2,1,0:T(8,128)S(1)} %get-tuple-element.24), channel_id=1, source_target_pairs={{0,448},{64,128},{128,64},{192,256},{256,192},{320,384},{384,320},... | collective-permute-start | bytes 884744 | tf_op jit(solution)/shard_map/ppermute | solution.py:392
  50.3 3.4 %collective-permute-start.2 = (f32[12,8,128]{2,1,0:T(8,128)S(1)}, f32[12,8,128]{2,1,0:T(8,128)S(1)}, u32[]{:S(2)}, u32[]{:S(2)}) collective-permute-start(f32[12,8,128]{2,1,0:T(8,128)S(1)} %get-tuple-element.25), channel_id=1, source_target_pairs={{0,1},{1,0},{2,3},{3,2},{4,5},{5,4},{6,7},{7,6},{8,9},{9,8},{10,11... | collective-permute-start | bytes 147464 | tf_op jit(solution)/shard_map/ppermute | solution.py:392
  53.7 6.2 %collective-permute-start.3 = (f32[12,8,128]{2,1,0:T(8,128)S(1)}, f32[12,8,128]{2,1,0:T(8,128)S(1)}, u32[]{:S(2)}, u32[]{:S(2)}) collective-permute-start(f32[12,8,128]{2,1,0:T(8,128)S(1)} %get-tuple-element.26), channel_id=1, source_target_pairs={{0,63},{1,2},{2,1},{3,4},{4,3},{5,6},{6,5},{7,8},{8,7},{9,10},{10,... | collective-permute-start | bytes 147464 | tf_op jit(solution)/shard_map/ppermute | solution.py:392
  59.9 0.0 copy-done
  59.9 1.2 %shard_map.70.y_ref = f32[6,24,8,128]{3,2,1,0:T(8,128)S(1)} custom-call(f32[6,24,8,128]{3,2,1,0:T(8,128)S(1)} %get-tuple-element.20.x_ref, f32[1152,128]{1,0:T(8,128)S(1)} %bitcast.12, f32[432,128]{1,0:T(8,128)S(1)} %get-tuple-element.21.links_ref, f32[8,128]{1,0:T(8,128)S(1)} %get-tuple-element.22.rate_ref), custom_call_target="tpu_custom_call" | custom-call | flops 10000000 | bytes 3000000 | tf_op jit(solution)/shard_map/pallas_call | solution.py:441
  61.2 0.0 collective-permute-done.2.tnear_ref
  61.2 5.9 %collective-permute-done.3.tfar_ref = f32[12,8,128]{2,1,0:T(8,128)S(1)} collective-permute-done((f32[12,8,128]{2,1,0:T(8,128)S(1)}, f32[12,8,128]{2,1,0:T(8,128)S(1)}, u32[]{:S(2)}, u32[]{:S(2)}) %collective-permute-start.3) | collective-permute-done | bytes 49184 | tf_op jit(solution)/shard_map/ppermute | solution.py:392
  67.1 0.0 collective-permute-done.znear_ref
  67.1 0.0 collective-permute-done.1.zfar_ref
  67.1 0.5 shard_map.71
  67.6 4.6 %collective-permute-start.4 = (f32[6,12,8,128]{3,2,1,0:T(8,128)S(1)}, f32[6,12,8,128]{3,2,1,0:T(8,128)S(1)}, u32[]{:S(2)}, u32[]{:S(2)}) collective-permute-start(f32[6,12,8,128]{3,2,1,0:T(8,128)S(1)} %get-tuple-element.28), channel_id=1, source_target_pairs={{0,64},{64,0},{128,192},{192,128},{256,320},{320,256},{384,448},{4... | collective-permute-start | bytes 884744 | tf_op jit(solution)/shard_map/ppermute | solution.py:392
  72.2 1.9 %collective-permute-start.5 = (f32[6,12,8,128]{3,2,1,0:T(8,128)S(1)}, f32[6,12,8,128]{3,2,1,0:T(8,128)S(1)}, u32[]{:S(2)}, u32[]{:S(2)}) collective-permute-start(f32[6,12,8,128]{3,2,1,0:T(8,128)S(1)} %get-tuple-element.29), channel_id=1, source_target_pairs={{0,448},{64,128},{128,64},{192,256},{256,192},{320,384},{384,320},... | collective-permute-start | bytes 884744 | tf_op jit(solution)/shard_map/ppermute | solution.py:392
  74.1 0.1 shard_map.73
  74.2 3.1 %collective-permute-start.6 = (f32[12,8,128]{2,1,0:T(8,128)S(1)}, f32[12,8,128]{2,1,0:T(8,128)S(1)}, u32[]{:S(2)}, u32[]{:S(2)}) collective-permute-start(f32[12,8,128]{2,1,0:T(8,128)S(1)} %get-tuple-element.30), channel_id=1, source_target_pairs={{0,1},{1,0},{2,3},{3,2},{4,5},{5,4},{6,7},{7,6},{8,9},{9,8},{10,11... | collective-permute-start | bytes 147464 | tf_op jit(solution)/shard_map/ppermute | solution.py:392
  77.4 4.9 %collective-permute-start.7 = (f32[12,8,128]{2,1,0:T(8,128)S(1)}, f32[12,8,128]{2,1,0:T(8,128)S(1)}, u32[]{:S(2)}, u32[]{:S(2)}) collective-permute-start(f32[12,8,128]{2,1,0:T(8,128)S(1)} %get-tuple-element.31), channel_id=1, source_target_pairs={{0,63},{1,2},{2,1},{3,4},{4,3},{5,6},{6,5},{7,8},{8,7},{9,10},{10,... | collective-permute-start | bytes 147464 | tf_op jit(solution)/shard_map/ppermute | solution.py:392
  82.3 0.8 copy.13
  83.1 1.2 %shard_map.72.y_ref = f32[6,24,8,128]{3,2,1,0:T(8,128)S(1)} custom-call(f32[6,24,8,128]{3,2,1,0:T(8,128)S(1)} %get-tuple-element.27.x_ref, f32[1152,128]{1,0:T(8,128)S(1)} %bitcast.13, f32[432,128]{1,0:T(8,128)S(1)} %get-tuple-element.21.links_ref, f32[8,128]{1,0:T(8,128)S(1)} %get-tuple-element.22.rate_ref), custom_call_target="tpu_custom_call" | custom-call | flops 10000000 | bytes 3000000 | tf_op jit(solution)/shard_map/pallas_call | solution.py:441
  84.4 0.0 collective-permute-done.6.tnear_ref
  84.4 6.1 %collective-permute-done.7.tfar_ref = f32[12,8,128]{2,1,0:T(8,128)S(1)} collective-permute-done((f32[12,8,128]{2,1,0:T(8,128)S(1)}, f32[12,8,128]{2,1,0:T(8,128)S(1)}, u32[]{:S(2)}, u32[]{:S(2)}) %collective-permute-start.7) | collective-permute-done | bytes 49184 | tf_op jit(solution)/shard_map/ppermute | solution.py:392
  90.5 0.0 collective-permute-done.4.znear_ref
  90.5 0.0 collective-permute-done.5.zfar_ref
  90.5 1.3 %shard_map.74 = f32[1152,128]{1,0:T(8,128)} custom-call(f32[6,24,8,128]{3,2,1,0:T(8,128)S(1)} %shard_map.72.y_ref, f32[432,128]{1,0:T(8,128)S(1)} %get-tuple-element.21.links_ref, f32[8,128]{1,0:T(8,128)S(1)} %get-tuple-element.22.rate_ref, f32[6,12,8,128]{3,2,1,0:T(8,128)S(1)} %collective-permute-done.4.znear_ref, ...), custom_call_target="tpu_custom_call" | custom-call | flops 5000000 | bytes 3000000 | tf_op jit(solution)/shard_map/pallas_call | solution.py:450
  (2 shorter events, 0.0 us)
Async XLA Ops:
  1.3 42.5 %copy-start.1 = (f32[32]{0:T(128)S(1)}, f32[32]{0:T(128)}, u32[]{:S(2)}) copy-start(f32[32]{0:T(128)} %param.7) | copy-start | bytes 388
  43.8 16.1 %copy-start = (f32[8,24,6,1,128]{4,3,2,1,0:T(1,128)S(1)}, f32[8,24,6,1,128]{4,3,2,1,0:T(1,128)}, u32[]{:S(2)}) copy-start(f32[8,24,6,1,128]{4,3,2,1,0:T(1,128)} %param.5) | copy-start | bytes 1769476
  45.9 21.2 %collective-permute-start = (f32[6,12,8,128]{3,2,1,0:T(8,128)S(1)}, f32[6,12,8,128]{3,2,1,0:T(8,128)S(1)}, u32[]{:S(2)}, u32[]{:S(2)}) collective-permute-start(f32[6,12,8,128]{3,2,1,0:T(8,128)S(1)} %get-tuple-element.23), channel_id=1, source_target_pairs={{0,64},{64,0},{128,192},{192,128},{256,320},{320,256},{384,448},{4... | collective-permute-start | bytes 884744 | tf_op jit(solution)/shard_map/ppermute | solution.py:392
  47.9 19.2 %collective-permute-start.1 = (f32[6,12,8,128]{3,2,1,0:T(8,128)S(1)}, f32[6,12,8,128]{3,2,1,0:T(8,128)S(1)}, u32[]{:S(2)}, u32[]{:S(2)}) collective-permute-start(f32[6,12,8,128]{3,2,1,0:T(8,128)S(1)} %get-tuple-element.24), channel_id=1, source_target_pairs={{0,448},{64,128},{128,64},{192,256},{256,192},{320,384},{384,320},... | collective-permute-start | bytes 884744 | tf_op jit(solution)/shard_map/ppermute | solution.py:392
  50.3 10.9 %collective-permute-start.2 = (f32[12,8,128]{2,1,0:T(8,128)S(1)}, f32[12,8,128]{2,1,0:T(8,128)S(1)}, u32[]{:S(2)}, u32[]{:S(2)}) collective-permute-start(f32[12,8,128]{2,1,0:T(8,128)S(1)} %get-tuple-element.25), channel_id=1, source_target_pairs={{0,1},{1,0},{2,3},{3,2},{4,5},{5,4},{6,7},{7,6},{8,9},{9,8},{10,11... | collective-permute-start | bytes 147464 | tf_op jit(solution)/shard_map/ppermute | solution.py:392
  53.7 13.4 %collective-permute-start.3 = (f32[12,8,128]{2,1,0:T(8,128)S(1)}, f32[12,8,128]{2,1,0:T(8,128)S(1)}, u32[]{:S(2)}, u32[]{:S(2)}) collective-permute-start(f32[12,8,128]{2,1,0:T(8,128)S(1)} %get-tuple-element.26), channel_id=1, source_target_pairs={{0,63},{1,2},{2,1},{3,4},{4,3},{5,6},{6,5},{7,8},{8,7},{9,10},{10,... | collective-permute-start | bytes 147464 | tf_op jit(solution)/shard_map/ppermute | solution.py:392
  67.6 22.9 %collective-permute-start.4 = (f32[6,12,8,128]{3,2,1,0:T(8,128)S(1)}, f32[6,12,8,128]{3,2,1,0:T(8,128)S(1)}, u32[]{:S(2)}, u32[]{:S(2)}) collective-permute-start(f32[6,12,8,128]{3,2,1,0:T(8,128)S(1)} %get-tuple-element.28), channel_id=1, source_target_pairs={{0,64},{64,0},{128,192},{192,128},{256,320},{320,256},{384,448},{4... | collective-permute-start | bytes 884744 | tf_op jit(solution)/shard_map/ppermute | solution.py:392
  72.2 18.4 %collective-permute-start.5 = (f32[6,12,8,128]{3,2,1,0:T(8,128)S(1)}, f32[6,12,8,128]{3,2,1,0:T(8,128)S(1)}, u32[]{:S(2)}, u32[]{:S(2)}) collective-permute-start(f32[6,12,8,128]{3,2,1,0:T(8,128)S(1)} %get-tuple-element.29), channel_id=1, source_target_pairs={{0,448},{64,128},{128,64},{192,256},{256,192},{320,384},{384,320},... | collective-permute-start | bytes 884744 | tf_op jit(solution)/shard_map/ppermute | solution.py:392
  74.2 10.2 %collective-permute-start.6 = (f32[12,8,128]{2,1,0:T(8,128)S(1)}, f32[12,8,128]{2,1,0:T(8,128)S(1)}, u32[]{:S(2)}, u32[]{:S(2)}) collective-permute-start(f32[12,8,128]{2,1,0:T(8,128)S(1)} %get-tuple-element.30), channel_id=1, source_target_pairs={{0,1},{1,0},{2,3},{3,2},{4,5},{5,4},{6,7},{7,6},{8,9},{9,8},{10,11... | collective-permute-start | bytes 147464 | tf_op jit(solution)/shard_map/ppermute | solution.py:392
  77.4 13.1 %collective-permute-start.7 = (f32[12,8,128]{2,1,0:T(8,128)S(1)}, f32[12,8,128]{2,1,0:T(8,128)S(1)}, u32[]{:S(2)}, u32[]{:S(2)}) collective-permute-start(f32[12,8,128]{2,1,0:T(8,128)S(1)} %get-tuple-element.31), channel_id=1, source_target_pairs={{0,63},{1,2},{2,1},{3,4},{4,3},{5,6},{6,5},{7,8},{8,7},{9,10},{10,... | collective-permute-start | bytes 147464 | tf_op jit(solution)/shard_map/ppermute | solution.py:392

commit v6 on v5

--- a/solution.py
+++ b/solution.py
@@ -128,7 +128,7 @@
 
 
 def correlation_kernel(
-    eig_hbm, src_hbm, damp_ref, out_ref, eig_ref, src_ref, sems, *, nev, slices
+    eig_hbm, src_hbm, links_hbm, damp_ref, out_ref, eig_ref, links_ref, src_ref, sems, *, nev, slices
 ):
     comps = 24
     sources = 8
@@ -142,7 +142,10 @@
     eig_copies = [
         pltpu.make_async_copy(eig_hbm.at[:, t], eig_ref.at[:, t], sems.at[t]) for t in range(slices)
     ]
-    for copy in src_copies + eig_copies:
+    links_copy = pltpu.make_async_copy(
+        links_hbm.at[:, lax.axis_index("src")], links_ref, sems.at[slices + 2]
+    )
+    for copy in src_copies + eig_copies + [links_copy]:
         copy.start()
     for copy in src_copies:
         copy.wait()
@@ -166,17 +169,18 @@
     crossed = jnp.where(gap == 12, full, 0.0) - jnp.where(gap == -12, full, 0.0)
     straight = straight.reshape(sources, comps, nev * comps).sum(1)
     crossed = crossed.reshape(sources, comps, nev * comps).sum(1)
+    both = jnp.concatenate([straight, crossed], axis=0)
+    high = both.astype(jnp.bfloat16)
+    middle = (both - high.astype(jnp.float32)).astype(jnp.bfloat16)
+    low = (both - high.astype(jnp.float32) - middle.astype(jnp.float32)).astype(jnp.bfloat16)
+    parts = jnp.concatenate([high, middle, low], axis=0)
     first = lax.broadcasted_iota(jnp.int32, (nev * comps, 128), 0)
-    lane = lax.broadcasted_iota(jnp.int32, (nev * comps, 128), 1)
-
-    def gather(which):
-        start = (lane - which * nev) * comps
-        return jnp.where((first >= start) & (first < start + comps), 1.0, 0.0)
-
-    dot = functools.partial(
-        jnp.dot, precision=lax.Precision.HIGHEST, preferred_element_type=jnp.float32
-    )
-    total = dot(straight, gather(0)) + dot(crossed, gather(1))
+    start = lax.broadcasted_iota(jnp.int32, (nev * comps, 128), 1) * comps
+    gather = jnp.where((first >= start) & (first < start + comps), 1.0, 0.0).astype(jnp.bfloat16)
+    sums = jnp.dot(parts, gather, preferred_element_type=jnp.float32)
+    sums = (sums[0:16] + sums[16:32]) + sums[32:48]
+    total = sums[0:8] + pltpu.roll(sums[8:16], nev, 1)
+    links_copy.wait()
     holder = (lax.axis_index("lat") == 0) & (lax.axis_index("sub") == 0)
     value = jnp.where(holder, damp_ref[0], 0.0)
     at_row = lax.broadcasted_iota(jnp.int32, (8, 128), 0) == lax.axis_index("src")
@@ -229,20 +233,11 @@
 
 
 def guess_kernel(
-    part_ref, ev_ref, eig_ref, links_hbm,
-    x_ref, links_ref, rate_ref, guess_ref, znear_ref, zfar_ref, tnear_ref, tfar_ref, sems,
+    part_ref, ev_ref, eig_ref, links_ref,
+    x_ref, rate_ref, guess_ref, znear_ref, zfar_ref, tnear_ref, tfar_ref,
     *, nev, slices, norm,
 ):
     comps = 24
-    copies = []
-    for i, first in enumerate((2, 0)):
-        rows = pl.ds(first * 18 * slices, 2 * 18 * slices)
-        copies.append(
-            pltpu.make_async_copy(
-                links_hbm.at[rows, lax.axis_index("src")], links_ref.at[rows], sems.at[i]
-            )
-        )
-        copies[-1].start()
     total = part_ref[0]
     for i in range(1, part_ref.shape[0]):
         total = total + part_ref[i]
@@ -266,7 +261,6 @@
             mix, eig_ref[:, t].reshape(nev * comps, 128), preferred_element_type=jnp.float32
         )
         x_ref[t] = res.reshape(comps, 8, 128)
-    copies[0].wait()
 
     def step(t, carry):
         for c in range(comps):
@@ -280,7 +274,6 @@
     lax.fori_loop(0, slices, step, 0)
     load = lambda t: lambda p, s, c: x_ref[t, 12 * p + 3 * s + c]
     emit_time_halos(load(slices - 1), load(0), links_ref, tnear_ref, tfar_ref, slices)
-    copies[1].wait()
 
 
 def local_kernel(x_ref, src_ref, links_ref, rate_ref, y_ref, behind_ref, *, slices):
@@ -406,15 +399,16 @@
     shape = lambda *dims: jax.ShapeDtypeStruct(dims, f32)
     lat, rest = lax.axis_size("lat"), lax.axis_size(("sub", "src"))
     hbm = lambda x: pltpu.with_memory_space_constraint(x, pltpu.HBM)
-    partial, eig = call(
+    slab = shape(4 * 18 * slices, 128)
+    partial, eig, flat_links = call(
         functools.partial(correlation_kernel, nev=nev, slices=slices),
-        (shape(lat, 8, 128), jax.ShapeDtypeStruct(eig.shape, eig.dtype)),
-        3, 226_000_000, hbm=(0, 1), smem=(2,),
+        (shape(lat, 8, 128), jax.ShapeDtypeStruct(eig.shape, eig.dtype), slab),
+        4, 226_000_000, hbm=(0, 1, 2), smem=(3,),
         scratch=[
             pltpu.VMEM(src.shape, f32),
-            pltpu.SemaphoreType.DMA((slices + 2,)),
+            pltpu.SemaphoreType.DMA((slices + 3,)),
         ],
-    )(hbm(eig), hbm(src), damping)
+    )(hbm(eig), hbm(src), hbm(links.reshape(4 * 18 * slices, zdim, 128)), damping)
     partial = lax.all_to_all(partial, "lat", 0, 0, tiled=True)
     partial = jnp.broadcast_to(partial.sum(0)[None], (rest, 8, 128))
     partial = lax.all_to_all(partial, ("sub", "src"), 0, 0, tiled=True)
@@ -423,13 +417,11 @@
     z_halos = (shape(slices, 12, 8, 128),) * 2
     t_halos = (shape(12, 8, 128),) * 2
     flat = shape(count * comps * slices, 128)
-    slab = shape(4 * 18 * slices, 128)
-    x, flat_links, rate, guess, znear, zfar, tnear, tfar = call(
+    x, rate, guess, znear, zfar, tnear, tfar = call(
         functools.partial(guess_kernel, nev=nev, slices=slices, norm=norm),
-        (field, slab, shape(8, 128), pltpu.VMEM(flat.shape, f32)) + z_halos + t_halos,
-        4, 226_000_000, hbm=(3,),
-        scratch=[pltpu.SemaphoreType.DMA((2,))],
-    )(partial, eigvals.reshape(1, nev), eig, hbm(links.reshape(4 * 18 * slices, zdim, 128)))
+        (field, shape(8, 128), pltpu.VMEM(flat.shape, f32)) + z_halos + t_halos,
+        4, 226_000_000,
+    )(partial, eigvals.reshape(1, nev), eig, flat_links)
 
     time = ("lat", "sub")
     for sweep in range(ITERS):

time: 92.2 us -> 91.2 us (0.989)
  Pallas kernels: 9.28 us -> 8.05 us
where the time goes in v6:
time: 91.2 us; the launch traced here: 90.7 us
  blocking collectives  39.8 us (44%)
  starting transfers between devices  28.6 us (31%)
  waiting for transfers between devices  12 us (13%)
  Pallas kernels  8.05 us (9%)
  between operations  1.42 us (2%)
    ppermute x8, starting transfers between devices, swap(): return lax.ppermute(x, axis, [(i, partner(i)) for i in range(n)])  28.6 us
    all_to_all x1, blocking collectives, shards(): partial = lax.all_to_all(partial, ('sub', 'src'), 0, 0, tiled=True)  20 us
    all_to_all x1, blocking collectives, shards(): partial = lax.all_to_all(partial, 'lat', 0, 0, tiled=True)  19.8 us
    ppermute x8, waiting for transfers between devices, swap(): return lax.ppermute(x, axis, [(i, partner(i)) for i in range(n)])  12 us
    pallas_call x2, Pallas kernels, shards(): call(functools.partial(local_kernel, slices=slices), field, 4, 10000000,...  2.48 us
    pallas_call x1, Pallas kernels, shards(): call(functools.partial(correlation_kernel, nev=nev, slices=slices), (shap...  2.46 us
  transfers between devices with their start and end apart: 8, of which 2 were waited for; matrix products, arithmetic and copies ran while one was open for 1% of the time, Pallas kernels for 3%

profile of v6, /device:TPU:1, one launch (start us, length us, event | category | flops | bytes accessed | tf_op | source)
XLA Modules:
  0.0 90.7 jit_solution(4453575626084529241)
XLA Ops:
  1.3 0.0 copy-start.1
  1.3 2.5 %shard_map.68 = (f32[32,8,128]{2,1,0:T(8,128)S(1)}, bf16[32,6,24,128]{3,2,1,0:T(8,128)(2,1)S(1)}, f32[432,128]{1,0:T(8,128)S(1)}) custom-call(bf16[32,6,24,128]{3,2,1,0:T(8,128)(2,1)} %bitcast.16, f32[1152,128]{1,0:T(8,128)} %bitcast.11, f32[432,8,128]{2,1,0:T(8,128)} %bitcast.15, f32[1]{0:T(128)S(6)} %copy.14.damp_ref), custom_call_target="tpu_custom_call" | custom-call | flops 226000000 | bytes 3000000 | tf_op jit(solution)/shard_map/pallas_call | solution.py:403
  3.8 0.0 copy-start
  3.8 19.8 %all_to_all.10 = f32[32,8,128]{2,1,0:T(8,128)S(1)} all-to-all(f32[32,8,128]{2,1,0:T(8,128)S(1)} %get-tuple-element.17), channel_id=1, replica_groups=mesh['src'=8,'lat'=32,'sub'=2] {'lat'}, dimensions={0} | all-to-all | bytes 262144 | tf_op jit(solution)/shard_map/all_to_all | solution.py:412
  23.6 20.0 %all_to_all.11.part_ref = f32[16,8,128]{2,1,0:T(8,128)S(1)} all-to-all(f32[16,8,128]{2,1,0:T(8,128)S(1)} %broadcast_in_dim.2), channel_id=1, replica_groups=mesh['src'=8,'lat'=32,'sub'=2] {'sub','src'}, dimensions={0} | all-to-all | bytes 131072 | tf_op jit(solution)/shard_map/all_to_all | solution.py:414
  43.6 0.0 copy-done.1
  43.6 1.2 %shard_map.69 = (f32[6,24,8,128]{3,2,1,0:T(8,128)S(1)}, f32[8,128]{1,0:T(8,128)S(1)}, f32[1152,128]{1,0:T(8,128)S(1)}, f32[6,12,8,128]{3,2,1,0:T(8,128)S(1)}, f3...) custom-call(f32[16,8,128]{2,1,0:T(8,128)S(1)} %all_to_all.11.part_ref, ...), custom_call_target="tpu_custom_call" | custom-call | flops 226000000 | bytes 3000000 | tf_op jit(solution)/shard_map/pallas_call | solution.py:420
  44.8 2.0 %collective-permute-start = (f32[6,12,8,128]{3,2,1,0:T(8,128)S(1)}, f32[6,12,8,128]{3,2,1,0:T(8,128)S(1)}, u32[]{:S(2)}, u32[]{:S(2)}) collective-permute-start(f32[6,12,8,128]{3,2,1,0:T(8,128)S(1)} %get-tuple-element.23), channel_id=1, source_target_pairs={{0,64},{64,0},{128,192},{192,128},{256,320},{320,256},{384,448},{4... | collective-permute-start | bytes 884744 | tf_op jit(solution)/shard_map/ppermute | solution.py:385
  46.8 2.4 %collective-permute-start.1 = (f32[6,12,8,128]{3,2,1,0:T(8,128)S(1)}, f32[6,12,8,128]{3,2,1,0:T(8,128)S(1)}, u32[]{:S(2)}, u32[]{:S(2)}) collective-permute-start(f32[6,12,8,128]{3,2,1,0:T(8,128)S(1)} %get-tuple-element.24), channel_id=1, source_target_pairs={{0,448},{64,128},{128,64},{192,256},{256,192},{320,384},{384,320},... | collective-permute-start | bytes 884744 | tf_op jit(solution)/shard_map/ppermute | solution.py:385
  49.2 3.4 %collective-permute-start.2 = (f32[12,8,128]{2,1,0:T(8,128)S(1)}, f32[12,8,128]{2,1,0:T(8,128)S(1)}, u32[]{:S(2)}, u32[]{:S(2)}) collective-permute-start(f32[12,8,128]{2,1,0:T(8,128)S(1)} %get-tuple-element.25), channel_id=1, source_target_pairs={{0,1},{1,0},{2,3},{3,2},{4,5},{5,4},{6,7},{7,6},{8,9},{9,8},{10,11... | collective-permute-start | bytes 147464 | tf_op jit(solution)/shard_map/ppermute | solution.py:385
  52.6 6.2 %collective-permute-start.3 = (f32[12,8,128]{2,1,0:T(8,128)S(1)}, f32[12,8,128]{2,1,0:T(8,128)S(1)}, u32[]{:S(2)}, u32[]{:S(2)}) collective-permute-start(f32[12,8,128]{2,1,0:T(8,128)S(1)} %get-tuple-element.26), channel_id=1, source_target_pairs={{0,63},{1,2},{2,1},{3,4},{4,3},{5,6},{6,5},{7,8},{8,7},{9,10},{10,... | collective-permute-start | bytes 147464 | tf_op jit(solution)/shard_map/ppermute | solution.py:385
  58.8 0.0 copy-done
  58.9 1.2 %shard_map.70.y_ref = f32[6,24,8,128]{3,2,1,0:T(8,128)S(1)} custom-call(f32[6,24,8,128]{3,2,1,0:T(8,128)S(1)} %get-tuple-element.21.x_ref, f32[1152,128]{1,0:T(8,128)S(1)} %bitcast.12, f32[432,128]{1,0:T(8,128)S(1)} %get-tuple-element.19.links_ref, f32[8,128]{1,0:T(8,128)S(1)} %get-tuple-element.22.rate_ref), custom_call_target="tpu_custom_call" | custom-call | flops 10000000 | bytes 3000000 | tf_op jit(solution)/shard_map/pallas_call | solution.py:433
  60.1 0.0 collective-permute-done.2.tnear_ref
  60.1 5.9 %collective-permute-done.3.tfar_ref = f32[12,8,128]{2,1,0:T(8,128)S(1)} collective-permute-done((f32[12,8,128]{2,1,0:T(8,128)S(1)}, f32[12,8,128]{2,1,0:T(8,128)S(1)}, u32[]{:S(2)}, u32[]{:S(2)}) %collective-permute-start.3) | collective-permute-done | bytes 49184 | tf_op jit(solution)/shard_map/ppermute | solution.py:385
  66.0 0.0 collective-permute-done.znear_ref
  66.0 0.0 collective-permute-done.1.zfar_ref
  66.0 0.5 shard_map.71
  66.5 4.6 %collective-permute-start.4 = (f32[6,12,8,128]{3,2,1,0:T(8,128)S(1)}, f32[6,12,8,128]{3,2,1,0:T(8,128)S(1)}, u32[]{:S(2)}, u32[]{:S(2)}) collective-permute-start(f32[6,12,8,128]{3,2,1,0:T(8,128)S(1)} %get-tuple-element.28), channel_id=1, source_target_pairs={{0,64},{64,0},{128,192},{192,128},{256,320},{320,256},{384,448},{4... | collective-permute-start | bytes 884744 | tf_op jit(solution)/shard_map/ppermute | solution.py:385
  71.1 1.9 %collective-permute-start.5 = (f32[6,12,8,128]{3,2,1,0:T(8,128)S(1)}, f32[6,12,8,128]{3,2,1,0:T(8,128)S(1)}, u32[]{:S(2)}, u32[]{:S(2)}) collective-permute-start(f32[6,12,8,128]{3,2,1,0:T(8,128)S(1)} %get-tuple-element.29), channel_id=1, source_target_pairs={{0,448},{64,128},{128,64},{192,256},{256,192},{320,384},{384,320},... | collective-permute-start | bytes 884744 | tf_op jit(solution)/shard_map/ppermute | solution.py:385
  73.0 0.1 shard_map.73
  73.2 3.1 %collective-permute-start.6 = (f32[12,8,128]{2,1,0:T(8,128)S(1)}, f32[12,8,128]{2,1,0:T(8,128)S(1)}, u32[]{:S(2)}, u32[]{:S(2)}) collective-permute-start(f32[12,8,128]{2,1,0:T(8,128)S(1)} %get-tuple-element.30), channel_id=1, source_target_pairs={{0,1},{1,0},{2,3},{3,2},{4,5},{5,4},{6,7},{7,6},{8,9},{9,8},{10,11... | collective-permute-start | bytes 147464 | tf_op jit(solution)/shard_map/ppermute | solution.py:385
  76.3 4.9 %collective-permute-start.7 = (f32[12,8,128]{2,1,0:T(8,128)S(1)}, f32[12,8,128]{2,1,0:T(8,128)S(1)}, u32[]{:S(2)}, u32[]{:S(2)}) collective-permute-start(f32[12,8,128]{2,1,0:T(8,128)S(1)} %get-tuple-element.31), channel_id=1, source_target_pairs={{0,63},{1,2},{2,1},{3,4},{4,3},{5,6},{6,5},{7,8},{8,7},{9,10},{10,... | collective-permute-start | bytes 147464 | tf_op jit(solution)/shard_map/ppermute | solution.py:385
  81.2 0.8 copy.13
  82.1 1.2 %shard_map.72.y_ref = f32[6,24,8,128]{3,2,1,0:T(8,128)S(1)} custom-call(f32[6,24,8,128]{3,2,1,0:T(8,128)S(1)} %get-tuple-element.27.x_ref, f32[1152,128]{1,0:T(8,128)S(1)} %bitcast.13, f32[432,128]{1,0:T(8,128)S(1)} %get-tuple-element.19.links_ref, f32[8,128]{1,0:T(8,128)S(1)} %get-tuple-element.22.rate_ref), custom_call_target="tpu_custom_call" | custom-call | flops 10000000 | bytes 3000000 | tf_op jit(solution)/shard_map/pallas_call | solution.py:433
  83.3 0.0 collective-permute-done.6.tnear_ref
  83.3 6.2 %collective-permute-done.7.tfar_ref = f32[12,8,128]{2,1,0:T(8,128)S(1)} collective-permute-done((f32[12,8,128]{2,1,0:T(8,128)S(1)}, f32[12,8,128]{2,1,0:T(8,128)S(1)}, u32[]{:S(2)}, u32[]{:S(2)}) %collective-permute-start.7) | collective-permute-done | bytes 49184 | tf_op jit(solution)/shard_map/ppermute | solution.py:385
  89.5 0.0 collective-permute-done.4.znear_ref
  89.5 0.0 collective-permute-done.5.zfar_ref
  89.5 1.3 %shard_map.74 = f32[1152,128]{1,0:T(8,128)} custom-call(f32[6,24,8,128]{3,2,1,0:T(8,128)S(1)} %shard_map.72.y_ref, f32[432,128]{1,0:T(8,128)S(1)} %get-tuple-element.19.links_ref, f32[8,128]{1,0:T(8,128)S(1)} %get-tuple-element.22.rate_ref, f32[6,12,8,128]{3,2,1,0:T(8,128)S(1)} %collective-permute-done.4.znear_ref, ...), custom_call_target="tpu_custom_call" | custom-call | flops 5000000 | bytes 3000000 | tf_op jit(solution)/shard_map/pallas_call | solution.py:442
  (2 shorter events, 0.0 us)
Async XLA Ops:
  1.3 42.3 %copy-start.1 = (f32[32]{0:T(128)S(1)}, f32[32]{0:T(128)}, u32[]{:S(2)}) copy-start(f32[32]{0:T(128)} %param.7) | copy-start | bytes 388
  3.8 55.1 %copy-start = (f32[8,24,6,1,128]{4,3,2,1,0:T(1,128)S(1)}, f32[8,24,6,1,128]{4,3,2,1,0:T(1,128)}, u32[]{:S(2)}) copy-start(f32[8,24,6,1,128]{4,3,2,1,0:T(1,128)} %param.5) | copy-start | bytes 1769476
  44.8 21.2 %collective-permute-start = (f32[6,12,8,128]{3,2,1,0:T(8,128)S(1)}, f32[6,12,8,128]{3,2,1,0:T(8,128)S(1)}, u32[]{:S(2)}, u32[]{:S(2)}) collective-permute-start(f32[6,12,8,128]{3,2,1,0:T(8,128)S(1)} %get-tuple-element.23), channel_id=1, source_target_pairs={{0,64},{64,0},{128,192},{192,128},{256,320},{320,256},{384,448},{4... | collective-permute-start | bytes 884744 | tf_op jit(solution)/shard_map/ppermute | solution.py:385
  46.8 19.2 %collective-permute-start.1 = (f32[6,12,8,128]{3,2,1,0:T(8,128)S(1)}, f32[6,12,8,128]{3,2,1,0:T(8,128)S(1)}, u32[]{:S(2)}, u32[]{:S(2)}) collective-permute-start(f32[6,12,8,128]{3,2,1,0:T(8,128)S(1)} %get-tuple-element.24), channel_id=1, source_target_pairs={{0,448},{64,128},{128,64},{192,256},{256,192},{320,384},{384,320},... | collective-permute-start | bytes 884744 | tf_op jit(solution)/shard_map/ppermute | solution.py:385
  49.2 10.9 %collective-permute-start.2 = (f32[12,8,128]{2,1,0:T(8,128)S(1)}, f32[12,8,128]{2,1,0:T(8,128)S(1)}, u32[]{:S(2)}, u32[]{:S(2)}) collective-permute-start(f32[12,8,128]{2,1,0:T(8,128)S(1)} %get-tuple-element.25), channel_id=1, source_target_pairs={{0,1},{1,0},{2,3},{3,2},{4,5},{5,4},{6,7},{7,6},{8,9},{9,8},{10,11... | collective-permute-start | bytes 147464 | tf_op jit(solution)/shard_map/ppermute | solution.py:385
  52.6 13.4 %collective-permute-start.3 = (f32[12,8,128]{2,1,0:T(8,128)S(1)}, f32[12,8,128]{2,1,0:T(8,128)S(1)}, u32[]{:S(2)}, u32[]{:S(2)}) collective-permute-start(f32[12,8,128]{2,1,0:T(8,128)S(1)} %get-tuple-element.26), channel_id=1, source_target_pairs={{0,63},{1,2},{2,1},{3,4},{4,3},{5,6},{6,5},{7,8},{8,7},{9,10},{10,... | collective-permute-start | bytes 147464 | tf_op jit(solution)/shard_map/ppermute | solution.py:385
  66.5 22.9 %collective-permute-start.4 = (f32[6,12,8,128]{3,2,1,0:T(8,128)S(1)}, f32[6,12,8,128]{3,2,1,0:T(8,128)S(1)}, u32[]{:S(2)}, u32[]{:S(2)}) collective-permute-start(f32[6,12,8,128]{3,2,1,0:T(8,128)S(1)} %get-tuple-element.28), channel_id=1, source_target_pairs={{0,64},{64,0},{128,192},{192,128},{256,320},{320,256},{384,448},{4... | collective-permute-start | bytes 884744 | tf_op jit(solution)/shard_map/ppermute | solution.py:385
  71.1 18.4 %collective-permute-start.5 = (f32[6,12,8,128]{3,2,1,0:T(8,128)S(1)}, f32[6,12,8,128]{3,2,1,0:T(8,128)S(1)}, u32[]{:S(2)}, u32[]{:S(2)}) collective-permute-start(f32[6,12,8,128]{3,2,1,0:T(8,128)S(1)} %get-tuple-element.29), channel_id=1, source_target_pairs={{0,448},{64,128},{128,64},{192,256},{256,192},{320,384},{384,320},... | collective-permute-start | bytes 884744 | tf_op jit(solution)/shard_map/ppermute | solution.py:385
  73.2 10.1 %collective-permute-start.6 = (f32[12,8,128]{2,1,0:T(8,128)S(1)}, f32[12,8,128]{2,1,0:T(8,128)S(1)}, u32[]{:S(2)}, u32[]{:S(2)}) collective-permute-start(f32[12,8,128]{2,1,0:T(8,128)S(1)} %get-tuple-element.30), channel_id=1, source_target_pairs={{0,1},{1,0},{2,3},{3,2},{4,5},{5,4},{6,7},{7,6},{8,9},{9,8},{10,11... | collective-permute-start | bytes 147464 | tf_op jit(solution)/shard_map/ppermute | solution.py:385
  76.3 13.1 %collective-permute-start.7 = (f32[12,8,128]{2,1,0:T(8,128)S(1)}, f32[12,8,128]{2,1,0:T(8,128)S(1)}, u32[]{:S(2)}, u32[]{:S(2)}) collective-permute-start(f32[12,8,128]{2,1,0:T(8,128)S(1)} %get-tuple-element.31), channel_id=1, source_target_pairs={{0,63},{1,2},{2,1},{3,4},{4,3},{5,6},{6,5},{7,8},{8,7},{9,10},{10,... | collective-permute-start | bytes 147464 | tf_op jit(solution)/shard_map/ppermute | solution.py:385

commit v7 on v6

--- a/solution.py
+++ b/solution.py
@@ -9,7 +9,6 @@
 from jax.sharding import PartitionSpec as P
 
 LX = 16
-ITERS = 2
 HOPPING = 0.12
 
 BLOCKS = [
@@ -208,13 +207,14 @@
     return place, lax.rem(place, 2) == 0
 
 
-def emit_halos(load, links_ref, t, near_ref, far_ref, slices):
+def emit_halos(load, links_ref, t, near_ref, far_ref, slices, near_t=None, far_t=None):
     even = z_even()
     up = project(1, 2, load)
     up = colour_mul(load_link(links_ref, slices, 2, t), up, True)
     down = project(-1, 2, load)
-    store_half(lambda i, v: near_ref.__setitem__((t, i), v), choose(even, up, down))
-    store_half(lambda i, v: far_ref.__setitem__((t, i), v), choose(even, down, up))
+    near_t, far_t = (t if place is None else place for place in (near_t, far_t))
+    store_half(lambda i, v: near_ref.__setitem__((near_t, i), v), choose(even, up, down))
+    store_half(lambda i, v: far_ref.__setitem__((far_t, i), v), choose(even, down, up))
 
 
 def emit_time_halos(load_last, load_first, links_ref, near_ref, far_ref, slices):
@@ -308,60 +308,100 @@
     lax.fori_loop(0, slices, step, 0)
 
 
-def z_hops(links_ref, znear_ref, zfar_ref, t, slices):
+def z_hops(links_ref, znear_ref, zfar_ref, t, slices, far_t=None):
     above_near = z_even()
     acc = {}
-    near, far = (load_half(lambda i, ref=ref: ref[t, i]) for ref in (znear_ref, zfar_ref))
+    far_t = t if far_t is None else far_t
+    near = load_half(lambda i: znear_ref[t, i])
+    far = load_half(lambda i: zfar_ref[far_t, i])
     link = load_link(links_ref, slices, 2, t)
     rebuild_into(acc, -1, 2, colour_mul(link, choose(above_near, near, far), False))
     rebuild_into(acc, 1, 2, choose(above_near, far, near))
     return acc
 
 
-def edge_kernel(y_ref, links_ref, rate_ref, znear_ref, zfar_ref, tnear_ref, tfar_ref, *, slices):
+def edge_kernel(
+    y_ref, links_ref, rate_ref, znear_ref, zfar_ref, first_ref, tnear_ref, tfar_ref, *, slices
+):
     rate = rate_ref[...] * HOPPING
 
     def load(t):
         hops = z_hops(links_ref, znear_ref, zfar_ref, t, slices)
         return lambda p, s, c: y_ref[t, 12 * p + 3 * s + c] + rate * hops[(p, s, c)]
 
-    emit_time_halos(load(slices - 1), load(0), links_ref, tnear_ref, tfar_ref, slices)
-
-
-def halo_kernel(
-    y_ref, links_ref, rate_ref, znear_ref, zfar_ref, tnear_ref, tfar_ref, *refs, slices, final
+    tfar_ref[0] = first_ref[...]
+    emit_time_halos(load(slices - 1), load(0), links_ref, tnear_ref, tfar_ref.at[1], slices)
+
+
+def inner_kernel(
+    y_ref, links_ref, rate_ref, znear_ref, zfar_ref, x_ref, near_ref, far_ref, *, slices
 ):
-    _, t_even = t_place()
-    edge_ref = refs[-1]
-    last = slices - 1
-    near, far = (load_half(lambda i, ref=ref: ref[i]) for ref in (tnear_ref, tfar_ref))
-    link = load_link(links_ref, slices, 3, last)
-    above = colour_mul(link, choose(t_even, near, far), False)
-    store_half(lambda i, v: edge_ref.__setitem__((0, i), v), above)
-    store_half(lambda i, v: edge_ref.__setitem__((1, i), v), choose(t_even, far, near))
-
     def step(t, carry):
-        acc = z_hops(links_ref, znear_ref, zfar_ref, t, slices)
-        top, bottom = (jnp.where(t == edge, 1.0, 0.0) for edge in (last, 0))
-        rebuild_into(acc, -1, 3, map_half(lambda v: v * top, load_half(lambda i: edge_ref[0, i])))
-        rebuild_into(acc, 1, 3, map_half(lambda v: v * bottom, load_half(lambda i: edge_ref[1, i])))
         rate = rate_ref[...] * HOPPING
         new = {}
-        for (p, s, c), hop in acc.items():
+        for (p, s, c), hop in z_hops(links_ref, znear_ref, zfar_ref, t, slices).items():
             comp = 12 * p + 3 * s + c
-            value = y_ref[t, comp] + rate * hop
-            new[(p, s, c)] = value
-            if final:
-                refs[0][pl.ds(comp * slices + t, 8, stride=24 * slices), :] = value
-            else:
-                refs[0][t, comp] = value
-        if not final:
-            emit_halos(
-                lambda p, s, c: new[(p, s, c)], links_ref, t, refs[1], refs[2], slices
-            )
+            new[(p, s, c)] = y_ref[t, comp] + rate * hop
+            x_ref[t - 1, comp] = new[(p, s, c)]
+        emit_halos(
+            lambda p, s, c: new[(p, s, c)], links_ref, t, near_ref, far_ref, slices, t - 1, t - 1
+        )
         return carry
 
-    lax.fori_loop(0, slices, step, 0)
+    lax.fori_loop(1, slices - 1, step, 0)
+
+
+def t_hops(links_ref, tnear_ref, tfar_ref, slices):
+    _, even = t_place()
+    near, far = (load_half(lambda i, ref=ref: ref[i]) for ref in (tnear_ref, tfar_ref))
+    first, last = {}, {}
+    rebuild_into(first, 1, 3, choose(even, far, near))
+    link = load_link(links_ref, slices, 3, slices - 1)
+    rebuild_into(last, -1, 3, colour_mul(link, choose(even, near, far), False))
+    return first, last
+
+
+def outer_kernel(
+    y_ref, links_ref, rate_ref, znear_ref, zfar_ref, tnear_ref, tfar_ref, inner_x_ref, inner_near_ref,
+    x_ref, near_ref, far_ref, *, slices,
+):
+    x_ref[1 : slices - 1] = inner_x_ref[...]
+    near_ref[1 : slices - 1] = inner_near_ref[...]
+    rate = rate_ref[...] * HOPPING
+    for i, hops in enumerate(t_hops(links_ref, tnear_ref, tfar_ref.at[0], slices)):
+        t = (slices - 1) * i
+        new = {}
+        for (p, s, c), hop in z_hops(links_ref, znear_ref, zfar_ref, t, slices).items():
+            comp = 12 * p + 3 * s + c
+            new[(p, s, c)] = y_ref[t, comp] + rate * (hop + hops[(p, s, c)])
+            x_ref[t, comp] = new[(p, s, c)]
+        emit_halos(
+            lambda p, s, c: new[(p, s, c)], links_ref, t, near_ref, far_ref, slices, t, i
+        )
+
+
+def last_kernel(
+    y_ref, links_ref, rate_ref, znear_ref, zinner_ref, zouter_ref, tnear_ref, tfar_ref, out_ref, *, slices
+):
+    rate = rate_ref[...] * HOPPING
+
+    def finish(t, hops, more=None):
+        for key, hop in hops.items():
+            p, s, c = key
+            comp = 12 * p + 3 * s + c
+            hop = hop if more is None else hop + more[key]
+            where = pl.ds(comp * slices + t, 8, stride=24 * slices)
+            out_ref[where, :] = y_ref[t, comp] + rate * hop
+
+    for i, more in enumerate(t_hops(links_ref, tnear_ref, tfar_ref.at[1], slices)):
+        t = (slices - 1) * i
+        finish(t, z_hops(links_ref, znear_ref, zouter_ref, t, slices, i), more)
+
+    def step(t, carry):
+        finish(t, z_hops(links_ref, znear_ref, zinner_ref, t, slices, t - 1))
+        return carry
+
+    lax.fori_loop(1, slices - 1, step, 0)
 
 
 def call(kernel, outs, ins, flops, hbm=(), smem=(), scratch=()):
@@ -424,31 +464,39 @@
     )(partial, eigvals.reshape(1, nev), eig, flat_links)
 
     time = ("lat", "sub")
-    for sweep in range(ITERS):
-        final = sweep == ITERS - 1
-        znear = swap(znear, "src", False)
-        zfar = swap(zfar, "src", True)
-        tnear = swap(tnear, time, False)
-        tfar = swap(tfar, time, True)
-        y = call(
-            functools.partial(local_kernel, slices=slices), field, 4,
-            10_000_000, scratch=[pltpu.VMEM((12, 8, 128), f32)],
-        )(x, src, flat_links, rate)
-        if not final:
-            next_tnear, next_tfar = call(
-                functools.partial(edge_kernel, slices=slices), t_halos, 5, 1_000_000,
-            )(y, flat_links, rate, znear, zfar)
-        outs = flat if final else (field,) + z_halos
-        res = call(
-            functools.partial(halo_kernel, slices=slices, final=final),
-            outs, 7, 5_000_000,
-            scratch=[pltpu.VMEM((2, 12, 8, 128), f32)],
-        )(y, flat_links, rate, znear, zfar, tnear, tfar)
-        if final:
-            x = res
-        else:
-            x, znear, zfar = res
-            tnear, tfar = next_tnear, next_tfar
+
+    def stage(kernel, outs, *args, scratch=()):
+        return call(
+            functools.partial(kernel, slices=slices), outs, len(args),
+            5_000_000, scratch=scratch,
+        )(*args)
+
+    carry = [pltpu.VMEM((12, 8, 128), f32)]
+    zfar = swap(zfar, "src", True)
+    znear = swap(znear, "src", False)
+    tnear = swap(tnear, time, False)
+    y = stage(local_kernel, field, x, src, flat_links, rate, scratch=carry)
+    next_tnear, both_tfar = stage(
+        edge_kernel, (shape(12, 8, 128), shape(2, 12, 8, 128)),
+        y, flat_links, rate, znear, zfar, tfar,
+    )
+    both_tfar = swap(both_tfar, time, True)
+    inner = slices - 2
+    inner_x, inner_near, zinner = stage(
+        inner_kernel,
+        (shape(inner, comps, 8, 128), shape(inner, 12, 8, 128), shape(inner, 12, 8, 128)),
+        y, flat_links, rate, znear, zfar,
+    )
+    zinner = swap(zinner, "src", True)
+    next_tnear = swap(next_tnear, time, False)
+    x, znear, zouter = stage(
+        outer_kernel, (field, z_halos[0], shape(2, 12, 8, 128)),
+        y, flat_links, rate, znear, zfar, tnear, both_tfar, inner_x, inner_near,
+    )
+    zouter = swap(zouter, "src", True)
+    znear = swap(znear, "src", False)
+    y = stage(local_kernel, field, x, src, flat_links, rate, scratch=carry)
+    x = stage(last_kernel, flat, y, flat_links, rate, znear, zinner, zouter, next_tnear, both_tfar)
     return (guess.reshape(sources.shape), x.reshape(sources.shape))
 
 

time: 91.2 us -> 93.5 us (1.025)
  the two profiles are of different devices: /device:TPU:1 before, /device:TPU:8 now
where the time goes in v7:
time: 93.5 us; the launch traced here: 93 us
  blocking collectives  37.8 us (40%)
  starting transfers between devices  28.6 us (31%)
  waiting for transfers between devices  16.4 us (18%)
  Pallas kernels  7.93 us (8%)
  between operations  1.43 us (2%)
    ppermute x8, starting transfers between devices, swap(): return lax.ppermute(x, axis, [(i, partner(i)) for i in range(n)])  28.6 us
    all_to_all x1, blocking collectives, shards(): partial = lax.all_to_all(partial, 'lat', 0, 0, tiled=True)  19.8 us
    all_to_all x1, blocking collectives, shards(): partial = lax.all_to_all(partial, ('sub', 'src'), 0, 0, tiled=True)  18 us
    ppermute x8, waiting for transfers between devices, swap(): return lax.ppermute(x, axis, [(i, partner(i)) for i in range(n)])  16.4 us
    pallas_call x6, Pallas kernels, stage(): call(functools.partial(kernel, slices=slices), outs, len(args), 5000000,...  4.27 us
    pallas_call x1, Pallas kernels, shards(): call(functools.partial(correlation_kernel, nev=nev, slices=slices), (shap...  2.46 us
  transfers between devices with their start and end apart: 8, of which 3 were waited for; matrix products, arithmetic and copies ran while one was open for 1% of the time, Pallas kernels for 3%

profile of v7, /device:TPU:8, one launch (start us, length us, event | category | flops | bytes accessed | tf_op | source)
XLA Modules:
  0.0 93.0 jit_solution(27616682079100702)
XLA Ops:
  1.3 0.0 copy-start.1
  1.3 2.5 %shard_map.68 = (f32[32,8,128]{2,1,0:T(8,128)S(1)}, bf16[32,6,24,128]{3,2,1,0:T(8,128)(2,1)S(1)}, f32[432,128]{1,0:T(8,128)S(1)}) custom-call(bf16[32,6,24,128]{3,2,1,0:T(8,128)(2,1)} %bitcast.16, f32[1152,128]{1,0:T(8,128)} %bitcast.11, f32[432,8,128]{2,1,0:T(8,128)} %bitcast.15, f32[1]{0:T(128)S(6)} %copy.14.damp_ref), custom_call_target="tpu_custom_call" | custom-call | flops 226000000 | bytes 3000000 | tf_op jit(solution)/shard_map/pallas_call | solution.py:443
  3.8 0.0 copy-start
  3.8 19.8 %all_to_all.10 = f32[32,8,128]{2,1,0:T(8,128)S(1)} all-to-all(f32[32,8,128]{2,1,0:T(8,128)S(1)} %get-tuple-element.20), channel_id=1, replica_groups=mesh['src'=8,'lat'=32,'sub'=2] {'lat'}, dimensions={0} | all-to-all | bytes 262144 | tf_op jit(solution)/shard_map/all_to_all | solution.py:452
  23.6 18.0 %all_to_all.11.part_ref = f32[16,8,128]{2,1,0:T(8,128)S(1)} all-to-all(f32[16,8,128]{2,1,0:T(8,128)S(1)} %broadcast_in_dim.2), channel_id=1, replica_groups=mesh['src'=8,'lat'=32,'sub'=2] {'sub','src'}, dimensions={0} | all-to-all | bytes 131072 | tf_op jit(solution)/shard_map/all_to_all | solution.py:454
  41.6 0.0 copy-done.1
  41.6 1.2 %shard_map.69 = (f32[6,24,8,128]{3,2,1,0:T(8,128)S(1)}, f32[8,128]{1,0:T(8,128)S(1)}, f32[1152,128]{1,0:T(8,128)S(1)}, f32[6,12,8,128]{3,2,1,0:T(8,128)S(1)}, f3...) custom-call(f32[16,8,128]{2,1,0:T(8,128)S(1)} %all_to_all.11.part_ref, ...), custom_call_target="tpu_custom_call" | custom-call | flops 226000000 | bytes 3000000 | tf_op jit(solution)/shard_map/pallas_call | solution.py:460
  42.8 2.3 %collective-permute-start = (f32[6,12,8,128]{3,2,1,0:T(8,128)S(1)}, f32[6,12,8,128]{3,2,1,0:T(8,128)S(1)}, u32[]{:S(2)}, u32[]{:S(2)}) collective-permute-start(f32[6,12,8,128]{3,2,1,0:T(8,128)S(1)} %get-tuple-element.26), channel_id=1, source_target_pairs={{0,64},{64,0},{128,192},{192,128},{256,320},{320,256},{384,448},{4... | collective-permute-start | bytes 884744 | tf_op jit(solution)/shard_map/ppermute | solution.py:425
  45.1 2.5 %collective-permute-start.1 = (f32[6,12,8,128]{3,2,1,0:T(8,128)S(1)}, f32[6,12,8,128]{3,2,1,0:T(8,128)S(1)}, u32[]{:S(2)}, u32[]{:S(2)}) collective-permute-start(f32[6,12,8,128]{3,2,1,0:T(8,128)S(1)} %get-tuple-element.27), channel_id=1, source_target_pairs={{0,448},{64,128},{128,64},{192,256},{256,192},{320,384},{384,320},... | collective-permute-start | bytes 884744 | tf_op jit(solution)/shard_map/ppermute | solution.py:425
  47.6 0.0 copy-done
  47.6 1.2 %shard_map.70.y_ref = f32[6,24,8,128]{3,2,1,0:T(8,128)S(1)} custom-call(f32[6,24,8,128]{3,2,1,0:T(8,128)S(1)} %get-tuple-element.24.x_ref, f32[1152,128]{1,0:T(8,128)S(1)} %bitcast.12, f32[432,128]{1,0:T(8,128)S(1)} %get-tuple-element.22.links_ref, f32[8,128]{1,0:T(8,128)S(1)} %get-tuple-element.25.rate_ref), custom_call_target="tpu_custom_call" | custom-call | flops 5000000 | bytes 3000000 | tf_op jit(solution)/shard_map/pallas_call | solution.py:469
  48.9 0.0 collective-permute-done.znear_ref
  48.9 7.9 %collective-permute-done.1.zfar_ref = f32[6,12,8,128]{3,2,1,0:T(8,128)S(1)} collective-permute-done((f32[6,12,8,128]{3,2,1,0:T(8,128)S(1)}, f32[6,12,8,128]{3,2,1,0:T(8,128)S(1)}, u32[]{:S(2)}, u32[]{:S(2)}) %collective-permute-start.1) | collective-permute-done | bytes 294944 | tf_op jit(solution)/shard_map/ppermute | solution.py:425
  56.8 0.1 shard_map.71
  56.9 5.1 %collective-permute-start.3 = (f32[2,12,8,128]{3,2,1,0:T(8,128)S(1)}, f32[2,12,8,128]{3,2,1,0:T(8,128)S(1)}, u32[]{:S(2)}, u32[]{:S(2)}) collective-permute-start(f32[2,12,8,128]{3,2,1,0:T(8,128)S(1)} %get-tuple-element.30), channel_id=1, source_target_pairs={{0,63},{1,2},{2,1},{3,4},{4,3},{5,6},{6,5},{7,8},{8,7},{9,10},{10,... | collective-permute-start | bytes 294920 | tf_op jit(solution)/shard_map/ppermute | solution.py:425
  62.1 4.6 %collective-permute-start.2 = (f32[12,8,128]{2,1,0:T(8,128)S(1)}, f32[12,8,128]{2,1,0:T(8,128)S(1)}, u32[]{:S(2)}, u32[]{:S(2)}) collective-permute-start(f32[12,8,128]{2,1,0:T(8,128)S(1)} %get-tuple-element.28), channel_id=1, source_target_pairs={{0,1},{1,0},{2,3},{3,2},{4,5},{5,4},{6,7},{7,6},{8,9},{9,8},{10,11... | collective-permute-start | bytes 147464 | tf_op jit(solution)/shard_map/ppermute | solution.py:425
  66.7 0.3 shard_map.72
  67.0 5.4 %collective-permute-done.2.tnear_ref = f32[12,8,128]{2,1,0:T(8,128)S(1)} collective-permute-done((f32[12,8,128]{2,1,0:T(8,128)S(1)}, f32[12,8,128]{2,1,0:T(8,128)S(1)}, u32[]{:S(2)}, u32[]{:S(2)}) %collective-permute-start.2) | collective-permute-done | bytes 49184 | tf_op jit(solution)/shard_map/ppermute | solution.py:425
  72.4 0.0 collective-permute-done.3.tfar_ref
  72.4 0.2 shard_map.73
  72.6 1.9 %collective-permute-start.4 = (f32[6,12,8,128]{3,2,1,0:T(8,128)S(1)}, f32[6,12,8,128]{3,2,1,0:T(8,128)S(1)}, u32[]{:S(2)}, u32[]{:S(2)}) collective-permute-start(f32[6,12,8,128]{3,2,1,0:T(8,128)S(1)} %get-tuple-element.34), channel_id=1, source_target_pairs={{0,64},{64,0},{128,192},{192,128},{256,320},{320,256},{384,448},{4... | collective-permute-start | bytes 884744 | tf_op jit(solution)/shard_map/ppermute | solution.py:425
  74.6 2.1 %collective-permute-start.5 = (f32[4,12,8,128]{3,2,1,0:T(8,128)S(1)}, f32[4,12,8,128]{3,2,1,0:T(8,128)S(1)}, u32[]{:S(2)}, u32[]{:S(2)}) collective-permute-start(f32[4,12,8,128]{3,2,1,0:T(8,128)S(1)} %get-tuple-element.35), channel_id=1, source_target_pairs={{0,448},{64,128},{128,64},{192,256},{256,192},{320,384},{384,320},... | collective-permute-start | bytes 589832 | tf_op jit(solution)/shard_map/ppermute | solution.py:425
  76.7 5.2 %collective-permute-start.6 = (f32[2,12,8,128]{3,2,1,0:T(8,128)S(1)}, f32[2,12,8,128]{3,2,1,0:T(8,128)S(1)}, u32[]{:S(2)}, u32[]{:S(2)}) collective-permute-start(f32[2,12,8,128]{3,2,1,0:T(8,128)S(1)} %get-tuple-element.36), channel_id=1, source_target_pairs={{0,448},{64,128},{128,64},{192,256},{256,192},{320,384},{384,320},... | collective-permute-start | bytes 294920 | tf_op jit(solution)/shard_map/ppermute | solution.py:425
  82.0 4.8 %collective-permute-start.7 = (f32[12,8,128]{2,1,0:T(8,128)S(1)}, f32[12,8,128]{2,1,0:T(8,128)S(1)}, u32[]{:S(2)}, u32[]{:S(2)}) collective-permute-start(f32[12,8,128]{2,1,0:T(8,128)S(1)} %get-tuple-element.37), channel_id=1, source_target_pairs={{0,1},{1,0},{2,3},{3,2},{4,5},{5,4},{6,7},{7,6},{8,9},{9,8},{10,11... | collective-permute-start | bytes 147464 | tf_op jit(solution)/shard_map/ppermute | solution.py:425
  86.7 0.8 copy.13
  87.5 1.2 %shard_map.74.y_ref = f32[6,24,8,128]{3,2,1,0:T(8,128)S(1)} custom-call(f32[6,24,8,128]{3,2,1,0:T(8,128)S(1)} %get-tuple-element.33.x_ref, f32[1152,128]{1,0:T(8,128)S(1)} %bitcast.13, f32[432,128]{1,0:T(8,128)S(1)} %get-tuple-element.22.links_ref, f32[8,128]{1,0:T(8,128)S(1)} %get-tuple-element.25.rate_ref), custom_call_target="tpu_custom_call" | custom-call | flops 5000000 | bytes 3000000 | tf_op jit(solution)/shard_map/pallas_call | solution.py:469
  88.8 3.1 %collective-permute-done.7.tnear_ref = f32[12,8,128]{2,1,0:T(8,128)S(1)} collective-permute-done((f32[12,8,128]{2,1,0:T(8,128)S(1)}, f32[12,8,128]{2,1,0:T(8,128)S(1)}, u32[]{:S(2)}, u32[]{:S(2)}) %collective-permute-start.7) | collective-permute-done | bytes 49184 | tf_op jit(solution)/shard_map/ppermute | solution.py:425
  91.8 0.0 collective-permute-done.6.zouter_ref
  91.8 0.0 collective-permute-done.5.zinner_ref
  91.8 0.0 collective-permute-done.4.znear_ref
  91.9 1.2 %shard_map.75 = f32[1152,128]{1,0:T(8,128)} custom-call(f32[6,24,8,128]{3,2,1,0:T(8,128)S(1)} %shard_map.74.y_ref, f32[432,128]{1,0:T(8,128)S(1)} %get-tuple-element.22.links_ref, f32[8,128]{1,0:T(8,128)S(1)} %get-tuple-element.25.rate_ref, f32[6,12,8,128]{3,2,1,0:T(8,128)S(1)} %collective-permute-done.4.znear_ref, ...), custom_call_target="tpu_custom_call" | custom-call | flops 5000000 | bytes 3000000 | tf_op jit(solution)/shard_map/pallas_call | solution.py:469
  (2 shorter events, 0.0 us)
Async XLA Ops:
  1.3 40.3 %copy-start.1 = (f32[32]{0:T(128)S(1)}, f32[32]{0:T(128)}, u32[]{:S(2)}) copy-start(f32[32]{0:T(128)} %param.7) | copy-start | bytes 388
  3.8 43.9 %copy-start = (f32[8,24,6,1,128]{4,3,2,1,0:T(1,128)S(1)}, f32[8,24,6,1,128]{4,3,2,1,0:T(1,128)}, u32[]{:S(2)}) copy-start(f32[8,24,6,1,128]{4,3,2,1,0:T(1,128)} %param.5) | copy-start | bytes 1769476
  42.8 6.1 %collective-permute-start = (f32[6,12,8,128]{3,2,1,0:T(8,128)S(1)}, f32[6,12,8,128]{3,2,1,0:T(8,128)S(1)}, u32[]{:S(2)}, u32[]{:S(2)}) collective-permute-start(f32[6,12,8,128]{3,2,1,0:T(8,128)S(1)} %get-tuple-element.26), channel_id=1, source_target_pairs={{0,64},{64,0},{128,192},{192,128},{256,320},{320,256},{384,448},{4... | collective-permute-start | bytes 884744 | tf_op jit(solution)/shard_map/ppermute | solution.py:425
  45.1 11.7 %collective-permute-start.1 = (f32[6,12,8,128]{3,2,1,0:T(8,128)S(1)}, f32[6,12,8,128]{3,2,1,0:T(8,128)S(1)}, u32[]{:S(2)}, u32[]{:S(2)}) collective-permute-start(f32[6,12,8,128]{3,2,1,0:T(8,128)S(1)} %get-tuple-element.27), channel_id=1, source_target_pairs={{0,448},{64,128},{128,64},{192,256},{256,192},{320,384},{384,320},... | collective-permute-start | bytes 884744 | tf_op jit(solution)/shard_map/ppermute | solution.py:425
  56.9 15.5 %collective-permute-start.3 = (f32[2,12,8,128]{3,2,1,0:T(8,128)S(1)}, f32[2,12,8,128]{3,2,1,0:T(8,128)S(1)}, u32[]{:S(2)}, u32[]{:S(2)}) collective-permute-start(f32[2,12,8,128]{3,2,1,0:T(8,128)S(1)} %get-tuple-element.30), channel_id=1, source_target_pairs={{0,63},{1,2},{2,1},{3,4},{4,3},{5,6},{6,5},{7,8},{8,7},{9,10},{10,... | collective-permute-start | bytes 294920 | tf_op jit(solution)/shard_map/ppermute | solution.py:425
  62.1 10.3 %collective-permute-start.2 = (f32[12,8,128]{2,1,0:T(8,128)S(1)}, f32[12,8,128]{2,1,0:T(8,128)S(1)}, u32[]{:S(2)}, u32[]{:S(2)}) collective-permute-start(f32[12,8,128]{2,1,0:T(8,128)S(1)} %get-tuple-element.28), channel_id=1, source_target_pairs={{0,1},{1,0},{2,3},{3,2},{4,5},{5,4},{6,7},{7,6},{8,9},{9,8},{10,11... | collective-permute-start | bytes 147464 | tf_op jit(solution)/shard_map/ppermute | solution.py:425
  72.6 19.2 %collective-permute-start.4 = (f32[6,12,8,128]{3,2,1,0:T(8,128)S(1)}, f32[6,12,8,128]{3,2,1,0:T(8,128)S(1)}, u32[]{:S(2)}, u32[]{:S(2)}) collective-permute-start(f32[6,12,8,128]{3,2,1,0:T(8,128)S(1)} %get-tuple-element.34), channel_id=1, source_target_pairs={{0,64},{64,0},{128,192},{192,128},{256,320},{320,256},{384,448},{4... | collective-permute-start | bytes 884744 | tf_op jit(solution)/shard_map/ppermute | solution.py:425
  74.6 17.3 %collective-permute-start.5 = (f32[4,12,8,128]{3,2,1,0:T(8,128)S(1)}, f32[4,12,8,128]{3,2,1,0:T(8,128)S(1)}, u32[]{:S(2)}, u32[]{:S(2)}) collective-permute-start(f32[4,12,8,128]{3,2,1,0:T(8,128)S(1)} %get-tuple-element.35), channel_id=1, source_target_pairs={{0,448},{64,128},{128,64},{192,256},{256,192},{320,384},{384,320},... | collective-permute-start | bytes 589832 | tf_op jit(solution)/shard_map/ppermute | solution.py:425
  76.7 15.1 %collective-permute-start.6 = (f32[2,12,8,128]{3,2,1,0:T(8,128)S(1)}, f32[2,12,8,128]{3,2,1,0:T(8,128)S(1)}, u32[]{:S(2)}, u32[]{:S(2)}) collective-permute-start(f32[2,12,8,128]{3,2,1,0:T(8,128)S(1)} %get-tuple-element.36), channel_id=1, source_target_pairs={{0,448},{64,128},{128,64},{192,256},{256,192},{320,384},{384,320},... | collective-permute-start | bytes 294920 | tf_op jit(solution)/shard_map/ppermute | solution.py:425
  82.0 9.9 %collective-permute-start.7 = (f32[12,8,128]{2,1,0:T(8,128)S(1)}, f32[12,8,128]{2,1,0:T(8,128)S(1)}, u32[]{:S(2)}, u32[]{:S(2)}) collective-permute-start(f32[12,8,128]{2,1,0:T(8,128)S(1)} %get-tuple-element.37), channel_id=1, source_target_pairs={{0,1},{1,0},{2,3},{3,2},{4,5},{5,4},{6,7},{7,6},{8,9},{9,8},{10,11... | collective-permute-start | bytes 147464 | tf_op jit(solution)/shard_map/ppermute | solution.py:425

commit v8 on v7

--- a/solution.py
+++ b/solution.py
@@ -276,6 +276,27 @@
     emit_time_halos(load(slices - 1), load(0), links_ref, tnear_ref, tfar_ref, slices)
 
 
+def copies_out(src_ref, dst_ref, sems):
+    rows = src_ref.shape[0] // 8
+    return [
+        pltpu.make_async_copy(
+            src_ref.at[pl.ds(i * rows, rows)], dst_ref.at[pl.ds(i * rows, rows)], sems.at[i]
+        )
+        for i in range(8)
+    ]
+
+
+def local_and_copy_kernel(
+    x_ref, src_ref, links_ref, rate_ref, held_ref, y_ref, out_hbm, behind_ref, sems, *, slices
+):
+    copies = copies_out(held_ref, out_hbm, sems)
+    for copy in copies:
+        copy.start()
+    local_kernel(x_ref, src_ref, links_ref, rate_ref, y_ref, behind_ref, slices=slices)
+    for copy in copies:
+        copy.wait()
+
+
 def local_kernel(x_ref, src_ref, links_ref, rate_ref, y_ref, behind_ref, *, slices):
     behind_ref[...] = jnp.zeros_like(behind_ref)
 
@@ -381,7 +402,8 @@
 
 
 def last_kernel(
-    y_ref, links_ref, rate_ref, znear_ref, zinner_ref, zouter_ref, tnear_ref, tfar_ref, out_ref, *, slices
+    y_ref, links_ref, rate_ref, znear_ref, zinner_ref, zouter_ref, tnear_ref, tfar_ref,
+    out_hbm, out_ref, sems, *, slices,
 ):
     rate = rate_ref[...] * HOPPING
 
@@ -402,15 +424,24 @@
         return carry
 
     lax.fori_loop(1, slices - 1, step, 0)
-
-
-def call(kernel, outs, ins, flops, hbm=(), smem=(), scratch=()):
+    copies = copies_out(out_ref, out_hbm, sems)
+    for copy in copies:
+        copy.start()
+    for copy in copies:
+        copy.wait()
+
+
+def call(kernel, outs, ins, flops, hbm=(), smem=(), scratch=(), hbm_outs=()):
     space = lambda i: pltpu.HBM if i in hbm else pltpu.SMEM if i in smem else pltpu.VMEM
+    out_space = lambda i: pltpu.HBM if i in hbm_outs else pltpu.VMEM
+    single = not isinstance(outs, tuple)
     return pl.pallas_call(
         kernel,
         out_shape=outs,
         in_specs=[pl.BlockSpec(memory_space=space(i)) for i in range(ins)],
-        out_specs=jax.tree.map(lambda _: pl.BlockSpec(memory_space=pltpu.VMEM), outs),
+        out_specs=pl.BlockSpec(memory_space=out_space(0))
+        if single
+        else tuple(pl.BlockSpec(memory_space=out_space(i)) for i in range(len(outs))),
         scratch_shapes=list(scratch),
         compiler_params=pltpu.CompilerParams(vmem_limit_bytes=24 << 20),
         cost_estimate=pl.CostEstimate(
@@ -465,10 +496,10 @@
 
     time = ("lat", "sub")
 
-    def stage(kernel, outs, *args, scratch=()):
+    def stage(kernel, outs, *args, scratch=(), hbm_outs=()):
         return call(
             functools.partial(kernel, slices=slices), outs, len(args),
-            5_000_000, scratch=scratch,
+            5_000_000, scratch=scratch, hbm_outs=hbm_outs,
         )(*args)
 
     carry = [pltpu.VMEM((12, 8, 128), f32)]
@@ -495,8 +526,14 @@
     )
     zouter = swap(zouter, "src", True)
     znear = swap(znear, "src", False)
-    y = stage(local_kernel, field, x, src, flat_links, rate, scratch=carry)
-    x = stage(last_kernel, flat, y, flat_links, rate, znear, zinner, zouter, next_tnear, both_tfar)
+    y, guess = stage(
+        local_and_copy_kernel, (field, flat), x, src, flat_links, rate, guess,
+        scratch=carry + [pltpu.SemaphoreType.DMA((8,))], hbm_outs=(1,),
+    )
+    x = stage(
+        last_kernel, flat, y, flat_links, rate, znear, zinner, zouter, next_tnear, both_tfar,
+        scratch=[pltpu.VMEM(flat.shape, f32), pltpu.SemaphoreType.DMA((8,))], hbm_outs=(0,),
+    )
     return (guess.reshape(sources.shape), x.reshape(sources.shape))
 
 

time: 93.5 us -> 93.5 us (level)
  transfers between devices with their start and end apart: 8 -> 8, of which waited for: 3 -> 3; matrix products, arithmetic and copies ran while one was open for 1% -> 0% of each run, Pallas kernels for 3% -> 3%
where the time goes in v8:
time: 93.5 us; the launch traced here: 93.1 us
  blocking collectives  37.8 us (40%)
  starting transfers between devices  28.6 us (31%)
  waiting for transfers between devices  17.1 us (18%)
  Pallas kernels  8.09 us (9%)
  between operations  1.43 us (2%)
    ppermute x8, starting transfers between devices, swap(): return lax.ppermute(x, axis, [(i, partner(i)) for i in range(n)])  28.6 us
    all_to_all x1, blocking collectives, shards(): partial = lax.all_to_all(partial, 'lat', 0, 0, tiled=True)  19.8 us
    all_to_all x1, blocking collectives, shards(): partial = lax.all_to_all(partial, ('sub', 'src'), 0, 0, tiled=True)  18 us
    ppermute x8, waiting for transfers between devices, swap(): return lax.ppermute(x, axis, [(i, partner(i)) for i in range(n)])  17.1 us
    pallas_call x6, Pallas kernels, stage(): call(functools.partial(kernel, slices=slices), outs, len(args), 5000000,...  4.42 us
    pallas_call x1, Pallas kernels, shards(): call(functools.partial(correlation_kernel, nev=nev, slices=slices), (shap...  2.46 us
  transfers between devices with their start and end apart: 8, of which 3 were waited for; matrix products, arithmetic and copies ran while one was open for 0% of the time, Pallas kernels for 3%

profile of v8, /device:TPU:8, one launch (start us, length us, event | category | flops | bytes accessed | tf_op | source)
XLA Modules:
  0.0 93.1 jit_solution(18320787406341649160)
XLA Ops:
  1.3 0.0 copy-start.1
  1.3 2.5 %shard_map.68 = (f32[32,8,128]{2,1,0:T(8,128)S(1)}, bf16[32,6,24,128]{3,2,1,0:T(8,128)(2,1)S(1)}, f32[432,128]{1,0:T(8,128)S(1)}) custom-call(bf16[32,6,24,128]{3,2,1,0:T(8,128)(2,1)} %bitcast.15, f32[1152,128]{1,0:T(8,128)} %bitcast.10, f32[432,8,128]{2,1,0:T(8,128)} %bitcast.14, f32[1]{0:T(128)S(6)} %copy.13.damp_ref), custom_call_target="tpu_custom_call" | custom-call | flops 226000000 | bytes 3000000 | tf_op jit(solution)/shard_map/pallas_call | solution.py:474
  3.8 0.0 copy-start
  3.8 19.8 %all_to_all.10 = f32[32,8,128]{2,1,0:T(8,128)S(1)} all-to-all(f32[32,8,128]{2,1,0:T(8,128)S(1)} %get-tuple-element.22), channel_id=1, replica_groups=mesh['src'=8,'lat'=32,'sub'=2] {'lat'}, dimensions={0} | all-to-all | bytes 262144 | tf_op jit(solution)/shard_map/all_to_all | solution.py:483
  23.6 18.0 %all_to_all.11.part_ref = f32[16,8,128]{2,1,0:T(8,128)S(1)} all-to-all(f32[16,8,128]{2,1,0:T(8,128)S(1)} %broadcast_in_dim.2), channel_id=1, replica_groups=mesh['src'=8,'lat'=32,'sub'=2] {'sub','src'}, dimensions={0} | all-to-all | bytes 131072 | tf_op jit(solution)/shard_map/all_to_all | solution.py:485
  41.6 0.0 copy-done.1
  41.6 1.2 %shard_map.69 = (f32[6,24,8,128]{3,2,1,0:T(8,128)S(1)}, f32[8,128]{1,0:T(8,128)S(1)}, f32[1152,128]{1,0:T(8,128)S(1)}, f32[6,12,8,128]{3,2,1,0:T(8,128)S(1)}, f3...) custom-call(f32[16,8,128]{2,1,0:T(8,128)S(1)} %all_to_all.11.part_ref, ...), custom_call_target="tpu_custom_call" | custom-call | flops 226000000 | bytes 3000000 | tf_op jit(solution)/shard_map/pallas_call | solution.py:491
  42.8 2.3 %collective-permute-start = (f32[6,12,8,128]{3,2,1,0:T(8,128)S(1)}, f32[6,12,8,128]{3,2,1,0:T(8,128)S(1)}, u32[]{:S(2)}, u32[]{:S(2)}) collective-permute-start(f32[6,12,8,128]{3,2,1,0:T(8,128)S(1)} %get-tuple-element.27), channel_id=1, source_target_pairs={{0,64},{64,0},{128,192},{192,128},{256,320},{320,256},{384,448},{4... | collective-permute-start | bytes 884744 | tf_op jit(solution)/shard_map/ppermute | solution.py:456
  45.1 2.5 %collective-permute-start.1 = (f32[6,12,8,128]{3,2,1,0:T(8,128)S(1)}, f32[6,12,8,128]{3,2,1,0:T(8,128)S(1)}, u32[]{:S(2)}, u32[]{:S(2)}) collective-permute-start(f32[6,12,8,128]{3,2,1,0:T(8,128)S(1)} %get-tuple-element.28), channel_id=1, source_target_pairs={{0,448},{64,128},{128,64},{192,256},{256,192},{320,384},{384,320},... | collective-permute-start | bytes 884744 | tf_op jit(solution)/shard_map/ppermute | solution.py:456
  47.6 0.0 copy-done
  47.6 1.2 %shard_map.70.y_ref = f32[6,24,8,128]{3,2,1,0:T(8,128)S(1)} custom-call(f32[6,24,8,128]{3,2,1,0:T(8,128)S(1)} %get-tuple-element.25.x_ref, f32[1152,128]{1,0:T(8,128)S(1)} %bitcast.11, f32[432,128]{1,0:T(8,128)S(1)} %get-tuple-element.24.links_ref, f32[8,128]{1,0:T(8,128)S(1)} %get-tuple-element.26.rate_ref), custom_call_target="tpu_custom_call" | custom-call | flops 5000000 | bytes 3000000 | tf_op jit(solution)/shard_map/pallas_call | solution.py:500
  48.9 0.0 collective-permute-done.znear_ref
  48.9 7.9 %collective-permute-done.1.zfar_ref = f32[6,12,8,128]{3,2,1,0:T(8,128)S(1)} collective-permute-done((f32[6,12,8,128]{3,2,1,0:T(8,128)S(1)}, f32[6,12,8,128]{3,2,1,0:T(8,128)S(1)}, u32[]{:S(2)}, u32[]{:S(2)}) %collective-permute-start.1) | collective-permute-done | bytes 294944 | tf_op jit(solution)/shard_map/ppermute | solution.py:456
  56.8 0.1 shard_map.71
  56.9 5.1 %collective-permute-start.3 = (f32[2,12,8,128]{3,2,1,0:T(8,128)S(1)}, f32[2,12,8,128]{3,2,1,0:T(8,128)S(1)}, u32[]{:S(2)}, u32[]{:S(2)}) collective-permute-start(f32[2,12,8,128]{3,2,1,0:T(8,128)S(1)} %get-tuple-element.31), channel_id=1, source_target_pairs={{0,63},{1,2},{2,1},{3,4},{4,3},{5,6},{6,5},{7,8},{8,7},{9,10},{10,... | collective-permute-start | bytes 294920 | tf_op jit(solution)/shard_map/ppermute | solution.py:456
  62.1 4.6 %collective-permute-start.2 = (f32[12,8,128]{2,1,0:T(8,128)S(1)}, f32[12,8,128]{2,1,0:T(8,128)S(1)}, u32[]{:S(2)}, u32[]{:S(2)}) collective-permute-start(f32[12,8,128]{2,1,0:T(8,128)S(1)} %get-tuple-element.29), channel_id=1, source_target_pairs={{0,1},{1,0},{2,3},{3,2},{4,5},{5,4},{6,7},{7,6},{8,9},{9,8},{10,11... | collective-permute-start | bytes 147464 | tf_op jit(solution)/shard_map/ppermute | solution.py:456
  66.7 0.3 shard_map.72
  67.0 5.4 %collective-permute-done.2.tnear_ref = f32[12,8,128]{2,1,0:T(8,128)S(1)} collective-permute-done((f32[12,8,128]{2,1,0:T(8,128)S(1)}, f32[12,8,128]{2,1,0:T(8,128)S(1)}, u32[]{:S(2)}, u32[]{:S(2)}) %collective-permute-start.2) | collective-permute-done | bytes 49184 | tf_op jit(solution)/shard_map/ppermute | solution.py:456
  72.4 0.0 collective-permute-done.3.tfar_ref
  72.4 0.2 shard_map.73
  72.6 1.9 %collective-permute-start.4 = (f32[6,12,8,128]{3,2,1,0:T(8,128)S(1)}, f32[6,12,8,128]{3,2,1,0:T(8,128)S(1)}, u32[]{:S(2)}, u32[]{:S(2)}) collective-permute-start(f32[6,12,8,128]{3,2,1,0:T(8,128)S(1)} %get-tuple-element.38), channel_id=1, source_target_pairs={{0,64},{64,0},{128,192},{192,128},{256,320},{320,256},{384,448},{4... | collective-permute-start | bytes 884744 | tf_op jit(solution)/shard_map/ppermute | solution.py:456
  74.6 2.1 %collective-permute-start.5 = (f32[4,12,8,128]{3,2,1,0:T(8,128)S(1)}, f32[4,12,8,128]{3,2,1,0:T(8,128)S(1)}, u32[]{:S(2)}, u32[]{:S(2)}) collective-permute-start(f32[4,12,8,128]{3,2,1,0:T(8,128)S(1)} %get-tuple-element.39), channel_id=1, source_target_pairs={{0,448},{64,128},{128,64},{192,256},{256,192},{320,384},{384,320},... | collective-permute-start | bytes 589832 | tf_op jit(solution)/shard_map/ppermute | solution.py:456
  76.7 5.2 %collective-permute-start.6 = (f32[2,12,8,128]{3,2,1,0:T(8,128)S(1)}, f32[2,12,8,128]{3,2,1,0:T(8,128)S(1)}, u32[]{:S(2)}, u32[]{:S(2)}) collective-permute-start(f32[2,12,8,128]{3,2,1,0:T(8,128)S(1)} %get-tuple-element.40), channel_id=1, source_target_pairs={{0,448},{64,128},{128,64},{192,256},{256,192},{320,384},{384,320},... | collective-permute-start | bytes 294920 | tf_op jit(solution)/shard_map/ppermute | solution.py:456
  82.0 4.8 %collective-permute-start.7 = (f32[12,8,128]{2,1,0:T(8,128)S(1)}, f32[12,8,128]{2,1,0:T(8,128)S(1)}, u32[]{:S(2)}, u32[]{:S(2)}) collective-permute-start(f32[12,8,128]{2,1,0:T(8,128)S(1)} %get-tuple-element.41), channel_id=1, source_target_pairs={{0,1},{1,0},{2,3},{3,2},{4,5},{5,4},{6,7},{7,6},{8,9},{9,8},{10,11... | collective-permute-start | bytes 147464 | tf_op jit(solution)/shard_map/ppermute | solution.py:456
  86.7 1.3 %shard_map.74 = (f32[6,24,8,128]{3,2,1,0:T(8,128)S(1)}, f32[1152,128]{1,0:T(8,128)}) custom-call(f32[6,24,8,128]{3,2,1,0:T(8,128)S(1)} %get-tuple-element.34.x_ref, f32[1152,128]{1,0:T(8,128)S(1)} %bitcast.12, f32[432,128]{1,0:T(8,128)S(1)} %get-tuple-element.24.links_ref, f32[8,128]{1,0:T(8,128)S(1)} %get-tuple-element.26.rate_ref, ...), custom_call_target="tpu_custom_call" | custom-call | flops 5000000 | bytes 3000000 | tf_op jit(solution)/shard_map/pallas_call | solution.py:500
  88.1 3.8 %collective-permute-done.7.tnear_ref = f32[12,8,128]{2,1,0:T(8,128)S(1)} collective-permute-done((f32[12,8,128]{2,1,0:T(8,128)S(1)}, f32[12,8,128]{2,1,0:T(8,128)S(1)}, u32[]{:S(2)}, u32[]{:S(2)}) %collective-permute-start.7) | collective-permute-done | bytes 49184 | tf_op jit(solution)/shard_map/ppermute | solution.py:456
  91.8 0.0 collective-permute-done.6.zouter_ref
  91.8 0.0 collective-permute-done.5.zinner_ref
  91.8 0.0 collective-permute-done.4.znear_ref
  91.9 1.2 %shard_map.75 = f32[1152,128]{1,0:T(8,128)} custom-call(f32[6,24,8,128]{3,2,1,0:T(8,128)S(1)} %get-tuple-element.37.y_ref, f32[432,128]{1,0:T(8,128)S(1)} %get-tuple-element.24.links_ref, f32[8,128]{1,0:T(8,128)S(1)} %get-tuple-element.26.rate_ref, f32[6,12,8,128]{3,2,1,0:T(8,128)S(1)} %collective-permute-done.4.znear_ref, ...), custom_call_target="tpu_custom_call" | custom-call | flops 5000000 | bytes 3000000 | tf_op jit(solution)/shard_map/pallas_call | solution.py:500
  (2 shorter events, 0.0 us)
Async XLA Ops:
  1.3 40.3 %copy-start.1 = (f32[32]{0:T(128)S(1)}, f32[32]{0:T(128)}, u32[]{:S(2)}) copy-start(f32[32]{0:T(128)} %param.7) | copy-start | bytes 388
  3.8 43.9 %copy-start = (f32[8,24,6,1,128]{4,3,2,1,0:T(1,128)S(1)}, f32[8,24,6,1,128]{4,3,2,1,0:T(1,128)}, u32[]{:S(2)}) copy-start(f32[8,24,6,1,128]{4,3,2,1,0:T(1,128)} %param.5) | copy-start | bytes 1769476
  42.8 6.1 %collective-permute-start = (f32[6,12,8,128]{3,2,1,0:T(8,128)S(1)}, f32[6,12,8,128]{3,2,1,0:T(8,128)S(1)}, u32[]{:S(2)}, u32[]{:S(2)}) collective-permute-start(f32[6,12,8,128]{3,2,1,0:T(8,128)S(1)} %get-tuple-element.27), channel_id=1, source_target_pairs={{0,64},{64,0},{128,192},{192,128},{256,320},{320,256},{384,448},{4... | collective-permute-start | bytes 884744 | tf_op jit(solution)/shard_map/ppermute | solution.py:456
  45.1 11.7 %collective-permute-start.1 = (f32[6,12,8,128]{3,2,1,0:T(8,128)S(1)}, f32[6,12,8,128]{3,2,1,0:T(8,128)S(1)}, u32[]{:S(2)}, u32[]{:S(2)}) collective-permute-start(f32[6,12,8,128]{3,2,1,0:T(8,128)S(1)} %get-tuple-element.28), channel_id=1, source_target_pairs={{0,448},{64,128},{128,64},{192,256},{256,192},{320,384},{384,320},... | collective-permute-start | bytes 884744 | tf_op jit(solution)/shard_map/ppermute | solution.py:456
  56.9 15.5 %collective-permute-start.3 = (f32[2,12,8,128]{3,2,1,0:T(8,128)S(1)}, f32[2,12,8,128]{3,2,1,0:T(8,128)S(1)}, u32[]{:S(2)}, u32[]{:S(2)}) collective-permute-start(f32[2,12,8,128]{3,2,1,0:T(8,128)S(1)} %get-tuple-element.31), channel_id=1, source_target_pairs={{0,63},{1,2},{2,1},{3,4},{4,3},{5,6},{6,5},{7,8},{8,7},{9,10},{10,... | collective-permute-start | bytes 294920 | tf_op jit(solution)/shard_map/ppermute | solution.py:456
  62.1 10.3 %collective-permute-start.2 = (f32[12,8,128]{2,1,0:T(8,128)S(1)}, f32[12,8,128]{2,1,0:T(8,128)S(1)}, u32[]{:S(2)}, u32[]{:S(2)}) collective-permute-start(f32[12,8,128]{2,1,0:T(8,128)S(1)} %get-tuple-element.29), channel_id=1, source_target_pairs={{0,1},{1,0},{2,3},{3,2},{4,5},{5,4},{6,7},{7,6},{8,9},{9,8},{10,11... | collective-permute-start | bytes 147464 | tf_op jit(solution)/shard_map/ppermute | solution.py:456
  72.6 19.2 %collective-permute-start.4 = (f32[6,12,8,128]{3,2,1,0:T(8,128)S(1)}, f32[6,12,8,128]{3,2,1,0:T(8,128)S(1)}, u32[]{:S(2)}, u32[]{:S(2)}) collective-permute-start(f32[6,12,8,128]{3,2,1,0:T(8,128)S(1)} %get-tuple-element.38), channel_id=1, source_target_pairs={{0,64},{64,0},{128,192},{192,128},{256,320},{320,256},{384,448},{4... | collective-permute-start | bytes 884744 | tf_op jit(solution)/shard_map/ppermute | solution.py:456
  74.6 17.3 %collective-permute-start.5 = (f32[4,12,8,128]{3,2,1,0:T(8,128)S(1)}, f32[4,12,8,128]{3,2,1,0:T(8,128)S(1)}, u32[]{:S(2)}, u32[]{:S(2)}) collective-permute-start(f32[4,12,8,128]{3,2,1,0:T(8,128)S(1)} %get-tuple-element.39), channel_id=1, source_target_pairs={{0,448},{64,128},{128,64},{192,256},{256,192},{320,384},{384,320},... | collective-permute-start | bytes 589832 | tf_op jit(solution)/shard_map/ppermute | solution.py:456
  76.7 15.1 %collective-permute-start.6 = (f32[2,12,8,128]{3,2,1,0:T(8,128)S(1)}, f32[2,12,8,128]{3,2,1,0:T(8,128)S(1)}, u32[]{:S(2)}, u32[]{:S(2)}) collective-permute-start(f32[2,12,8,128]{3,2,1,0:T(8,128)S(1)} %get-tuple-element.40), channel_id=1, source_target_pairs={{0,448},{64,128},{128,64},{192,256},{256,192},{320,384},{384,320},... | collective-permute-start | bytes 294920 | tf_op jit(solution)/shard_map/ppermute | solution.py:456
  82.0 9.9 %collective-permute-start.7 = (f32[12,8,128]{2,1,0:T(8,128)S(1)}, f32[12,8,128]{2,1,0:T(8,128)S(1)}, u32[]{:S(2)}, u32[]{:S(2)}) collective-permute-start(f32[12,8,128]{2,1,0:T(8,128)S(1)} %get-tuple-element.41), channel_id=1, source_target_pairs={{0,1},{1,0},{2,3},{3,2},{4,5},{5,4},{6,7},{7,6},{8,9},{9,8},{10,11... | collective-permute-start | bytes 147464 | tf_op jit(solution)/shard_map/ppermute | solution.py:456

commit v9 on v8

--- a/solution.py
+++ b/solution.py
@@ -148,22 +148,25 @@
         copy.start()
     for copy in src_copies:
         copy.wait()
+    row = lax.rem(lax.broadcasted_iota(jnp.int32, (sources * comps, 1), 0), comps)
+    col = lax.rem(lax.broadcasted_iota(jnp.int32, (1, nev * comps), 1), comps)
+    gap = row - col
+    first = lax.broadcasted_iota(jnp.int32, (nev * comps, 128), 0)
+    start = lax.broadcasted_iota(jnp.int32, (nev * comps, 128), 1) * comps
+    gather = jnp.where((first >= start) & (first < start + comps), 1.0, 0.0).astype(jnp.bfloat16)
+    lhs = [
+        src_ref[pl.ds(t, sources * comps, stride=slices), :].astype(jnp.bfloat16)
+        for t in range(slices)
+    ]
     full = jnp.zeros((sources * comps, nev * comps), jnp.float32)
     for t in range(0, slices, 2):
-        lhs = [
-            src_ref[pl.ds(u, sources * comps, stride=slices), :].astype(jnp.bfloat16)
-            for u in (t, t + 1)
-        ]
         eig_copies[t].wait()
         eig_copies[t + 1].wait()
         rhs = [eig_ref[:, u].reshape(nev * comps, 128) for u in (t, t + 1)]
         full = full + lax.dot_general(
-            jnp.concatenate(lhs, axis=1), jnp.concatenate(rhs, axis=1),
+            jnp.concatenate(lhs[t : t + 2], axis=1), jnp.concatenate(rhs, axis=1),
             (((1,), (1,)), ((), ())), preferred_element_type=jnp.float32,
         )
-    row = lax.rem(lax.broadcasted_iota(jnp.int32, (sources * comps, 1), 0), comps)
-    col = lax.rem(lax.broadcasted_iota(jnp.int32, (1, nev * comps), 1), comps)
-    gap = row - col
     straight = jnp.where(gap == 0, full, 0.0)
     crossed = jnp.where(gap == 12, full, 0.0) - jnp.where(gap == -12, full, 0.0)
     straight = straight.reshape(sources, comps, nev * comps).sum(1)
@@ -173,9 +176,6 @@
     middle = (both - high.astype(jnp.float32)).astype(jnp.bfloat16)
     low = (both - high.astype(jnp.float32) - middle.astype(jnp.float32)).astype(jnp.bfloat16)
     parts = jnp.concatenate([high, middle, low], axis=0)
-    first = lax.broadcasted_iota(jnp.int32, (nev * comps, 128), 0)
-    start = lax.broadcasted_iota(jnp.int32, (nev * comps, 128), 1) * comps
-    gather = jnp.where((first >= start) & (first < start + comps), 1.0, 0.0).astype(jnp.bfloat16)
     sums = jnp.dot(parts, gather, preferred_element_type=jnp.float32)
     sums = (sums[0:16] + sums[16:32]) + sums[32:48]
     total = sums[0:8] + pltpu.roll(sums[8:16], nev, 1)

time: 93.5 us -> 93.4 us (level)
  no operation moved by 1% of the time
where the time goes in v9:
time: 93.4 us; the launch traced here: 93 us
  blocking collectives  37.8 us (40%)
  starting transfers between devices  28.6 us (31%)
  waiting for transfers between devices  17.1 us (18%)
  Pallas kernels  8.01 us (9%)
  between operations  1.43 us (2%)
    ppermute x8, starting transfers between devices, swap(): return lax.ppermute(x, axis, [(i, partner(i)) for i in range(n)])  28.6 us
    all_to_all x1, blocking collectives, shards(): partial = lax.all_to_all(partial, 'lat', 0, 0, tiled=True)  19.8 us
    all_to_all x1, blocking collectives, shards(): partial = lax.all_to_all(partial, ('sub', 'src'), 0, 0, tiled=True)  18 us
    ppermute x8, waiting for transfers between devices, swap(): return lax.ppermute(x, axis, [(i, partner(i)) for i in range(n)])  17.1 us
    pallas_call x6, Pallas kernels, stage(): call(functools.partial(kernel, slices=slices), outs, len(args), 5000000,...  4.42 us
    pallas_call x1, Pallas kernels, shards(): call(functools.partial(correlation_kernel, nev=nev, slices=slices), (shap...  2.38 us
  transfers between devices with their start and end apart: 8, of which 3 were waited for; matrix products, arithmetic and copies ran while one was open for 0% of the time, Pallas kernels for 3%

profile of v9, /device:TPU:8, one launch (start us, length us, event | category | flops | bytes accessed | tf_op | source)
XLA Modules:
  0.0 93.0 jit_solution(10106903067943323368)
XLA Ops:
  1.3 0.0 copy-start.1
  1.3 2.4 %shard_map.68 = (f32[32,8,128]{2,1,0:T(8,128)S(1)}, bf16[32,6,24,128]{3,2,1,0:T(8,128)(2,1)S(1)}, f32[432,128]{1,0:T(8,128)S(1)}) custom-call(bf16[32,6,24,128]{3,2,1,0:T(8,128)(2,1)} %bitcast.15, f32[1152,128]{1,0:T(8,128)} %bitcast.10, f32[432,8,128]{2,1,0:T(8,128)} %bitcast.14, f32[1]{0:T(128)S(6)} %copy.13.damp_ref), custom_call_target="tpu_custom_call" | custom-call | flops 226000000 | bytes 3000000 | tf_op jit(solution)/shard_map/pallas_call | solution.py:474
  3.7 0.0 copy-start
  3.7 19.8 %all_to_all.10 = f32[32,8,128]{2,1,0:T(8,128)S(1)} all-to-all(f32[32,8,128]{2,1,0:T(8,128)S(1)} %get-tuple-element.22), channel_id=1, replica_groups=mesh['src'=8,'lat'=32,'sub'=2] {'lat'}, dimensions={0} | all-to-all | bytes 262144 | tf_op jit(solution)/shard_map/all_to_all | solution.py:483
  23.5 18.0 %all_to_all.11.part_ref = f32[16,8,128]{2,1,0:T(8,128)S(1)} all-to-all(f32[16,8,128]{2,1,0:T(8,128)S(1)} %broadcast_in_dim.2), channel_id=1, replica_groups=mesh['src'=8,'lat'=32,'sub'=2] {'sub','src'}, dimensions={0} | all-to-all | bytes 131072 | tf_op jit(solution)/shard_map/all_to_all | solution.py:485
  41.5 0.0 copy-done.1
  41.5 1.2 %shard_map.69 = (f32[6,24,8,128]{3,2,1,0:T(8,128)S(1)}, f32[8,128]{1,0:T(8,128)S(1)}, f32[1152,128]{1,0:T(8,128)S(1)}, f32[6,12,8,128]{3,2,1,0:T(8,128)S(1)}, f3...) custom-call(f32[16,8,128]{2,1,0:T(8,128)S(1)} %all_to_all.11.part_ref, ...), custom_call_target="tpu_custom_call" | custom-call | flops 226000000 | bytes 3000000 | tf_op jit(solution)/shard_map/pallas_call | solution.py:491
  42.7 2.3 %collective-permute-start = (f32[6,12,8,128]{3,2,1,0:T(8,128)S(1)}, f32[6,12,8,128]{3,2,1,0:T(8,128)S(1)}, u32[]{:S(2)}, u32[]{:S(2)}) collective-permute-start(f32[6,12,8,128]{3,2,1,0:T(8,128)S(1)} %get-tuple-element.27), channel_id=1, source_target_pairs={{0,64},{64,0},{128,192},{192,128},{256,320},{320,256},{384,448},{4... | collective-permute-start | bytes 884744 | tf_op jit(solution)/shard_map/ppermute | solution.py:456
  45.0 2.5 %collective-permute-start.1 = (f32[6,12,8,128]{3,2,1,0:T(8,128)S(1)}, f32[6,12,8,128]{3,2,1,0:T(8,128)S(1)}, u32[]{:S(2)}, u32[]{:S(2)}) collective-permute-start(f32[6,12,8,128]{3,2,1,0:T(8,128)S(1)} %get-tuple-element.28), channel_id=1, source_target_pairs={{0,448},{64,128},{128,64},{192,256},{256,192},{320,384},{384,320},... | collective-permute-start | bytes 884744 | tf_op jit(solution)/shard_map/ppermute | solution.py:456
  47.6 0.0 copy-done
  47.6 1.2 %shard_map.70.y_ref = f32[6,24,8,128]{3,2,1,0:T(8,128)S(1)} custom-call(f32[6,24,8,128]{3,2,1,0:T(8,128)S(1)} %get-tuple-element.25.x_ref, f32[1152,128]{1,0:T(8,128)S(1)} %bitcast.11, f32[432,128]{1,0:T(8,128)S(1)} %get-tuple-element.24.links_ref, f32[8,128]{1,0:T(8,128)S(1)} %get-tuple-element.26.rate_ref), custom_call_target="tpu_custom_call" | custom-call | flops 5000000 | bytes 3000000 | tf_op jit(solution)/shard_map/pallas_call | solution.py:500
  48.8 0.0 collective-permute-done.znear_ref
  48.8 7.9 %collective-permute-done.1.zfar_ref = f32[6,12,8,128]{3,2,1,0:T(8,128)S(1)} collective-permute-done((f32[6,12,8,128]{3,2,1,0:T(8,128)S(1)}, f32[6,12,8,128]{3,2,1,0:T(8,128)S(1)}, u32[]{:S(2)}, u32[]{:S(2)}) %collective-permute-start.1) | collective-permute-done | bytes 294944 | tf_op jit(solution)/shard_map/ppermute | solution.py:456
  56.7 0.1 shard_map.71
  56.9 5.1 %collective-permute-start.3 = (f32[2,12,8,128]{3,2,1,0:T(8,128)S(1)}, f32[2,12,8,128]{3,2,1,0:T(8,128)S(1)}, u32[]{:S(2)}, u32[]{:S(2)}) collective-permute-start(f32[2,12,8,128]{3,2,1,0:T(8,128)S(1)} %get-tuple-element.31), channel_id=1, source_target_pairs={{0,63},{1,2},{2,1},{3,4},{4,3},{5,6},{6,5},{7,8},{8,7},{9,10},{10,... | collective-permute-start | bytes 294920 | tf_op jit(solution)/shard_map/ppermute | solution.py:456
  62.0 4.6 %collective-permute-start.2 = (f32[12,8,128]{2,1,0:T(8,128)S(1)}, f32[12,8,128]{2,1,0:T(8,128)S(1)}, u32[]{:S(2)}, u32[]{:S(2)}) collective-permute-start(f32[12,8,128]{2,1,0:T(8,128)S(1)} %get-tuple-element.29), channel_id=1, source_target_pairs={{0,1},{1,0},{2,3},{3,2},{4,5},{5,4},{6,7},{7,6},{8,9},{9,8},{10,11... | collective-permute-start | bytes 147464 | tf_op jit(solution)/shard_map/ppermute | solution.py:456
  66.6 0.3 shard_map.72
  66.9 5.4 %collective-permute-done.2.tnear_ref = f32[12,8,128]{2,1,0:T(8,128)S(1)} collective-permute-done((f32[12,8,128]{2,1,0:T(8,128)S(1)}, f32[12,8,128]{2,1,0:T(8,128)S(1)}, u32[]{:S(2)}, u32[]{:S(2)}) %collective-permute-start.2) | collective-permute-done | bytes 49184 | tf_op jit(solution)/shard_map/ppermute | solution.py:456
  72.4 0.0 collective-permute-done.3.tfar_ref
  72.4 0.2 shard_map.73
  72.6 1.9 %collective-permute-start.4 = (f32[6,12,8,128]{3,2,1,0:T(8,128)S(1)}, f32[6,12,8,128]{3,2,1,0:T(8,128)S(1)}, u32[]{:S(2)}, u32[]{:S(2)}) collective-permute-start(f32[6,12,8,128]{3,2,1,0:T(8,128)S(1)} %get-tuple-element.38), channel_id=1, source_target_pairs={{0,64},{64,0},{128,192},{192,128},{256,320},{320,256},{384,448},{4... | collective-permute-start | bytes 884744 | tf_op jit(solution)/shard_map/ppermute | solution.py:456
  74.5 2.1 %collective-permute-start.5 = (f32[4,12,8,128]{3,2,1,0:T(8,128)S(1)}, f32[4,12,8,128]{3,2,1,0:T(8,128)S(1)}, u32[]{:S(2)}, u32[]{:S(2)}) collective-permute-start(f32[4,12,8,128]{3,2,1,0:T(8,128)S(1)} %get-tuple-element.39), channel_id=1, source_target_pairs={{0,448},{64,128},{128,64},{192,256},{256,192},{320,384},{384,320},... | collective-permute-start | bytes 589832 | tf_op jit(solution)/shard_map/ppermute | solution.py:456
  76.6 5.2 %collective-permute-start.6 = (f32[2,12,8,128]{3,2,1,0:T(8,128)S(1)}, f32[2,12,8,128]{3,2,1,0:T(8,128)S(1)}, u32[]{:S(2)}, u32[]{:S(2)}) collective-permute-start(f32[2,12,8,128]{3,2,1,0:T(8,128)S(1)} %get-tuple-element.40), channel_id=1, source_target_pairs={{0,448},{64,128},{128,64},{192,256},{256,192},{320,384},{384,320},... | collective-permute-start | bytes 294920 | tf_op jit(solution)/shard_map/ppermute | solution.py:456
  81.9 4.8 %collective-permute-start.7 = (f32[12,8,128]{2,1,0:T(8,128)S(1)}, f32[12,8,128]{2,1,0:T(8,128)S(1)}, u32[]{:S(2)}, u32[]{:S(2)}) collective-permute-start(f32[12,8,128]{2,1,0:T(8,128)S(1)} %get-tuple-element.41), channel_id=1, source_target_pairs={{0,1},{1,0},{2,3},{3,2},{4,5},{5,4},{6,7},{7,6},{8,9},{9,8},{10,11... | collective-permute-start | bytes 147464 | tf_op jit(solution)/shard_map/ppermute | solution.py:456
  86.6 1.3 %shard_map.74 = (f32[6,24,8,128]{3,2,1,0:T(8,128)S(1)}, f32[1152,128]{1,0:T(8,128)}) custom-call(f32[6,24,8,128]{3,2,1,0:T(8,128)S(1)} %get-tuple-element.34.x_ref, f32[1152,128]{1,0:T(8,128)S(1)} %bitcast.12, f32[432,128]{1,0:T(8,128)S(1)} %get-tuple-element.24.links_ref, f32[8,128]{1,0:T(8,128)S(1)} %get-tuple-element.26.rate_ref, ...), custom_call_target="tpu_custom_call" | custom-call | flops 5000000 | bytes 3000000 | tf_op jit(solution)/shard_map/pallas_call | solution.py:500
  88.0 3.8 %collective-permute-done.7.tnear_ref = f32[12,8,128]{2,1,0:T(8,128)S(1)} collective-permute-done((f32[12,8,128]{2,1,0:T(8,128)S(1)}, f32[12,8,128]{2,1,0:T(8,128)S(1)}, u32[]{:S(2)}, u32[]{:S(2)}) %collective-permute-start.7) | collective-permute-done | bytes 49184 | tf_op jit(solution)/shard_map/ppermute | solution.py:456
  91.8 0.0 collective-permute-done.6.zouter_ref
  91.8 0.0 collective-permute-done.5.zinner_ref
  91.8 0.0 collective-permute-done.4.znear_ref
  91.8 1.2 %shard_map.75 = f32[1152,128]{1,0:T(8,128)} custom-call(f32[6,24,8,128]{3,2,1,0:T(8,128)S(1)} %get-tuple-element.37.y_ref, f32[432,128]{1,0:T(8,128)S(1)} %get-tuple-element.24.links_ref, f32[8,128]{1,0:T(8,128)S(1)} %get-tuple-element.26.rate_ref, f32[6,12,8,128]{3,2,1,0:T(8,128)S(1)} %collective-permute-done.4.znear_ref, ...), custom_call_target="tpu_custom_call" | custom-call | flops 5000000 | bytes 3000000 | tf_op jit(solution)/shard_map/pallas_call | solution.py:500
  (2 shorter events, 0.0 us)
Async XLA Ops:
  1.3 40.2 %copy-start.1 = (f32[32]{0:T(128)S(1)}, f32[32]{0:T(128)}, u32[]{:S(2)}) copy-start(f32[32]{0:T(128)} %param.7) | copy-start | bytes 388
  3.7 43.9 %copy-start = (f32[8,24,6,1,128]{4,3,2,1,0:T(1,128)S(1)}, f32[8,24,6,1,128]{4,3,2,1,0:T(1,128)}, u32[]{:S(2)}) copy-start(f32[8,24,6,1,128]{4,3,2,1,0:T(1,128)} %param.5) | copy-start | bytes 1769476
  42.7 6.1 %collective-permute-start = (f32[6,12,8,128]{3,2,1,0:T(8,128)S(1)}, f32[6,12,8,128]{3,2,1,0:T(8,128)S(1)}, u32[]{:S(2)}, u32[]{:S(2)}) collective-permute-start(f32[6,12,8,128]{3,2,1,0:T(8,128)S(1)} %get-tuple-element.27), channel_id=1, source_target_pairs={{0,64},{64,0},{128,192},{192,128},{256,320},{320,256},{384,448},{4... | collective-permute-start | bytes 884744 | tf_op jit(solution)/shard_map/ppermute | solution.py:456
  45.0 11.7 %collective-permute-start.1 = (f32[6,12,8,128]{3,2,1,0:T(8,128)S(1)}, f32[6,12,8,128]{3,2,1,0:T(8,128)S(1)}, u32[]{:S(2)}, u32[]{:S(2)}) collective-permute-start(f32[6,12,8,128]{3,2,1,0:T(8,128)S(1)} %get-tuple-element.28), channel_id=1, source_target_pairs={{0,448},{64,128},{128,64},{192,256},{256,192},{320,384},{384,320},... | collective-permute-start | bytes 884744 | tf_op jit(solution)/shard_map/ppermute | solution.py:456
  56.9 15.5 %collective-permute-start.3 = (f32[2,12,8,128]{3,2,1,0:T(8,128)S(1)}, f32[2,12,8,128]{3,2,1,0:T(8,128)S(1)}, u32[]{:S(2)}, u32[]{:S(2)}) collective-permute-start(f32[2,12,8,128]{3,2,1,0:T(8,128)S(1)} %get-tuple-element.31), channel_id=1, source_target_pairs={{0,63},{1,2},{2,1},{3,4},{4,3},{5,6},{6,5},{7,8},{8,7},{9,10},{10,... | collective-permute-start | bytes 294920 | tf_op jit(solution)/shard_map/ppermute | solution.py:456
  62.0 10.3 %collective-permute-start.2 = (f32[12,8,128]{2,1,0:T(8,128)S(1)}, f32[12,8,128]{2,1,0:T(8,128)S(1)}, u32[]{:S(2)}, u32[]{:S(2)}) collective-permute-start(f32[12,8,128]{2,1,0:T(8,128)S(1)} %get-tuple-element.29), channel_id=1, source_target_pairs={{0,1},{1,0},{2,3},{3,2},{4,5},{5,4},{6,7},{7,6},{8,9},{9,8},{10,11... | collective-permute-start | bytes 147464 | tf_op jit(solution)/shard_map/ppermute | solution.py:456
  72.6 19.2 %collective-permute-start.4 = (f32[6,12,8,128]{3,2,1,0:T(8,128)S(1)}, f32[6,12,8,128]{3,2,1,0:T(8,128)S(1)}, u32[]{:S(2)}, u32[]{:S(2)}) collective-permute-start(f32[6,12,8,128]{3,2,1,0:T(8,128)S(1)} %get-tuple-element.38), channel_id=1, source_target_pairs={{0,64},{64,0},{128,192},{192,128},{256,320},{320,256},{384,448},{4... | collective-permute-start | bytes 884744 | tf_op jit(solution)/shard_map/ppermute | solution.py:456
  74.5 17.3 %collective-permute-start.5 = (f32[4,12,8,128]{3,2,1,0:T(8,128)S(1)}, f32[4,12,8,128]{3,2,1,0:T(8,128)S(1)}, u32[]{:S(2)}, u32[]{:S(2)}) collective-permute-start(f32[4,12,8,128]{3,2,1,0:T(8,128)S(1)} %get-tuple-element.39), channel_id=1, source_target_pairs={{0,448},{64,128},{128,64},{192,256},{256,192},{320,384},{384,320},... | collective-permute-start | bytes 589832 | tf_op jit(solution)/shard_map/ppermute | solution.py:456
  76.6 15.1 %collective-permute-start.6 = (f32[2,12,8,128]{3,2,1,0:T(8,128)S(1)}, f32[2,12,8,128]{3,2,1,0:T(8,128)S(1)}, u32[]{:S(2)}, u32[]{:S(2)}) collective-permute-start(f32[2,12,8,128]{3,2,1,0:T(8,128)S(1)} %get-tuple-element.40), channel_id=1, source_target_pairs={{0,448},{64,128},{128,64},{192,256},{256,192},{320,384},{384,320},... | collective-permute-start | bytes 294920 | tf_op jit(solution)/shard_map/ppermute | solution.py:456
  81.9 9.9 %collective-permute-start.7 = (f32[12,8,128]{2,1,0:T(8,128)S(1)}, f32[12,8,128]{2,1,0:T(8,128)S(1)}, u32[]{:S(2)}, u32[]{:S(2)}) collective-permute-start(f32[12,8,128]{2,1,0:T(8,128)S(1)} %get-tuple-element.41), channel_id=1, source_target_pairs={{0,1},{1,0},{2,3},{3,2},{4,5},{5,4},{6,7},{7,6},{8,9},{9,8},{10,11... | collective-permute-start | bytes 147464 | tf_op jit(solution)/shard_map/ppermute | solution.py:456
